TPU v7x, 32 devices: a whole 2x2x4 slice. The times are simulated.
32 devices in a mesh: row: 16 (over z, y, core), col: 2 (over x).
Axes of the slice: x: 2, y: 2, z: 4, core: 2. Of those that a mesh axis runs over, the one named last changes fastest.
Arguments:
- jacobian: bfloat16 [512, 256, 128], P(('col', 'row')), may hold values from -1.5 to 1.5
- weights: bfloat16 [32, 512, 256], P('row', 'col'), may hold values from 0.25 to 4
- panel_weights: bfloat16 [512, 256], P(('col', 'row')), may hold values from 0.25 to 4
- damping: float32 [32, 128], P('row'), may hold values from 0.01 to 1
- panel_inverse: float32 [128, 128], replicated, may hold values from -0.12 to 0.12
Outputs:
- schur: float32 [4096, 65536], P('row', 'col')
All inputs are finite; a program needn't handle non-finite values.
Results may differ from a plain program's by a relative error of at most 0.0022.
Values may be sent and summed in bfloat16 or wider, within the bound.
No kernel may reach another device: no remote copies, remote signals or barrier semaphores. Data moves between devices by JAX's collectives and lax.ppermute only.
A program may use at most 128 MiB of HBM per device.

v0:
```python
import functools

import jax
import jax.numpy as jnp
import numpy as np
from jax import lax
from jax.experimental import pallas as pl
from jax.experimental.pallas import tpu as pltpu
from jax.sharding import PartitionSpec as P

HIGHEST = lax.Precision.HIGHEST
F32 = jnp.float32
BF16 = jnp.bfloat16


def dot_nt(a, b):
    return lax.dot_general(a, b, (((1,), (1,)), ((), ())), preferred_element_type=F32)


def prep_kernel(slab, panel, w_panel, inverse, slab_t, panel_t, fac, fac_b):
    width = panel.shape[1]
    p_t = panel[...].T
    panel_t[...] = p_t
    for i in range(slab.shape[0]):
        s = slab[i]
        slab_t[i] = s.T
        scaled = p_t * w_panel[pl.ds(i, 1), :].astype(BF16)
        hess = jnp.dot(scaled, s, preferred_element_type=F32)
        f = jnp.dot(hess, inverse[...], precision=HIGHEST, preferred_element_type=F32)
        fac[i * width : (i + 1) * width] = f
        fac_b[i * width : (i + 1) * width] = f.astype(BF16)


def prep_call(slab, panel, w_panel, inverse):
    slabs, rows, width = slab.shape
    return pl.pallas_call(
        prep_kernel,
        out_shape=[
            jax.ShapeDtypeStruct((slabs, width, rows), BF16),
            jax.ShapeDtypeStruct((width, rows), BF16),
            jax.ShapeDtypeStruct((slabs * width, width), F32),
            jax.ShapeDtypeStruct((slabs * width, width), BF16),
        ],
    )(slab, panel, w_panel, inverse)


def block_kernel(slot, half, count, skip, sc, w, slab_t, panel_t, fac, fac_b, gin, *refs):
    blocks = refs[:count]
    out, gout, token, jbuf, obuf, in_sem, out_sem = refs[count + skip :]
    token[...] = jnp.zeros_like(token)
    slabs, width, rows = slab_t.shape
    extra = sc.shape[0] - slabs - 1
    for b in range(count):
        pltpu.make_async_copy(blocks[b], jbuf.at[b], in_sem.at[b]).start()
    gout[...] = gin[...]

    def write(b):
        col = pl.multiple_of(sc[slot + b] * width, half * width)
        return pltpu.make_async_copy(
            obuf.at[b % 2], out.at[:, pl.ds(col, half * width)], out_sem.at[b % 2]
        )

    def one(b, carry):
        pltpu.make_async_copy(blocks[0], jbuf.at[b], in_sem.at[b]).wait()

        @pl.when(b >= 2)
        def _():
            write(b - 2).wait()

        first = sc[slot + b]
        pw = jbuf[b, half * rows : half * rows + 2 * half, :].astype(F32)
        acc = None
        parts, panels = [], []
        for k in range(half):
            j = first + k
            jac_t = jbuf[b, k * rows : (k + 1) * rows, :].T
            ws = [
                jnp.where(j == sc[extra + 1 + i], 0.0, w[i, pl.ds(j, 1), :]).astype(BF16)
                for i in range(slabs)
            ]
            row_p = jnp.concatenate([pw[k : k + 1], pw[half + k : half + k + 1]], 1).astype(BF16)
            parts.append(
                dot_nt(jac_t, jnp.concatenate([slab_t[i] * ws[i] for i in range(slabs)], 0))
            )
            panels.append(dot_nt(jac_t, panel_t[...] * row_p).astype(BF16))
            part = dot_nt(jac_t, jnp.concatenate([jac_t * ws[i] for i in range(slabs)], 0))
            acc = part if acc is None else acc + part
        corr = jnp.dot(fac_b[...], jnp.concatenate(panels, 1), preferred_element_type=F32)
        o = obuf.at[b % 2]
        for k in range(half):
            for i in range(slabs):
                here = (slice(i * width, (i + 1) * width), slice(k * width, (k + 1) * width))
                o[here] = parts[k][:, i * width : (i + 1) * width] - corr[here]
        gout[...] += acc
        where_p = sc[extra] - first

        @pl.when((where_p >= 0) & (where_p < half))
        def _():
            for k in range(half):

                @pl.when(where_p == k)
                def _():
                    o[:, k * width : (k + 1) * width] = fac[...]

        write(b).start()
        return carry

    lax.fori_loop(0, count, one, 0)
    for b in range(max(count - 2, 0), count):
        write(b).wait()


def block_call(slot, half, sc, blocks, w, slab_t, panel_t, fac, fac_b, gram, after, out, shape):
    slabs, width, rows = slab_t.shape
    count = len(blocks)
    args = [w, slab_t, panel_t, fac, fac_b, gram] + list(blocks) + list(after)
    specs = [pl.BlockSpec(memory_space=pltpu.VMEM)] * 6
    specs += [pl.BlockSpec(memory_space=pltpu.HBM)] * count
    specs += [pl.BlockSpec(memory_space=pl.ANY)] * len(after)
    aliases = {6: 1}
    if out is not None:
        aliases[1 + len(args)] = 0
        args.append(out)
        specs.append(pl.BlockSpec(memory_space=pl.ANY))
    stations = half * count
    return pl.pallas_call(
        functools.partial(
            block_kernel, slot, half, count, len(after) + (out is not None)
        ),
        in_specs=[pl.BlockSpec(memory_space=pltpu.SMEM)] + specs,
        out_specs=[pl.BlockSpec(memory_space=pl.ANY)] + [pl.BlockSpec(memory_space=pltpu.VMEM)] * 2,
        out_shape=[
            jax.ShapeDtypeStruct(shape, F32),
            jax.ShapeDtypeStruct(gram.shape, F32),
            jax.ShapeDtypeStruct((8, 128), F32),
        ],
        scratch_shapes=[
            pltpu.VMEM((count,) + blocks[0].shape, BF16),
            pltpu.VMEM((2, slabs * width, half * width), F32),
            pltpu.SemaphoreType.DMA((count,)),
            pltpu.SemaphoreType.DMA((2,)),
        ],
        input_output_aliases=aliases,
        compiler_params=pltpu.CompilerParams(vmem_limit_bytes=24 << 20),
        cost_estimate=pl.CostEstimate(
            flops=stations * 14 * width * width * rows,
            bytes_accessed=stations * (slabs * width * width * 4 + rows * width * 2),
            transcendentals=0,
        ),
    )(sc, *args)


def patch_kernel(sc, gram, other, damp, tile, out):
    i = pl.program_id(0)
    width = tile.shape[0]
    g = (gram[...] + other[...]).T
    eye = lax.broadcasted_iota(jnp.int32, (width, width), 0) == lax.broadcasted_iota(
        jnp.int32, (width, width), 1
    )
    full = jnp.where(eye, g * (1.0 + damp[pl.ds(i, 1), :]), g)
    out[...] = jnp.where(sc[2 * i + 1] > 0, tile[...] + full, tile[...])


def patch_call(sc, gram, other, damping, out):
    slabs, width = damping.shape
    tile = pl.BlockSpec((width, width), lambda i, s: (i, s[2 * i]))
    part = pl.BlockSpec((width, width), lambda i, s: (0, i))
    return pl.pallas_call(
        patch_kernel,
        grid_spec=pltpu.PrefetchScalarGridSpec(
            num_scalar_prefetch=1,
            grid=(slabs,),
            in_specs=[part, part, pl.BlockSpec((slabs, width), lambda i, s: (0, 0)), tile],
            out_specs=tile,
        ),
        out_shape=jax.ShapeDtypeStruct(out.shape, F32),
        input_output_aliases={4: 0},
    )(sc, gram, other, damping, out)


def chip_cycle(chips, cols):
    if cols == 2:
        return list(range(0, chips, 2)) + list(range(chips - 1, 0, -2))
    half = chips // 2
    return list(range(half)) + list(range(chips - 1, half - 1, -1))


def spread_direct(jacobian, weights, row, col):
    per_dev, samples, width = jacobian.shape
    slabs = weights.shape[0]
    core, y = row % 2, (row // 2) % 2
    both = ("row", "col")
    w_mine = weights[:, -1].reshape(slabs * samples // width, width)
    w_mine = jnp.pad(w_mine, ((0, samples - w_mine.shape[0]), (0, 0)))
    quads = 2 * slabs
    ends = [None, (11, 1), (7, 1), (3, 1)]
    is_panel = col == 1
    mine = jacobian[per_dev - 1]
    panel_pay = jnp.concatenate([mine[None]] + [jnp.zeros_like(jacobian[: quads - 1])], 0)
    total = jnp.where((row == 15) & is_panel, panel_pay, jnp.zeros_like(panel_pay))
    total = total + jnp.where((row == 0) & (col == 0), jacobian[:quads], jnp.zeros_like(panel_pay))
    for m in (1, 2, 3, 0):
        pay = jnp.where(is_panel, panel_pay, lax.slice_in_dim(jacobian, quads * m, quads * (m + 1)))
        pairs = [(2, 2 * (8 + 2 * m))]
        if m:
            pairs += [(0, 4 * m), (31, 2 * ends[m][0] + ends[m][1])]
        total = total + lax.ppermute(pay, both, pairs)
    hop = [(2 * r, 2 * (r ^ 1)) for r in range(16)] + [(2 * r + 1, 2 * (r ^ 2) + 1) for r in range(16)]
    first = lax.ppermute(jnp.where(is_panel, total[:slabs], total[slabs:]), both, hop)
    slab = jnp.where(core == 0, total[:slabs], first)
    panel = jnp.where(y == 1, total[0], first[0])
    far = jnp.stack([panel, w_mine], 0)
    second = lax.ppermute(jnp.where(is_panel, far, slab), "col", [(0, 1), (1, 0)])
    slab = jnp.where(is_panel, second, slab)
    far = jnp.where(is_panel, far, second)
    third = lax.ppermute(far[0], "row", [(r, r ^ 1) for r in range(16)])
    panel = jnp.where(core == 1, far[0], third)
    w_panel = far[1][: slabs * samples // width].reshape(slabs, samples)
    return slab, panel, w_panel


def spread_general(jacobian, weights, row, col, rows, cols):
    per_dev, samples, width = jacobian.shape
    slabs = weights.shape[0]
    holds = (row == rows - 1) & (col == cols - 1)
    panel = lax.psum(
        jnp.where(holds, jacobian[per_dev - 1], jnp.zeros_like(jacobian[0])), ("row", "col")
    )
    w_panel = lax.psum(
        jnp.where(col == cols - 1, weights[:, -1], jnp.zeros_like(weights[:, 0])), "col"
    )
    slab = jnp.zeros((slabs, samples, width), BF16)
    for offset in range(0, per_dev, slabs):
        piece = lax.slice_in_dim(jacobian, offset, offset + slabs, axis=0)
        pairs = []
        for t in range(rows):
            if (t * slabs) % per_dev == offset:
                home = (t * slabs) // per_dev
                source, target = (home % rows) * cols + home // rows, t * cols
                if source == target:
                    slab = slab + jnp.where((row == t) & (col == 0), piece, jnp.zeros_like(piece))
                else:
                    pairs.append((source, target))
        if pairs:
            slab = slab + lax.ppermute(piece, ("row", "col"), pairs)
    spread = slab
    for c in range(1, cols):
        spread = spread + lax.ppermute(slab, "col", [(0, c)])
    return spread, panel, w_panel


def shards(jacobian, weights, panel_weights, damping, panel_inverse):
    per_dev, samples, width = jacobian.shape
    slabs, col_block, _ = weights.shape
    rows = lax.axis_size("row")
    cols = lax.axis_size("col")
    row = lax.axis_index("row")
    col = lax.axis_index("col")
    panel_id = col_block * cols - 1

    chips = rows // 2
    cycle = chip_cycle(chips, cols)
    place = {c: p for p, c in enumerate(cycle)}
    ahead = [(2 * c + k, 2 * cycle[(place[c] + 1) % chips] + k) for c in cycle for k in (0, 1)]
    back = [(t, s) for s, t in ahead]
    swap = [(r, r ^ 1) for r in range(rows)]
    half = per_dev // 2

    if (rows, cols, per_dev) == (16, 2, 8 * slabs):
        slab, panel_jac, w_panel = spread_direct(jacobian, weights, row, col)
    else:
        slab, panel_jac, w_panel = spread_general(jacobian, weights, row, col, rows, cols)
    slab_t, panel_t, factor, factor_b = prep_call(
        slab, panel_jac, w_panel.astype(F32), panel_inverse
    )
    w32 = weights.astype(F32)

    def pack(k):
        own = slice(k * half, (k + 1) * half)
        p = panel_weights[own]
        tail = jnp.concatenate([p[:, :width], p[:, width:]], 0)
        tail = jnp.pad(tail, ((0, -tail.shape[0] % 16), (0, 0)))
        return jnp.concatenate([jacobian[own].reshape(half * samples, width), tail], 0)

    def over(value, perm):
        return lax.ppermute(value, "row", perm)

    own = [pack(0), pack(1)]
    tokens, after = [], []
    gram = jnp.zeros((width, slabs * width), F32)
    shape = (slabs * width, col_block * width)
    out = None
    plan = []

    def compute(call):
        nonlocal out, gram
        slot = len(plan)
        plan.extend(p[1:] for p in call)
        out, gram, token = block_call(
            slot, half, sc, [p[0] for p in call],
            w32, slab_t, panel_t, factor, factor_b, gram, tuple(after), out, shape,
        )
        after.clear()
        tokens.append(token)

    order = [(0, 0, 0), (0, 0, 1), (0, 1, 0), (0, 1, 1)]
    far = chips // 2
    for d in range(1, far):
        for k in (0, 1):
            order += [(-d, 0, k), (d, 0, k), (-d, 1, k), (d, 1, k)]
    order += [(-far, 0, 0), (far, 0, 1), (-far, 1, 0), (far, 1, 1)]
    table = np.zeros((rows, len(order)), np.int32)
    for r in range(rows):
        for n, (dist, other, k) in enumerate(order):
            chip = cycle[(place[r // 2] + dist) % chips]
            table[r, n] = (2 * chip + ((r % 2) ^ other)) * per_dev + k * half
    starts = lax.dynamic_index_in_dim(jnp.asarray(table), row, 0, keepdims=False)
    base = col * col_block
    ids = row * slabs + jnp.arange(slabs, dtype=jnp.int32) - base
    sc = jnp.concatenate([starts, (panel_id - base)[None].astype(jnp.int32), ids])
    held = ((ids >= 0) & (ids < col_block)).astype(jnp.int32)
    spots = jnp.stack([jnp.clip(ids, 0, col_block - 1), held], 1).reshape(-1)

    hops = [(over(own[k], ahead), over(own[k], back)) for k in (0, 1)]
    compute(
        [(own[0], 0, 0, 0), (own[1], 0, 0, 1)] + [(over(own[k], swap), 0, 1, k) for k in (0, 1)]
    )
    for q in range(2 * (far - 1)):
        d, k = q // 2 + 1, q % 2
        f, b = hops[q]
        if q == 1:
            f, b, factor_b = lax.optimization_barrier((f, b, factor_b))
        elif q > 1:
            f, b, ready = lax.optimization_barrier((f, b, tokens[q - 1]))
            after.append(ready)
        if d + 1 < far:
            hops.append((over(f, ahead), over(b, back)))
        elif k == 0:
            last_f = over(f, ahead)
        else:
            last_b = over(b, back)
        compute([(f, -d, 0, k), (b, d, 0, k), (over(f, swap), -d, 1, k), (over(b, swap), d, 1, k)])
    compute([(last_f, -far, 0, 0), (last_b, far, 0, 1)])
    compute([(over(last_f, swap), -far, 1, 0), (over(last_b, swap), far, 1, 1)])
    assert plan == order
    if cols == 2:
        other = lax.ppermute(gram, "col", [(0, 1), (1, 0)])
    else:
        other = lax.psum(gram, "col") - gram
    return patch_call(spots, gram, other, damping, out)


def solution(mesh):
    return jax.shard_map(
        shards,
        mesh=mesh,
        in_specs=(
            P(("col", "row"), None, None),
            P("row", "col", None),
            P(("col", "row"), None),
            P("row", None),
            P(),
        ),
        out_specs=P("row", "col"),
        check_vma=False,
    )
```

profile of v0, /device:TPU:0, one launch (start us, length us, event | category | flops | bytes accessed | tf_op | source)
XLA Modules:
  0.0 157.8 jit_solution(12498242432014863736)
XLA Ops:
  0.0 0.8 slice.66
  0.8 1.3 pad_select_fusion.3
  2.1 0.7 collective-permute-start.3
  2.8 5.9 %collective-permute-start.2 = (bf16[4,256,128]{2,1,0:T(8,128)(2,1)S(1)}, bf16[4,256,128]{2,1,0:T(8,128)(2,1)S(1)}, u32[]{:S(2)}, u32[]{:S(2)}) collective-permute-start(bf16[4,256,128]{2,1,0:T(8,128)(2,1)S(1)} %get-tuple-element.89), channel_id=1, source_target_pairs={{2,28},{0,12},{31,7}} | collective-permute-start | bytes 786440 | tf_op jit(solution)/shard_map/ppermute | solution.py:207
  8.7 2.0 %collective-permute-start.1 = (bf16[4,256,128]{2,1,0:T(8,128)(2,1)S(1)}, bf16[4,256,128]{2,1,0:T(8,128)(2,1)}, u32[]{:S(2)}, u32[]{:S(2)}) collective-permute-start(bf16[4,256,128]{2,1,0:T(8,128)(2,1)S(1)} %get-tuple-element.88), channel_id=1, source_target_pairs={{2,24},{0,8},{31,15}} | collective-permute-start | bytes 786440 | tf_op jit(solution)/shard_map/ppermute | solution.py:207
  10.7 2.0 %collective-permute-start = (bf16[4,256,128]{2,1,0:T(8,128)(2,1)S(1)}, bf16[4,256,128]{2,1,0:T(8,128)(2,1)}, u32[]{:S(2)}, u32[]{:S(2)}) collective-permute-start(bf16[4,256,128]{2,1,0:T(8,128)(2,1)S(1)} %get-tuple-element.87), channel_id=1, source_target_pairs={{2,20},{0,4},{31,23}} | collective-permute-start | bytes 786440 | tf_op jit(solution)/shard_map/ppermute | solution.py:207
  12.7 1.3 fusion.6
  14.0 0.7 fusion.7
  14.7 0.8 pad_maximum_fusion.refs_1_
  15.6 0.7 slice_reduce_fusion
  16.4 2.1 %collective-permute-start.8 = (bf16[2064,128]{1,0:T(8,128)(2,1)}, bf16[2064,128]{1,0:T(8,128)(2,1)S(1)}, u32[]{:S(2)}, u32[]{:S(2)}) collective-permute-start(bf16[2064,128]{1,0:T(8,128)(2,1)} %pad_maximum_fusion.refs_1_), channel_id=1, source_target_pairs={{8,0},{10,2},{16,8},{18,10},{24,16},{26,18},{28,24},{30,26},{20,28... | collective-permute-start | bytes 1585160 | tf_op jit(solution)/shard_map/ppermute | solution.py:286
  18.5 2.5 %collective-permute-done.1 = bf16[4,256,128]{2,1,0:T(8,128)(2,1)} collective-permute-done((bf16[4,256,128]{2,1,0:T(8,128)(2,1)S(1)}, bf16[4,256,128]{2,1,0:T(8,128)(2,1)}, u32[]{:S(2)}, u32[]{:S(2)}) %collective-permute-start.1) | collective-permute-done | bytes 262176 | tf_op jit(solution)/shard_map/ppermute | solution.py:207
  21.0 1.3 fusion.4
  22.4 8.9 %collective-permute-start.4 = (bf16[2,256,128]{2,1,0:T(8,128)(2,1)S(1)}, bf16[2,256,128]{2,1,0:T(8,128)(2,1)S(1)}, u32[]{:S(2)}, u32[]{:S(2)}) collective-permute-start(bf16[2,256,128]{2,1,0:T(8,128)(2,1)S(1)} %slice_select_fusion), channel_id=1, source_target_pairs={{0,2},{2,0},{4,6},{6,4},{8,10},{10,8},{12,14},{14,12},{16,18},{18,... | collective-permute-start | bytes 393224 | tf_op jit(solution)/shard_map/ppermute | solution.py:209
  31.4 0.9 collective-permute-done.4
  32.3 0.7 broadcast_select_fusion.3
  33.0 8.3 %collective-permute-start.5 = (bf16[2,256,128]{2,1,0:T(8,128)(2,1)}, bf16[2,256,128]{2,1,0:T(8,128)(2,1)}, u32[]{:S(2)}, u32[]{:S(2)}) collective-permute-start(bf16[2,256,128]{2,1,0:T(8,128)(2,1)} %broadcast_select_fusion.3), channel_id=1, source_target_pairs={{0,1},{1,0},{2,3},{3,2},{4,5},{5,4},{6,7},{7,6},{8,9},{9,8},{10,11... | collective-permute-start | bytes 393224 | tf_op jit(solution)/shard_map/ppermute | solution.py:213
  41.3 0.7 dynamic-slice_bitcast_fusion
  42.0 1.0 convert_element_type.21.w
  43.0 0.1 pad_add_fusion.1.sc
  43.1 1.5 collective-permute-done.5
  44.6 1.6 %broadcast_select_fusion.1 = (bf16[2,256,128]{2,1,0:T(8,128)(2,1)S(1)}, bf16[2,256,128]{2,1,0:T(8,128)(2,1)}) fusion(bf16[2,256,128]{2,1,0:T(8,128)(2,1)} %collective-permute-done.5, pred[]{:T(512)S(6)} %eq.24, bf16[1,256,128]{2,1,0:T(8,128)(2,1)} %copy-done.8, bf16[1,256,128]{2,1,0:T(8,128)(2,1)S(1)} %slice_select_fusion.1, ...), kind=kLoop, calls=%fused_computation.15 | loop fusion | flops 262144 | bytes 786434 | tf_op jit(solution)/shard_map/jit(_where)/select_n | solution.py:215
  46.2 0.6 collective-permute-start.10
  46.8 1.4 collective-permute-start.13
  48.2 0.6 collective-permute-start.6
  48.8 0.6 reshape.43.w_panel
  49.4 2.2 %collective-permute-start.17 = (bf16[2064,128]{1,0:T(8,128)(2,1)S(1)}, bf16[2064,128]{1,0:T(8,128)(2,1)S(1)}, u32[]{:S(2)}, u32[]{:S(2)}) collective-permute-start(bf16[2064,128]{1,0:T(8,128)(2,1)S(1)} %collective-permute-done.11.refs_0_), channel_id=1, source_target_pairs={{0,8},{2,10},{8,16},{10,18},{16,24},{18,26},{24,28},{26,30},{28,20... | collective-permute-start | bytes 1585160 | tf_op jit(solution)/shard_map/ppermute | solution.py:286
  51.6 1.5 broadcast_select_fusion.4.panel
  53.1 2.0 %shard_map.64 = (bf16[2,128,256]{2,1,0:T(8,128)(2,1)}, bf16[128,256]{1,0:T(8,128)(2,1)}, f32[256,128]{1,0:T(8,128)}, bf16[256,128]{1,0:T(8,128)(2,1)}) custom-call(bf16[2,256,128]{2,1,0:T(8,128)(2,1)} %get-tuple-element.94.slab, bf16[256,128]{1,0:T(8,128)(2,1)} %broadcast_select_fusion.4.panel, f32[2,256]{1,0:T(2,128)} %reshape.43.w_panel, f32[128,128]{1,0:T(8,128)} %inverse.1), custom_call_target="tpu_custom_call" | custom-call | tf_op jit(solution)/shard_map/pallas_call | solution.py:36
  55.2 2.0 %collective-permute-start.21 = (bf16[2064,128]{1,0:T(8,128)(2,1)S(1)}, bf16[2064,128]{1,0:T(8,128)(2,1)S(1)}, u32[]{:S(2)}, u32[]{:S(2)}) collective-permute-start(bf16[2064,128]{1,0:T(8,128)(2,1)S(1)} %collective-permute-done.7.refs_0_), channel_id=1, source_target_pairs={{0,8},{2,10},{8,16},{10,18},{16,24},{18,26},{24,28},{26,30},{28,20... | collective-permute-start | bytes 1585160 | tf_op jit(solution)/shard_map/ppermute | solution.py:286
  57.2 0.2 collective-permute-start.16
  57.4 0.9 copy-done.1
  58.3 0.9 copy-done.2
  59.2 0.8 copy-done.3
  60.0 0.8 copy-done.4
  60.9 1.0 copy-done.6
  61.9 6.6 %shard_map.65 = (f32[256,32768]{1,0:T(8,128)}, f32[128,256]{1,0:T(8,128)S(1)}, f32[8,128]{1,0:T(8,128)}) custom-call(s32[35]{0:T(128)S(1)} %pad_add_fusion.1.sc, f32[2,256,256]{2,1,0:T(8,128)S(1)} %convert_element_type.21.w, bf16[2,128,256]{2,1,0:T(8,128)(2,1)S(1)} %copy-done.1, bf16[128,256]{1,0:T(8,128)(2,1)S(1)} %copy-done.3, ...), custom_call_target="tpu_custom_call", output_to_operand_aliasing={{1}: (6, {})} | custom-call | flops 1879048192 | bytes 6291456 | tf_op jit(solution)/shard_map/pallas_call | solution.py:126
  68.5 6.0 %shard_map.66 = (f32[256,32768]{1,0:T(8,128)}, f32[128,256]{1,0:T(8,128)S(1)}, f32[8,128]{1,0:T(8,128)S(1)}) custom-call(s32[35]{0:T(128)S(1)} %pad_add_fusion.1.sc, f32[2,256,256]{2,1,0:T(8,128)S(1)} %convert_element_type.21.w, bf16[2,128,256]{2,1,0:T(8,128)(2,1)S(1)} %copy-done.1, ...), custom_call_target="tpu_custom_call", output_to_operand_aliasing={{1}: (6, {}), {0}: (11, {})} | custom-call | flops 1879048192 | bytes 6291456 | tf_op jit(solution)/shard_map/pallas_call | solution.py:126
  74.5 0.1 collective-permute-start.22
  74.6 0.4 collective-permute-start.19
  75.0 0.2 collective-permute-start.20
  75.2 2.4 %collective-permute-start.25 = (bf16[2064,128]{1,0:T(8,128)(2,1)S(1)}, bf16[2064,128]{1,0:T(8,128)(2,1)S(1)}, u32[]{:S(2)}, u32[]{:S(2)}) collective-permute-start(bf16[2064,128]{1,0:T(8,128)(2,1)S(1)} %collective-permute-done.17.refs_0_), channel_id=1, source_target_pairs={{0,8},{2,10},{8,16},{10,18},{16,24},{18,26},{24,28},{26,30},{28,20... | collective-permute-start | bytes 1585160 | tf_op jit(solution)/shard_map/ppermute | solution.py:286
  77.6 6.1 %shard_map.67 = (f32[256,32768]{1,0:T(8,128)}, f32[128,256]{1,0:T(8,128)S(1)}, f32[8,128]{1,0:T(8,128)S(1)}) custom-call(s32[35]{0:T(128)S(1)} %pad_add_fusion.1.sc, f32[2,256,256]{2,1,0:T(8,128)S(1)} %convert_element_type.21.w, bf16[2,128,256]{2,1,0:T(8,128)(2,1)S(1)} %copy-done.1, ...), custom_call_target="tpu_custom_call", output_to_operand_aliasing={{1}: (6, {}), {0}: (11, {})} | custom-call | flops 1879048192 | bytes 6291456 | tf_op jit(solution)/shard_map/pallas_call | solution.py:126
  83.7 6.1 %collective-permute-done.22.refs_1_ = bf16[2064,128]{1,0:T(8,128)(2,1)S(1)} collective-permute-done((bf16[2064,128]{1,0:T(8,128)(2,1)S(1)}, bf16[2064,128]{1,0:T(8,128)(2,1)S(1)}, u32[]{:S(2)}, u32[]{:S(2)}) %collective-permute-start.22) | collective-permute-done | bytes 528416 | tf_op jit(solution)/shard_map/ppermute | solution.py:286
  89.8 0.5 collective-permute-start.24
  90.4 2.0 %collective-permute-start.29 = (bf16[2064,128]{1,0:T(8,128)(2,1)S(1)}, bf16[2064,128]{1,0:T(8,128)(2,1)S(1)}, u32[]{:S(2)}, u32[]{:S(2)}) collective-permute-start(bf16[2064,128]{1,0:T(8,128)(2,1)S(1)} %collective-permute-done.21.refs_0_), channel_id=1, source_target_pairs={{0,8},{2,10},{8,16},{10,18},{16,24},{18,26},{24,28},{26,30},{28,20... | collective-permute-start | bytes 1585160 | tf_op jit(solution)/shard_map/ppermute | solution.py:286
  92.4 6.0 %shard_map.68 = (f32[256,32768]{1,0:T(8,128)}, f32[128,256]{1,0:T(8,128)S(1)}, f32[8,128]{1,0:T(8,128)S(1)}) custom-call(s32[35]{0:T(128)S(1)} %pad_add_fusion.1.sc, f32[2,256,256]{2,1,0:T(8,128)S(1)} %convert_element_type.21.w, bf16[2,128,256]{2,1,0:T(8,128)(2,1)S(1)} %copy-done.1, ...), custom_call_target="tpu_custom_call", output_to_operand_aliasing={{1}: (6, {}), {0}: (12, {})} | custom-call | flops 1879048192 | bytes 6291456 | tf_op jit(solution)/shard_map/pallas_call | solution.py:126
  98.4 2.7 %collective-permute-done.26.refs_1_ = bf16[2064,128]{1,0:T(8,128)(2,1)S(1)} collective-permute-done((bf16[2064,128]{1,0:T(8,128)(2,1)}, bf16[2064,128]{1,0:T(8,128)(2,1)S(1)}, u32[]{:S(2)}, u32[]{:S(2)}) %collective-permute-start.26) | collective-permute-done | bytes 528416 | tf_op jit(solution)/shard_map/ppermute | solution.py:286
  101.2 2.0 %collective-permute-start.33 = (bf16[2064,128]{1,0:T(8,128)(2,1)S(1)}, bf16[2064,128]{1,0:T(8,128)(2,1)S(1)}, u32[]{:S(2)}, u32[]{:S(2)}) collective-permute-start(bf16[2064,128]{1,0:T(8,128)(2,1)S(1)} %collective-permute-done.25.refs_0_), channel_id=1, source_target_pairs={{0,8},{2,10},{8,16},{10,18},{16,24},{18,26},{24,28},{26,30},{28,20... | collective-permute-start | bytes 1585160 | tf_op jit(solution)/shard_map/ppermute | solution.py:286
  103.2 6.1 %shard_map.69 = (f32[256,32768]{1,0:T(8,128)}, f32[128,256]{1,0:T(8,128)S(1)}, f32[8,128]{1,0:T(8,128)S(1)}) custom-call(s32[35]{0:T(128)S(1)} %pad_add_fusion.1.sc, f32[2,256,256]{2,1,0:T(8,128)S(1)} %convert_element_type.21.w, bf16[2,128,256]{2,1,0:T(8,128)(2,1)S(1)} %copy-done.1, ...), custom_call_target="tpu_custom_call", output_to_operand_aliasing={{1}: (6, {}), {0}: (12, {})} | custom-call | flops 1879048192 | bytes 6291456 | tf_op jit(solution)/shard_map/pallas_call | solution.py:126
  109.3 3.0 %collective-permute-done.30.refs_1_ = bf16[2064,128]{1,0:T(8,128)(2,1)S(1)} collective-permute-done((bf16[2064,128]{1,0:T(8,128)(2,1)S(1)}, bf16[2064,128]{1,0:T(8,128)(2,1)S(1)}, u32[]{:S(2)}, u32[]{:S(2)}) %collective-permute-start.30) | collective-permute-done | bytes 528416 | tf_op jit(solution)/shard_map/ppermute | solution.py:286
  112.2 0.5 collective-permute-start.31
  112.8 2.9 %collective-permute-done.33.refs_0_ = bf16[2064,128]{1,0:T(8,128)(2,1)S(1)} collective-permute-done((bf16[2064,128]{1,0:T(8,128)(2,1)S(1)}, bf16[2064,128]{1,0:T(8,128)(2,1)S(1)}, u32[]{:S(2)}, u32[]{:S(2)}) %collective-permute-start.33) | collective-permute-done | bytes 528416 | tf_op jit(solution)/shard_map/ppermute | solution.py:286
  115.7 10.4 %collective-permute-done.34.refs_1_ = bf16[2064,128]{1,0:T(8,128)(2,1)S(1)} collective-permute-done((bf16[2064,128]{1,0:T(8,128)(2,1)S(1)}, bf16[2064,128]{1,0:T(8,128)(2,1)S(1)}, u32[]{:S(2)}, u32[]{:S(2)}) %collective-permute-start.34) | collective-permute-done | bytes 528416 | tf_op jit(solution)/shard_map/ppermute | solution.py:286
  126.1 6.7 %shard_map.70 = (f32[256,32768]{1,0:T(8,128)}, f32[128,256]{1,0:T(8,128)S(1)}, f32[8,128]{1,0:T(8,128)}) custom-call(s32[35]{0:T(128)S(1)} %pad_add_fusion.1.sc, f32[2,256,256]{2,1,0:T(8,128)S(1)} %convert_element_type.21.w, bf16[2,128,256]{2,1,0:T(8,128)(2,1)S(1)} %copy-done.1, ...), custom_call_target="tpu_custom_call", output_to_operand_aliasing={{1}: (6, {}), {0}: (12, {})} | custom-call | flops 1879048192 | bytes 6291456 | tf_op jit(solution)/shard_map/pallas_call | solution.py:126
  132.8 6.7 %shard_map.71 = (f32[256,32768]{1,0:T(8,128)}, f32[128,256]{1,0:T(8,128)S(1)}, f32[8,128]{1,0:T(8,128)}) custom-call(s32[35]{0:T(128)S(1)} %pad_add_fusion.1.sc, f32[2,256,256]{2,1,0:T(8,128)S(1)} %convert_element_type.21.w, bf16[2,128,256]{2,1,0:T(8,128)(2,1)S(1)} %copy-done.1, ...), custom_call_target="tpu_custom_call", output_to_operand_aliasing={{1}: (6, {}), {0}: (12, {})} | custom-call | flops 1879048192 | bytes 6291456 | tf_op jit(solution)/shard_map/pallas_call | solution.py:126
  139.5 4.4 %shard_map.72 = (f32[256,32768]{1,0:T(8,128)}, f32[128,256]{1,0:T(8,128)S(1)}, f32[8,128]{1,0:T(8,128)}) custom-call(s32[35]{0:T(128)S(1)} %pad_add_fusion.1.sc, f32[2,256,256]{2,1,0:T(8,128)S(1)} %convert_element_type.21.w, bf16[2,128,256]{2,1,0:T(8,128)(2,1)S(1)} %copy-done.1, ...), custom_call_target="tpu_custom_call", output_to_operand_aliasing={{1}: (6, {}), {0}: (9, {})} | custom-call | flops 939524096 | bytes 3145728 | tf_op jit(solution)/shard_map/pallas_call | solution.py:126
  143.9 4.4 %shard_map.73 = (f32[256,32768]{1,0:T(8,128)}, f32[128,256]{1,0:T(8,128)S(1)}, f32[8,128]{1,0:T(8,128)}) custom-call(s32[35]{0:T(128)S(1)} %pad_add_fusion.1.sc, f32[2,256,256]{2,1,0:T(8,128)S(1)} %convert_element_type.21.w, bf16[2,128,256]{2,1,0:T(8,128)(2,1)S(1)} %copy-done.1, ...), custom_call_target="tpu_custom_call", output_to_operand_aliasing={{1}: (6, {}), {0}: (9, {})} | custom-call | flops 939524096 | bytes 3145728 | tf_op jit(solution)/shard_map/pallas_call | solution.py:126
  148.4 2.2 %collective-permute-start.37 = (f32[128,256]{1,0:T(8,128)S(1)}, f32[128,256]{1,0:T(8,128)S(1)}, u32[]{:S(2)}, u32[]{:S(2)}) collective-permute-start(f32[128,256]{1,0:T(8,128)S(1)} %get-tuple-element.85.gram), channel_id=1, source_target_pairs={{0,1},{1,0},{2,3},{3,2},{4,5},{5,4},{6,7},{7,6},{8,9},{9,8},{10,11... | collective-permute-start | bytes 393224 | tf_op jit(solution)/shard_map/ppermute | solution.py:347
  150.5 0.1 pad_add_fusion
  150.6 0.7 reshape.40.sc
  151.3 3.4 %collective-permute-done.37.other = f32[128,256]{1,0:T(8,128)S(1)} collective-permute-done((f32[128,256]{1,0:T(8,128)S(1)}, f32[128,256]{1,0:T(8,128)S(1)}, u32[]{:S(2)}, u32[]{:S(2)}) %collective-permute-start.37) | collective-permute-done | bytes 131104 | tf_op jit(solution)/shard_map/ppermute | solution.py:347
  154.7 0.6 copy-done.12
  155.3 2.5 %shard_map.74 = f32[256,32768]{1,0:T(8,128)} custom-call(s32[4]{0:T(128)} %reshape.40.sc, f32[128,256]{1,0:T(8,128)} %copy-done, f32[128,256]{1,0:T(8,128)} %copy-done.12, f32[2,128]{1,0:T(2,128)} %damp.1, f32[256,32768]{1,0:T(8,128)} %get-tuple-element.86.tile), custom_call_target="tpu_custom_call", output_to_operand_aliasing={{}: (4, {})} | custom-call | tf_op jit(solution)/shard_map/pallas_call | solution.py:168
  (76 shorter events, 0.4 us)
Async XLA Ops:
  2.1 14.2 %collective-permute-start.3 = (bf16[4,256,128]{2,1,0:T(8,128)(2,1)S(1)}, bf16[4,256,128]{2,1,0:T(8,128)(2,1)S(1)}, u32[]{:S(2)}, u32[]{:S(2)}) collective-permute-start(bf16[4,256,128]{2,1,0:T(8,128)(2,1)S(1)} %get-tuple-element.90), channel_id=1, source_target_pairs={{2,16}} | collective-permute-start | bytes 786440 | tf_op jit(solution)/shard_map/ppermute | solution.py:207
  2.8 15.6 %collective-permute-start.2 = (bf16[4,256,128]{2,1,0:T(8,128)(2,1)S(1)}, bf16[4,256,128]{2,1,0:T(8,128)(2,1)S(1)}, u32[]{:S(2)}, u32[]{:S(2)}) collective-permute-start(bf16[4,256,128]{2,1,0:T(8,128)(2,1)S(1)} %get-tuple-element.89), channel_id=1, source_target_pairs={{2,28},{0,12},{31,7}} | collective-permute-start | bytes 786440 | tf_op jit(solution)/shard_map/ppermute | solution.py:207
  8.7 12.3 %collective-permute-start.1 = (bf16[4,256,128]{2,1,0:T(8,128)(2,1)S(1)}, bf16[4,256,128]{2,1,0:T(8,128)(2,1)}, u32[]{:S(2)}, u32[]{:S(2)}) collective-permute-start(bf16[4,256,128]{2,1,0:T(8,128)(2,1)S(1)} %get-tuple-element.88), channel_id=1, source_target_pairs={{2,24},{0,8},{31,15}} | collective-permute-start | bytes 786440 | tf_op jit(solution)/shard_map/ppermute | solution.py:207
  10.7 10.3 %collective-permute-start = (bf16[4,256,128]{2,1,0:T(8,128)(2,1)S(1)}, bf16[4,256,128]{2,1,0:T(8,128)(2,1)}, u32[]{:S(2)}, u32[]{:S(2)}) collective-permute-start(bf16[4,256,128]{2,1,0:T(8,128)(2,1)S(1)} %get-tuple-element.87), channel_id=1, source_target_pairs={{2,20},{0,4},{31,23}} | collective-permute-start | bytes 786440 | tf_op jit(solution)/shard_map/ppermute | solution.py:207
  15.6 30.6 %collective-permute-start.7 = (bf16[2064,128]{1,0:T(8,128)(2,1)}, bf16[2064,128]{1,0:T(8,128)(2,1)S(1)}, u32[]{:S(2)}, u32[]{:S(2)}) collective-permute-start(bf16[2064,128]{1,0:T(8,128)(2,1)} %pad_maximum_fusion.refs_1_), channel_id=1, source_target_pairs={{0,8},{2,10},{8,16},{10,18},{16,24},{18,26},{24,28},{26,30},{28,20... | collective-permute-start | bytes 1585160 | tf_op jit(solution)/shard_map/ppermute | solution.py:286
  16.3 33.0 %copy-start.5 = (bf16[2064,128]{1,0:T(8,128)(2,1)}, bf16[2064,128]{1,0:T(8,128)(2,1)S(1)}, u32[]{:S(2)}) copy-start(bf16[2064,128]{1,0:T(8,128)(2,1)S(1)} %pad_maximum_fusion.1.refs_0_) | copy-start | bytes 1585156
  16.4 2.1 %copy-start.10 = (bf16[4,256,128]{2,1,0:T(8,128)(2,1)}, bf16[4,256,128]{2,1,0:T(8,128)(2,1)S(1)}, u32[]{:S(2)}) copy-start(bf16[4,256,128]{2,1,0:T(8,128)(2,1)S(1)} %collective-permute-done.3) | copy-start | bytes 786436
  16.4 31.8 %collective-permute-start.8 = (bf16[2064,128]{1,0:T(8,128)(2,1)}, bf16[2064,128]{1,0:T(8,128)(2,1)S(1)}, u32[]{:S(2)}, u32[]{:S(2)}) collective-permute-start(bf16[2064,128]{1,0:T(8,128)(2,1)} %pad_maximum_fusion.refs_1_), channel_id=1, source_target_pairs={{8,0},{10,2},{16,8},{18,10},{24,16},{26,18},{28,24},{30,26},{20,28... | collective-permute-start | bytes 1585160 | tf_op jit(solution)/shard_map/ppermute | solution.py:286
  18.4 2.6 %copy-start.11 = (bf16[4,256,128]{2,1,0:T(8,128)(2,1)}, bf16[4,256,128]{2,1,0:T(8,128)(2,1)S(1)}, u32[]{:S(2)}) copy-start(bf16[4,256,128]{2,1,0:T(8,128)(2,1)S(1)} %collective-permute-done.2) | copy-start | bytes 786436
  18.4 28.3 %collective-permute-start.11 = (bf16[2064,128]{1,0:T(8,128)(2,1)S(1)}, bf16[2064,128]{1,0:T(8,128)(2,1)S(1)}, u32[]{:S(2)}, u32[]{:S(2)}) collective-permute-start(bf16[2064,128]{1,0:T(8,128)(2,1)S(1)} %pad_maximum_fusion.1.refs_0_), channel_id=1, source_target_pairs={{0,8},{2,10},{8,16},{10,18},{16,24},{18,26},{24,28},{26,30},{28,20... | collective-permute-start | bytes 1585160 | tf_op jit(solution)/shard_map/ppermute | solution.py:286
  21.0 27.2 %collective-permute-start.12 = (bf16[2064,128]{1,0:T(8,128)(2,1)S(1)}, bf16[2064,128]{1,0:T(8,128)(2,1)S(1)}, u32[]{:S(2)}, u32[]{:S(2)}) collective-permute-start(bf16[2064,128]{1,0:T(8,128)(2,1)S(1)} %pad_maximum_fusion.1.refs_0_), channel_id=1, source_target_pairs={{8,0},{10,2},{16,8},{18,10},{24,16},{26,18},{28,24},{30,26},{20,28... | collective-permute-start | bytes 1585160 | tf_op jit(solution)/shard_map/ppermute | solution.py:286
  22.4 9.9 %collective-permute-start.4 = (bf16[2,256,128]{2,1,0:T(8,128)(2,1)S(1)}, bf16[2,256,128]{2,1,0:T(8,128)(2,1)S(1)}, u32[]{:S(2)}, u32[]{:S(2)}) collective-permute-start(bf16[2,256,128]{2,1,0:T(8,128)(2,1)S(1)} %slice_select_fusion), channel_id=1, source_target_pairs={{0,2},{2,0},{4,6},{6,4},{8,10},{10,8},{12,14},{14,12},{16,18},{18,... | collective-permute-start | bytes 393224 | tf_op jit(solution)/shard_map/ppermute | solution.py:209
  31.4 9.9 %copy-start.8 = (bf16[1,256,128]{2,1,0:T(8,128)(2,1)}, bf16[1,256,128]{2,1,0:T(8,128)(2,1)S(1)}, u32[]{:S(2)}) copy-start(bf16[1,256,128]{2,1,0:T(8,128)(2,1)S(1)} %pad_bitcast_fusion) | copy-start | bytes 196612
  32.3 9.0 %copy-start.7 = (bf16[2,256,128]{2,1,0:T(8,128)(2,1)}, bf16[2,256,128]{2,1,0:T(8,128)(2,1)S(1)}, u32[]{:S(2)}) copy-start(bf16[2,256,128]{2,1,0:T(8,128)(2,1)S(1)} %collective-permute-done.4) | copy-start | bytes 393220
  33.0 11.6 %collective-permute-start.5 = (bf16[2,256,128]{2,1,0:T(8,128)(2,1)}, bf16[2,256,128]{2,1,0:T(8,128)(2,1)}, u32[]{:S(2)}, u32[]{:S(2)}) collective-permute-start(bf16[2,256,128]{2,1,0:T(8,128)(2,1)} %broadcast_select_fusion.3), channel_id=1, source_target_pairs={{0,1},{1,0},{2,3},{3,2},{4,5},{5,4},{6,7},{7,6},{8,9},{9,8},{10,11... | collective-permute-start | bytes 393224 | tf_op jit(solution)/shard_map/ppermute | solution.py:213
  44.6 4.8 %collective-permute-start.9 = (bf16[2064,128]{1,0:T(8,128)(2,1)S(1)}, bf16[2064,128]{1,0:T(8,128)(2,1)}, u32[]{:S(2)}, u32[]{:S(2)}) collective-permute-start(bf16[2064,128]{1,0:T(8,128)(2,1)S(1)} %pad_maximum_fusion.1.refs_0_), channel_id=1, source_target_pairs={{0,2},{2,0},{4,6},{6,4},{8,10},{10,8},{12,14},{14,12},{16,18},{18,... | collective-permute-start | bytes 1585160 | tf_op jit(solution)/shard_map/ppermute | solution.py:286
  46.2 2.6 %copy-start.9 = (bf16[2,256,128]{2,1,0:T(8,128)(2,1)}, bf16[2,256,128]{2,1,0:T(8,128)(2,1)S(1)}, u32[]{:S(2)}) copy-start(bf16[2,256,128]{2,1,0:T(8,128)(2,1)S(1)} %get-tuple-element.93) | copy-start | bytes 393220
  46.2 9.0 %collective-permute-start.10 = (bf16[2064,128]{1,0:T(8,128)(2,1)}, bf16[2064,128]{1,0:T(8,128)(2,1)}, u32[]{:S(2)}, u32[]{:S(2)}) collective-permute-start(bf16[2064,128]{1,0:T(8,128)(2,1)} %pad_maximum_fusion.refs_1_), channel_id=1, source_target_pairs={{0,2},{2,0},{4,6},{6,4},{8,10},{10,8},{12,14},{14,12},{16,18},{18,... | collective-permute-start | bytes 1585160 | tf_op jit(solution)/shard_map/ppermute | solution.py:286
  46.8 8.4 %collective-permute-start.13 = (bf16[2064,128]{1,0:T(8,128)(2,1)S(1)}, bf16[2064,128]{1,0:T(8,128)(2,1)}, u32[]{:S(2)}, u32[]{:S(2)}) collective-permute-start(bf16[2064,128]{1,0:T(8,128)(2,1)S(1)} %collective-permute-done.11.refs_0_), channel_id=1, source_target_pairs={{0,2},{2,0},{4,6},{6,4},{8,10},{10,8},{12,14},{14,12},{16,18},{18,... | collective-permute-start | bytes 1585160 | tf_op jit(solution)/shard_map/ppermute | solution.py:286
  48.2 9.0 %collective-permute-start.14 = (bf16[2064,128]{1,0:T(8,128)(2,1)S(1)}, bf16[2064,128]{1,0:T(8,128)(2,1)}, u32[]{:S(2)}, u32[]{:S(2)}) collective-permute-start(bf16[2064,128]{1,0:T(8,128)(2,1)S(1)} %collective-permute-done.12.refs_1_), channel_id=1, source_target_pairs={{0,2},{2,0},{4,6},{6,4},{8,10},{10,8},{12,14},{14,12},{16,18},{18,... | collective-permute-start | bytes 1585160 | tf_op jit(solution)/shard_map/ppermute | solution.py:286
  48.2 3.4 %collective-permute-start.6 = (bf16[256,128]{1,0:T(8,128)(2,1)S(1)}, bf16[256,128]{1,0:T(8,128)(2,1)S(1)}, u32[]{:S(2)}, u32[]{:S(2)}) collective-permute-start(bf16[256,128]{1,0:T(8,128)(2,1)S(1)} %slice_bitcast_fusion), channel_id=1, source_target_pairs={{0,2},{2,0},{4,6},{6,4},{8,10},{10,8},{12,14},{14,12},{16,18},{18,... | collective-permute-start | bytes 196616 | tf_op jit(solution)/shard_map/ppermute | solution.py:216
  49.4 25.1 %collective-permute-start.17 = (bf16[2064,128]{1,0:T(8,128)(2,1)S(1)}, bf16[2064,128]{1,0:T(8,128)(2,1)S(1)}, u32[]{:S(2)}, u32[]{:S(2)}) collective-permute-start(bf16[2064,128]{1,0:T(8,128)(2,1)S(1)} %collective-permute-done.11.refs_0_), channel_id=1, source_target_pairs={{0,8},{2,10},{8,16},{10,18},{16,24},{18,26},{24,28},{26,30},{28,20... | collective-permute-start | bytes 1585160 | tf_op jit(solution)/shard_map/ppermute | solution.py:286
  51.6 23.0 %collective-permute-start.18 = (bf16[2064,128]{1,0:T(8,128)(2,1)S(1)}, bf16[2064,128]{1,0:T(8,128)(2,1)}, u32[]{:S(2)}, u32[]{:S(2)}) collective-permute-start(bf16[2064,128]{1,0:T(8,128)(2,1)S(1)} %collective-permute-done.12.refs_1_), channel_id=1, source_target_pairs={{8,0},{10,2},{16,8},{18,10},{24,16},{26,18},{28,24},{30,26},{20,28... | collective-permute-start | bytes 1585160 | tf_op jit(solution)/shard_map/ppermute | solution.py:286
  55.1 19.8 %collective-permute-start.15 = (bf16[2064,128]{1,0:T(8,128)(2,1)S(1)}, bf16[2064,128]{1,0:T(8,128)(2,1)S(1)}, u32[]{:S(2)}, u32[]{:S(2)}) collective-permute-start(bf16[2064,128]{1,0:T(8,128)(2,1)S(1)} %collective-permute-done.7.refs_0_), channel_id=1, source_target_pairs={{0,2},{2,0},{4,6},{6,4},{8,10},{10,8},{12,14},{14,12},{16,18},{18,... | collective-permute-start | bytes 1585160 | tf_op jit(solution)/shard_map/ppermute | solution.py:286
  55.2 22.4 %collective-permute-start.21 = (bf16[2064,128]{1,0:T(8,128)(2,1)S(1)}, bf16[2064,128]{1,0:T(8,128)(2,1)S(1)}, u32[]{:S(2)}, u32[]{:S(2)}) collective-permute-start(bf16[2064,128]{1,0:T(8,128)(2,1)S(1)} %collective-permute-done.7.refs_0_), channel_id=1, source_target_pairs={{0,8},{2,10},{8,16},{10,18},{16,24},{18,26},{24,28},{26,30},{28,20... | collective-permute-start | bytes 1585160 | tf_op jit(solution)/shard_map/ppermute | solution.py:286
  57.2 18.0 %collective-permute-start.16 = (bf16[2064,128]{1,0:T(8,128)(2,1)S(1)}, bf16[2064,128]{1,0:T(8,128)(2,1)S(1)}, u32[]{:S(2)}, u32[]{:S(2)}) collective-permute-start(bf16[2064,128]{1,0:T(8,128)(2,1)S(1)} %collective-permute-done.8.refs_1_), channel_id=1, source_target_pairs={{0,2},{2,0},{4,6},{6,4},{8,10},{10,8},{12,14},{14,12},{16,18},{18,... | collective-permute-start | bytes 1585160 | tf_op jit(solution)/shard_map/ppermute | solution.py:286
  57.4 0.9 copy-start.1
  58.3 0.9 copy-start.2
  59.2 0.8 copy-start.3
  60.0 0.8 copy-start.4
  60.9 1.0 copy-start.6
  74.5 15.3 %collective-permute-start.22 = (bf16[2064,128]{1,0:T(8,128)(2,1)S(1)}, bf16[2064,128]{1,0:T(8,128)(2,1)S(1)}, u32[]{:S(2)}, u32[]{:S(2)}) collective-permute-start(bf16[2064,128]{1,0:T(8,128)(2,1)S(1)} %collective-permute-done.8.refs_1_), channel_id=1, source_target_pairs={{8,0},{10,2},{16,8},{18,10},{24,16},{26,18},{28,24},{30,26},{20,28... | collective-permute-start | bytes 1585160 | tf_op jit(solution)/shard_map/ppermute | solution.py:286
  74.6 15.3 %collective-permute-start.19 = (bf16[2064,128]{1,0:T(8,128)(2,1)S(1)}, bf16[2064,128]{1,0:T(8,128)(2,1)S(1)}, u32[]{:S(2)}, u32[]{:S(2)}) collective-permute-start(bf16[2064,128]{1,0:T(8,128)(2,1)S(1)} %collective-permute-done.17.refs_0_), channel_id=1, source_target_pairs={{0,2},{2,0},{4,6},{6,4},{8,10},{10,8},{12,14},{14,12},{16,18},{18,... | collective-permute-start | bytes 1585160 | tf_op jit(solution)/shard_map/ppermute | solution.py:286
  75.0 15.4 %collective-permute-start.20 = (bf16[2064,128]{1,0:T(8,128)(2,1)}, bf16[2064,128]{1,0:T(8,128)(2,1)S(1)}, u32[]{:S(2)}, u32[]{:S(2)}) collective-permute-start(bf16[2064,128]{1,0:T(8,128)(2,1)} %collective-permute-done.18.refs_1_), channel_id=1, source_target_pairs={{0,2},{2,0},{4,6},{6,4},{8,10},{10,8},{12,14},{14,12},{16,18},{18,... | collective-permute-start | bytes 1585160 | tf_op jit(solution)/shard_map/ppermute | solution.py:286
  75.2 17.2 %collective-permute-start.25 = (bf16[2064,128]{1,0:T(8,128)(2,1)S(1)}, bf16[2064,128]{1,0:T(8,128)(2,1)S(1)}, u32[]{:S(2)}, u32[]{:S(2)}) collective-permute-start(bf16[2064,128]{1,0:T(8,128)(2,1)S(1)} %collective-permute-done.17.refs_0_), channel_id=1, source_target_pairs={{0,8},{2,10},{8,16},{10,18},{16,24},{18,26},{24,28},{26,30},{28,20... | collective-permute-start | bytes 1585160 | tf_op jit(solution)/shard_map/ppermute | solution.py:286
  77.6 23.6 %collective-permute-start.26 = (bf16[2064,128]{1,0:T(8,128)(2,1)}, bf16[2064,128]{1,0:T(8,128)(2,1)S(1)}, u32[]{:S(2)}, u32[]{:S(2)}) collective-permute-start(bf16[2064,128]{1,0:T(8,128)(2,1)} %collective-permute-done.18.refs_1_), channel_id=1, source_target_pairs={{8,0},{10,2},{16,8},{18,10},{24,16},{26,18},{28,24},{30,26},{20,28... | collective-permute-start | bytes 1585160 | tf_op jit(solution)/shard_map/ppermute | solution.py:286
  89.8 11.3 %collective-permute-start.23 = (bf16[2064,128]{1,0:T(8,128)(2,1)S(1)}, bf16[2064,128]{1,0:T(8,128)(2,1)S(1)}, u32[]{:S(2)}, u32[]{:S(2)}) collective-permute-start(bf16[2064,128]{1,0:T(8,128)(2,1)S(1)} %collective-permute-done.21.refs_0_), channel_id=1, source_target_pairs={{0,2},{2,0},{4,6},{6,4},{8,10},{10,8},{12,14},{14,12},{16,18},{18,... | collective-permute-start | bytes 1585160 | tf_op jit(solution)/shard_map/ppermute | solution.py:286
  89.8 13.3 %collective-permute-start.24 = (bf16[2064,128]{1,0:T(8,128)(2,1)S(1)}, bf16[2064,128]{1,0:T(8,128)(2,1)S(1)}, u32[]{:S(2)}, u32[]{:S(2)}) collective-permute-start(bf16[2064,128]{1,0:T(8,128)(2,1)S(1)} %collective-permute-done.22.refs_1_), channel_id=1, source_target_pairs={{0,2},{2,0},{4,6},{6,4},{8,10},{10,8},{12,14},{14,12},{16,18},{18,... | collective-permute-start | bytes 1585160 | tf_op jit(solution)/shard_map/ppermute | solution.py:286
  90.4 18.9 %collective-permute-start.29 = (bf16[2064,128]{1,0:T(8,128)(2,1)S(1)}, bf16[2064,128]{1,0:T(8,128)(2,1)S(1)}, u32[]{:S(2)}, u32[]{:S(2)}) collective-permute-start(bf16[2064,128]{1,0:T(8,128)(2,1)S(1)} %collective-permute-done.21.refs_0_), channel_id=1, source_target_pairs={{0,8},{2,10},{8,16},{10,18},{16,24},{18,26},{24,28},{26,30},{28,20... | collective-permute-start | bytes 1585160 | tf_op jit(solution)/shard_map/ppermute | solution.py:286
  92.4 19.9 %collective-permute-start.30 = (bf16[2064,128]{1,0:T(8,128)(2,1)S(1)}, bf16[2064,128]{1,0:T(8,128)(2,1)S(1)}, u32[]{:S(2)}, u32[]{:S(2)}) collective-permute-start(bf16[2064,128]{1,0:T(8,128)(2,1)S(1)} %collective-permute-done.22.refs_1_), channel_id=1, source_target_pairs={{8,0},{10,2},{16,8},{18,10},{24,16},{26,18},{28,24},{30,26},{20,28... | collective-permute-start | bytes 1585160 | tf_op jit(solution)/shard_map/ppermute | solution.py:286
  101.2 11.6 %collective-permute-start.27 = (bf16[2064,128]{1,0:T(8,128)(2,1)S(1)}, bf16[2064,128]{1,0:T(8,128)(2,1)S(1)}, u32[]{:S(2)}, u32[]{:S(2)}) collective-permute-start(bf16[2064,128]{1,0:T(8,128)(2,1)S(1)} %collective-permute-done.25.refs_0_), channel_id=1, source_target_pairs={{0,2},{2,0},{4,6},{6,4},{8,10},{10,8},{12,14},{14,12},{16,18},{18,... | collective-permute-start | bytes 1585160 | tf_op jit(solution)/shard_map/ppermute | solution.py:286
  101.2 14.5 %collective-permute-start.33 = (bf16[2064,128]{1,0:T(8,128)(2,1)S(1)}, bf16[2064,128]{1,0:T(8,128)(2,1)S(1)}, u32[]{:S(2)}, u32[]{:S(2)}) collective-permute-start(bf16[2064,128]{1,0:T(8,128)(2,1)S(1)} %collective-permute-done.25.refs_0_), channel_id=1, source_target_pairs={{0,8},{2,10},{8,16},{10,18},{16,24},{18,26},{24,28},{26,30},{28,20... | collective-permute-start | bytes 1585160 | tf_op jit(solution)/shard_map/ppermute | solution.py:286
  112.2 13.9 %collective-permute-start.34 = (bf16[2064,128]{1,0:T(8,128)(2,1)S(1)}, bf16[2064,128]{1,0:T(8,128)(2,1)S(1)}, u32[]{:S(2)}, u32[]{:S(2)}) collective-permute-start(bf16[2064,128]{1,0:T(8,128)(2,1)S(1)} %collective-permute-done.30.refs_1_), channel_id=1, source_target_pairs={{8,0},{10,2},{16,8},{18,10},{24,16},{26,18},{28,24},{30,26},{20,28... | collective-permute-start | bytes 1585160 | tf_op jit(solution)/shard_map/ppermute | solution.py:286
  112.2 13.9 %collective-permute-start.28 = (bf16[2064,128]{1,0:T(8,128)(2,1)S(1)}, bf16[2064,128]{1,0:T(8,128)(2,1)S(1)}, u32[]{:S(2)}, u32[]{:S(2)}) collective-permute-start(bf16[2064,128]{1,0:T(8,128)(2,1)S(1)} %collective-permute-done.26.refs_1_), channel_id=1, source_target_pairs={{0,2},{2,0},{4,6},{6,4},{8,10},{10,8},{12,14},{14,12},{16,18},{18,... | collective-permute-start | bytes 1585160 | tf_op jit(solution)/shard_map/ppermute | solution.py:286
  112.2 20.6 %collective-permute-start.31 = (bf16[2064,128]{1,0:T(8,128)(2,1)S(1)}, bf16[2064,128]{1,0:T(8,128)(2,1)S(1)}, u32[]{:S(2)}, u32[]{:S(2)}) collective-permute-start(bf16[2064,128]{1,0:T(8,128)(2,1)S(1)} %collective-permute-done.29.refs_0_), channel_id=1, source_target_pairs={{0,2},{2,0},{4,6},{6,4},{8,10},{10,8},{12,14},{14,12},{16,18},{18,... | collective-permute-start | bytes 1585160 | tf_op jit(solution)/shard_map/ppermute | solution.py:286
  112.8 20.1 %collective-permute-start.32 = (bf16[2064,128]{1,0:T(8,128)(2,1)S(1)}, bf16[2064,128]{1,0:T(8,128)(2,1)S(1)}, u32[]{:S(2)}, u32[]{:S(2)}) collective-permute-start(bf16[2064,128]{1,0:T(8,128)(2,1)S(1)} %collective-permute-done.30.refs_1_), channel_id=1, source_target_pairs={{0,2},{2,0},{4,6},{6,4},{8,10},{10,8},{12,14},{14,12},{16,18},{18,... | collective-permute-start | bytes 1585160 | tf_op jit(solution)/shard_map/ppermute | solution.py:286
  115.7 28.3 %collective-permute-start.35 = (bf16[2064,128]{1,0:T(8,128)(2,1)S(1)}, bf16[2064,128]{1,0:T(8,128)(2,1)S(1)}, u32[]{:S(2)}, u32[]{:S(2)}) collective-permute-start(bf16[2064,128]{1,0:T(8,128)(2,1)S(1)} %collective-permute-done.33.refs_0_), channel_id=1, source_target_pairs={{0,2},{2,0},{4,6},{6,4},{8,10},{10,8},{12,14},{14,12},{16,18},{18,... | collective-permute-start | bytes 1585160 | tf_op jit(solution)/shard_map/ppermute | solution.py:286
  126.1 17.8 %collective-permute-start.36 = (bf16[2064,128]{1,0:T(8,128)(2,1)S(1)}, bf16[2064,128]{1,0:T(8,128)(2,1)S(1)}, u32[]{:S(2)}, u32[]{:S(2)}) collective-permute-start(bf16[2064,128]{1,0:T(8,128)(2,1)S(1)} %collective-permute-done.34.refs_1_), channel_id=1, source_target_pairs={{0,2},{2,0},{4,6},{6,4},{8,10},{10,8},{12,14},{14,12},{16,18},{18,... | collective-permute-start | bytes 1585160 | tf_op jit(solution)/shard_map/ppermute | solution.py:286
  148.4 6.3 %copy-start = (f32[128,256]{1,0:T(8,128)}, f32[128,256]{1,0:T(8,128)S(1)}, u32[]{:S(2)}) copy-start(f32[128,256]{1,0:T(8,128)S(1)} %get-tuple-element.85.gram) | copy-start | bytes 393220
  148.4 6.3 %collective-permute-start.37 = (f32[128,256]{1,0:T(8,128)S(1)}, f32[128,256]{1,0:T(8,128)S(1)}, u32[]{:S(2)}, u32[]{:S(2)}) collective-permute-start(f32[128,256]{1,0:T(8,128)S(1)} %get-tuple-element.85.gram), channel_id=1, source_target_pairs={{0,1},{1,0},{2,3},{3,2},{4,5},{5,4},{6,7},{7,6},{8,9},{9,8},{10,11... | collective-permute-start | bytes 393224 | tf_op jit(solution)/shard_map/ppermute | solution.py:347
  154.7 0.7 copy-start.12
where the time goes:
time: 159 us; the launch traced here: 158 us
  Pallas kernels  57.4 us (36%)
  starting transfers between devices  47.3 us (30%)
  waiting for transfers between devices  33.6 us (21%)
  local copies, waits for them, and re-layouts  10.8 us (7%)
  other arithmetic  8.42 us (5%)
    pallas_call x9, Pallas kernels, block_call(): pl.pallas_call(functools.partial(block_kernel, slot, half, count, len(aft...  52.9 us
    ppermute x30, waiting for transfers between devices, over(): return lax.ppermute(value, 'row', perm)  25.2 us
    ppermute x30, starting transfers between devices, over(): return lax.ppermute(value, 'row', perm)  16.7 us
    ppermute x4, starting transfers between devices, spread_direct(): total = total + lax.ppermute(pay, both, pairs)  10.6 us
    ppermute x1, starting transfers between devices, spread_direct(): lax.ppermute(jnp.where(is_panel, total[:slabs], total[slabs:]), both, hop)  8.93 us
    ppermute x1, starting transfers between devices, spread_direct(): lax.ppermute(jnp.where(is_panel, far, slab), 'col', [(0, 1), (1, 0)])  8.3 us
    unnamed x26, local copies, waits for them, and re-layouts  5.2 us
    ppermute x1, waiting for transfers between devices, shards(): other = lax.ppermute(gram, 'col', [(0, 1), (1, 0)])  3.39 us
  transfers between devices with their start and end apart: 38, of which 9 were waited for; matrix products, arithmetic and copies ran while one was open for 8% of the time, Pallas kernels for 32%

commit v1 on v0

v1 whole, which is shorter than its diff:
```python
import functools

import jax
import jax.numpy as jnp
import numpy as np
from jax import lax
from jax.experimental import pallas as pl
from jax.experimental.pallas import tpu as pltpu
from jax.sharding import PartitionSpec as P

HIGHEST = lax.Precision.HIGHEST
F32 = jnp.float32
BF16 = jnp.bfloat16


def dot_nt(a, b):
    return lax.dot_general(a, b, (((1,), (1,)), ((), ())), preferred_element_type=F32)


def prep_kernel(pick, slab_a, slab_b, panel_a, panel_b, w_a, w_b, inverse, *outs):
    turned, fac = outs
    slabs, rows, width = slab_a.shape
    lanes = rows // width
    panel = jnp.where(pick[1] > 0, panel_a[...], panel_b[...])
    w = jnp.where(pick[2] > 0, w_a[...], w_b[...]).astype(F32)
    p_t = panel.T
    turned[slabs] = p_t
    for i in range(slabs):
        s = jnp.where(pick[0] > 0, slab_a[i], slab_b[i])
        turned[i] = s.T
        row = jnp.concatenate([w[i * lanes + n : i * lanes + n + 1] for n in range(lanes)], 1)
        scaled = p_t * row.astype(BF16)
        hess = jnp.dot(scaled, s, preferred_element_type=F32)
        fac[i * width : (i + 1) * width] = jnp.dot(
            hess, inverse[...], precision=HIGHEST, preferred_element_type=F32
        )


def prep_call(pick, slab_a, slab_b, panel_a, panel_b, w_a, w_b, inverse):
    slabs, rows, width = slab_a.shape
    return pl.pallas_call(
        prep_kernel,
        in_specs=[pl.BlockSpec(memory_space=pltpu.SMEM)]
        + [pl.BlockSpec(memory_space=pltpu.VMEM)] * 7,
        out_specs=[pl.BlockSpec(memory_space=pltpu.VMEM)] * 2,
        out_shape=[
            jax.ShapeDtypeStruct((slabs + 1, width, rows), BF16),
            jax.ShapeDtypeStruct((slabs * width, width), F32),
        ],
    )(pick, slab_a, slab_b, panel_a, panel_b, w_a, w_b, inverse)


def block_kernel(slot, half, count, skip, sc, w, turned, fac, gin, *refs):
    units = refs[: count // 2]
    out, gout, token, jbuf, pbuf, obuf, in_sem, out_sem = refs[count // 2 + skip :]
    slabs = w.shape[0]
    _, width, rows = turned.shape
    extra = sc.shape[0] - slabs - 1
    size, tail = half * rows, pbuf.shape[1]

    def fetch(b):
        unit, h = units[b // 2], b % 2
        return (
            pltpu.make_async_copy(unit.at[pl.ds(h * size, size)], jbuf.at[b], in_sem.at[0, b]),
            pltpu.make_async_copy(
                unit.at[pl.ds(2 * size + h * tail, tail)], pbuf.at[b], in_sem.at[1, b]
            ),
        )

    for b in range(count):
        for copy in fetch(b):
            copy.start()
    token[...] = jnp.zeros_like(token)
    gout[...] = gin[...]
    fac_b = fac[...].astype(BF16)

    def write(b):
        col = pl.multiple_of(sc[slot + b] * width, half * width)
        return pltpu.make_async_copy(
            obuf.at[b % 2], out.at[:, pl.ds(col, half * width)], out_sem.at[b % 2]
        )

    def one(b, carry):
        pltpu.make_async_copy(units[0].at[pl.ds(0, size)], jbuf.at[b], in_sem.at[0, b]).wait()
        pltpu.make_async_copy(units[0].at[pl.ds(0, tail)], pbuf.at[b], in_sem.at[1, b]).wait()

        @pl.when(b >= 2)
        def _():
            write(b - 2).wait()

        first = sc[slot + b]
        pw = pbuf[b].astype(F32)
        acc = None
        parts, panels = [], []
        for k in range(half):
            j = first + k
            jac_t = jbuf[b, k * rows : (k + 1) * rows, :].T
            ws = [
                jnp.where(j == sc[extra + 1 + i], 0.0, w[i, pl.ds(j, 1), :]).astype(BF16)
                for i in range(slabs)
            ]
            row_p = jnp.concatenate([pw[k : k + 1], pw[half + k : half + k + 1]], 1).astype(BF16)
            parts.append(
                dot_nt(jac_t, jnp.concatenate([turned[i] * ws[i] for i in range(slabs)], 0))
            )
            panels.append(dot_nt(jac_t, turned[slabs] * row_p).astype(BF16))
            part = dot_nt(jac_t, jnp.concatenate([jac_t * ws[i] for i in range(slabs)], 0))
            acc = part if acc is None else acc + part
        corr = jnp.dot(fac_b, jnp.concatenate(panels, 1), preferred_element_type=F32)
        o = obuf.at[b % 2]
        for k in range(half):
            for i in range(slabs):
                here = (slice(i * width, (i + 1) * width), slice(k * width, (k + 1) * width))
                o[here] = parts[k][:, i * width : (i + 1) * width] - corr[here]
        gout[...] += acc
        where_p = sc[extra] - first

        @pl.when((where_p >= 0) & (where_p < half))
        def _():
            for k in range(half):

                @pl.when(where_p == k)
                def _():
                    o[:, k * width : (k + 1) * width] = fac[...]

        write(b).start()
        return carry

    lax.fori_loop(0, count, one, 0)
    for b in range(max(count - 2, 0), count):
        write(b).wait()


def block_call(slot, half, sc, units, w, turned, fac, gram, after, out, shape):
    slabs = w.shape[0]
    _, width, rows = turned.shape
    count = 2 * len(units)
    args = [w, turned, fac, gram] + list(units) + list(after)
    specs = [pl.BlockSpec(memory_space=pltpu.VMEM)] * 4
    specs += [pl.BlockSpec(memory_space=pltpu.HBM)] * len(units)
    specs += [pl.BlockSpec(memory_space=pl.ANY)] * len(after)
    aliases = {4: 1}
    if out is not None:
        aliases[1 + len(args)] = 0
        args.append(out)
        specs.append(pl.BlockSpec(memory_space=pl.ANY))
    stations = half * count
    tail = units[0].shape[0] // 2 - half * rows
    return pl.pallas_call(
        functools.partial(block_kernel, slot, half, count, len(after) + (out is not None)),
        in_specs=[pl.BlockSpec(memory_space=pltpu.SMEM)] + specs,
        out_specs=[pl.BlockSpec(memory_space=pl.ANY)] + [pl.BlockSpec(memory_space=pltpu.VMEM)] * 2,
        out_shape=[
            jax.ShapeDtypeStruct(shape, F32),
            jax.ShapeDtypeStruct(gram.shape, F32),
            jax.ShapeDtypeStruct((8, 128), F32),
        ],
        scratch_shapes=[
            pltpu.VMEM((count, half * rows, width), BF16),
            pltpu.VMEM((count, tail, width), BF16),
            pltpu.VMEM((2, slabs * width, half * width), F32),
            pltpu.SemaphoreType.DMA((2, count)),
            pltpu.SemaphoreType.DMA((2,)),
        ],
        input_output_aliases=aliases,
        compiler_params=pltpu.CompilerParams(vmem_limit_bytes=24 << 20),
        cost_estimate=pl.CostEstimate(
            flops=stations * 14 * width * width * rows,
            bytes_accessed=stations * (slabs * width * width * 4 + rows * width * 2),
            transcendentals=0,
        ),
    )(sc, *args)


def patch_kernel(sc, gram, other, damp, tile, out):
    i = pl.program_id(0)
    width = tile.shape[0]
    g = (gram[...] + other[...]).T
    eye = lax.broadcasted_iota(jnp.int32, (width, width), 0) == lax.broadcasted_iota(
        jnp.int32, (width, width), 1
    )
    full = jnp.where(eye, g * (1.0 + damp[pl.ds(i, 1), :]), g)
    out[...] = jnp.where(sc[2 * i + 1] > 0, tile[...] + full, tile[...])


def patch_call(sc, gram, other, damping, out):
    slabs, width = damping.shape
    tile = pl.BlockSpec((width, width), lambda i, s: (i, s[2 * i]))
    part = pl.BlockSpec((width, width), lambda i, s: (0, i))
    return pl.pallas_call(
        patch_kernel,
        grid_spec=pltpu.PrefetchScalarGridSpec(
            num_scalar_prefetch=1,
            grid=(slabs,),
            in_specs=[part, part, pl.BlockSpec((slabs, width), lambda i, s: (0, 0)), tile],
            out_specs=tile,
        ),
        out_shape=jax.ShapeDtypeStruct(out.shape, F32),
        input_output_aliases={4: 0},
    )(sc, gram, other, damping, out)


def chip_cycle(chips, cols):
    if cols == 2:
        return list(range(0, chips, 2)) + list(range(chips - 1, 0, -2))
    half = chips // 2
    return list(range(half)) + list(range(chips - 1, half - 1, -1))


def spread_direct(jacobian, weights, row, col, later):
    per_dev, samples, width = jacobian.shape
    slabs = weights.shape[0]
    core, y = row % 2, (row // 2) % 2
    both = ("row", "col")
    w_mine = weights[:, -1].reshape(slabs * samples // width, width)
    w_mine = jnp.pad(w_mine, ((0, 16 - w_mine.shape[0]), (0, 0)))
    quads = 2 * slabs
    ends = [None, (11, 1), (7, 1), (3, 1)]
    is_panel = col == 1
    mine = jacobian[per_dev - 1]
    panel_pay = jnp.concatenate([mine[None]] + [jnp.zeros_like(jacobian[: quads - 1])], 0)
    total = jnp.where((row == 15) & is_panel, panel_pay, jnp.zeros_like(panel_pay))
    total = total + jnp.where((row == 0) & (col == 0), jacobian[:quads], jnp.zeros_like(panel_pay))
    for m in (1, 2, 3, 0):
        pay = jnp.where(is_panel, panel_pay, lax.slice_in_dim(jacobian, quads * m, quads * (m + 1)))
        pairs = [(2, 2 * (8 + 2 * m))]
        if m:
            pairs += [(0, 4 * m), (31, 2 * ends[m][0] + ends[m][1])]
        total = total + lax.ppermute(pay, both, pairs)
    hop = [(2 * r, 2 * (r ^ 1)) for r in range(16)] + [(2 * r + 1, 2 * (r ^ 2) + 1) for r in range(16)]
    total, later = lax.optimization_barrier((total, later))
    first = lax.ppermute(jnp.where(is_panel, total[:slabs], total[slabs:]), both, hop)
    panel = jnp.where(y == 1, total[0], first[0])
    w_rest = jnp.pad(w_mine, ((0, samples - 16), (0, 0)))
    mixed = jnp.where(core == 0, total[:slabs], first)
    send = jnp.where(is_panel, jnp.stack([panel, w_rest], 0), mixed)
    second = lax.ppermute(send, "col", [(0, 1), (1, 0)])
    far = jnp.where(is_panel, panel, second[0])
    third = lax.ppermute(far, "row", [(r, r ^ 1) for r in range(16)])
    pick = jnp.stack([is_panel, core == 1, is_panel]).astype(jnp.int32)
    return (pick, second, send, far, third, w_mine, second[1, :16]), later


def spread_general(jacobian, weights, row, col, rows, cols):
    per_dev, samples, width = jacobian.shape
    slabs = weights.shape[0]
    holds = (row == rows - 1) & (col == cols - 1)
    panel = lax.psum(
        jnp.where(holds, jacobian[per_dev - 1], jnp.zeros_like(jacobian[0])), ("row", "col")
    )
    w_panel = lax.psum(
        jnp.where(col == cols - 1, weights[:, -1], jnp.zeros_like(weights[:, 0])), "col"
    )
    slab = jnp.zeros((slabs, samples, width), BF16)
    for offset in range(0, per_dev, slabs):
        piece = lax.slice_in_dim(jacobian, offset, offset + slabs, axis=0)
        pairs = []
        for t in range(rows):
            if (t * slabs) % per_dev == offset:
                home = (t * slabs) // per_dev
                source, target = (home % rows) * cols + home // rows, t * cols
                if source == target:
                    slab = slab + jnp.where((row == t) & (col == 0), piece, jnp.zeros_like(piece))
                else:
                    pairs.append((source, target))
        if pairs:
            slab = slab + lax.ppermute(piece, ("row", "col"), pairs)
    spread = slab
    for c in range(1, cols):
        spread = spread + lax.ppermute(slab, "col", [(0, c)])
    lanes = samples // width
    w_panel = w_panel.reshape(slabs * lanes, width)
    w_panel = jnp.pad(w_panel, ((0, -w_panel.shape[0] % 16), (0, 0)))
    return (jnp.ones((3,), jnp.int32), spread, spread, panel, panel, w_panel, w_panel)


def shards(jacobian, weights, panel_weights, damping, panel_inverse):
    per_dev, samples, width = jacobian.shape
    slabs, col_block, _ = weights.shape
    rows = lax.axis_size("row")
    cols = lax.axis_size("col")
    row = lax.axis_index("row")
    col = lax.axis_index("col")
    panel_id = col_block * cols - 1

    chips = rows // 2
    cycle = chip_cycle(chips, cols)
    place = {c: p for p, c in enumerate(cycle)}
    ring = [(2 * c, 2 * cycle[(place[c] + 1) % chips]) for c in cycle]
    ring += [(2 * c + 1, 2 * cycle[(place[c] - 1) % chips] + 1) for c in cycle]
    swap = [(r, r ^ 1) for r in range(rows)]
    half = per_dev // 2

    def over(value, perm):
        return lax.ppermute(value, "row", perm)

    tail = panel_weights.reshape(2, half, samples // width, width).swapaxes(1, 2)
    tail = tail.reshape(2, per_dev, width)
    tail = jnp.pad(tail, ((0, 0), (0, -per_dev % 16), (0, 0))).reshape(-1, width)
    own = jnp.concatenate([jacobian.reshape(per_dev * samples, width), tail], 0)
    other_core = over(own, swap)
    if (rows, cols, per_dev) == (16, 2, 8 * slabs):
        small, other_core = spread_direct(jacobian, weights, row, col, other_core)
    else:
        small = spread_general(jacobian, weights, row, col, rows, cols)
    hops = [over(own, ring), over(other_core, ring)]
    turned, factor = prep_call(*small, panel_inverse)
    w32 = weights.astype(F32)

    far = chips // 2
    order = [None] + [(d, s) for d in range(1, far) for s in (0, 1)] + [(far, 0)]
    table = np.zeros((rows, len(order), 2, 2), np.int32)
    for r in range(rows):
        p, c = place[r // 2], r % 2
        for n, hop in enumerate(order):
            if hop is None:
                owners = (r, r ^ 1)
            else:
                d, s = hop
                step = d if c else -d
                owners = (
                    2 * cycle[(p + step) % chips] + (c ^ s),
                    2 * cycle[(p - step) % chips] + (1 ^ c ^ s),
                )
            for u, owner in enumerate(owners):
                table[r, n, u] = owner * per_dev + np.array([0, half])
    table = table.reshape(rows, -1)
    starts = lax.dynamic_index_in_dim(jnp.asarray(table), row, 0, keepdims=False)
    base = col * col_block
    ids = row * slabs + jnp.arange(slabs, dtype=jnp.int32) - base
    held = ((ids >= 0) & (ids < col_block)).astype(jnp.int32)
    spots = jnp.stack([jnp.clip(ids, 0, col_block - 1), held], 1).reshape(-1)
    sc = jnp.concatenate([starts, (panel_id - base)[None].astype(jnp.int32), ids])
    sc, spots = lax.optimization_barrier((sc, spots))

    tokens, after = [], []
    gram = jnp.zeros((width, slabs * width), F32)
    shape = (slabs * width, col_block * width)
    out = None

    def compute(units):
        nonlocal out, gram
        out, gram, token = block_call(
            4 * len(tokens), half, sc, units, w32, turned, factor, gram, tuple(after), out, shape
        )
        after.clear()
        tokens.append(token)

    for q in range(len(order) - 1):
        x = hops[q]
        if q == 0:
            x, factor = lax.optimization_barrier((x, factor))
            compute([own, other_core])
        else:
            x, ready = lax.optimization_barrier((x, tokens[q - 1 if q < len(order) - 2 else q]))
            after.append(ready)
        if q + 2 < len(order) - 1:
            hops.append(over(x, ring))
        compute([x, over(x, swap)])
    if cols == 2:
        other = lax.ppermute(gram, "col", [(0, 1), (1, 0)])
    else:
        other = lax.psum(gram, "col") - gram
    return patch_call(spots, gram, other, damping, out)


def solution(mesh):
    return jax.shard_map(
        shards,
        mesh=mesh,
        in_specs=(
            P(("col", "row"), None, None),
            P("row", "col", None),
            P(("col", "row"), None),
            P("row", None),
            P(),
        ),
        out_specs=P("row", "col"),
        check_vma=False,
    )
```

time: 159 us -> 129 us (0.81)
  starting transfers between devices: 47.3 us -> 28.7 us
  local copies, waits for them, and re-layouts: 10.8 us -> 7.02 us
  waiting for transfers between devices: 33.6 us -> 30 us
  other arithmetic: 8.42 us -> 6.33 us
  Pallas kernels: 57.4 us -> 55.6 us
    ppermute x30 -> x15, waiting for transfers between devices: 25.2 us -> 13.3 us  [over(): return lax.ppermute(value, 'row', perm)]
    ppermute x2, starting transfers between devices: 8.87 us -> 0.14 us  [the longest x1 0.07 us: spread_direct(): third = lax.ppermute(far, 'row', [(r, r ^ 1) for r in range(16)])]
    ppermute x30 -> x15, starting transfers between devices: 16.7 us -> 9.76 us  [over(): return lax.ppermute(value, 'row', perm)]
    ppermute x4, waiting for transfers between devices: 2.51 us -> 6.94 us  [spread_direct(): total = total + lax.ppermute(pay, both, pairs)]
    select_n x3 -> x2, other arithmetic: 3.75 us -> 0.04 us  [the longest x1 0.03 us: spread_direct(): send = jnp.where(is_panel, jnp.stack([panel, w_rest], 0), mixed)]
    ppermute x2, waiting for transfers between devices: 1.49 us -> 4.1 us  [the longest x1 3.44 us: spread_direct(): second = lax.ppermute(send, 'col', [(0, 1), (1, 0)])]
    ppermute x1, waiting for transfers between devices: 3.39 us -> 5.52 us  [shards(): other = lax.ppermute(gram, 'col', [(0, 1), (1, 0)])]
    ppermute x1, starting transfers between devices: 2.18 us -> 0.07 us  [shards(): other = lax.ppermute(gram, 'col', [(0, 1), (1, 0)])]
  transfers between devices with their start and end apart: 38 -> 23, of which waited for: 9 -> 10; matrix products, arithmetic and copies ran while one was open for 8% -> 5% of each run, Pallas kernels for 32% -> 36%
where the time goes in v1:
time: 129 us; the launch traced here: 128 us
  Pallas kernels  55.6 us (43%)
  waiting for transfers between devices  30 us (23%)
  starting transfers between devices  28.7 us (22%)
  local copies, waits for them, and re-layouts  7.02 us (5%)
  other arithmetic  6.33 us (5%)
    pallas_call x8, Pallas kernels, block_call(): pl.pallas_call(functools.partial(block_kernel, slot, half, count, len(aft...  51 us
    ppermute x15, waiting for transfers between devices, over(): return lax.ppermute(value, 'row', perm)  13.3 us
    ppermute x4, starting transfers between devices, spread_direct(): total = total + lax.ppermute(pay, both, pairs)  11.5 us
    ppermute x15, starting transfers between devices, over(): return lax.ppermute(value, 'row', perm)  9.76 us
    ppermute x1, starting transfers between devices, spread_direct(): lax.ppermute(jnp.where(is_panel, total[:slabs], total[slabs:]), both, hop)  7.3 us
    ppermute x4, waiting for transfers between devices, spread_direct(): total = total + lax.ppermute(pay, both, pairs)  6.94 us
    ppermute x1, waiting for transfers between devices, shards(): other = lax.ppermute(gram, 'col', [(0, 1), (1, 0)])  5.52 us
    unnamed x24, local copies, waits for them, and re-layouts  4.34 us
  transfers between devices with their start and end apart: 23, of which 10 were waited for; matrix products, arithmetic and copies ran while one was open for 5% of the time, Pallas kernels for 36%

profile of v1, /device:TPU:0, one launch (start us, length us, event | category | flops | bytes accessed | tf_op | source)
XLA Modules:
  0.0 128.0 jit_solution(8047244034770484575)
XLA Ops:
  0.0 2.4 %pad_maximum_fusion.refs_0_ = bf16[4128,128]{1,0:T(8,128)(2,1)} fusion(bf16[32,128]{1,0:T(8,128)(2,1)} %bitcast.18, bf16[4096,128]{1,0:T(8,128)(2,1)} %bitcast.17), kind=kLoop, calls=%fused_computation | loop fusion | flops 2113536 | bytes 2113536 | tf_op jit(solution)/shard_map/concatenate | solution.py:300
  2.4 0.5 collective-permute-start.4
  2.9 0.9 pad_select_fusion.3
  3.7 1.4 %collective-permute-start.3 = (bf16[4,256,128]{2,1,0:T(8,128)(2,1)S(1)}, bf16[4,256,128]{2,1,0:T(8,128)(2,1)}, u32[]{:S(2)}, u32[]{:S(2)}) collective-permute-start(bf16[4,256,128]{2,1,0:T(8,128)(2,1)S(1)} %get-tuple-element.92), channel_id=1, source_target_pairs={{2,16}} | collective-permute-start | bytes 786440 | tf_op jit(solution)/shard_map/ppermute | solution.py:229
  5.1 6.1 %collective-permute-start.2 = (bf16[4,256,128]{2,1,0:T(8,128)(2,1)}, bf16[4,256,128]{2,1,0:T(8,128)(2,1)}, u32[]{:S(2)}, u32[]{:S(2)}) collective-permute-start(bf16[4,256,128]{2,1,0:T(8,128)(2,1)} %get-tuple-element.91), channel_id=1, source_target_pairs={{2,28},{0,12},{31,7}} | collective-permute-start | bytes 786440 | tf_op jit(solution)/shard_map/ppermute | solution.py:229
  11.2 2.0 %collective-permute-start.1 = (bf16[4,256,128]{2,1,0:T(8,128)(2,1)}, bf16[4,256,128]{2,1,0:T(8,128)(2,1)}, u32[]{:S(2)}, u32[]{:S(2)}) collective-permute-start(bf16[4,256,128]{2,1,0:T(8,128)(2,1)} %get-tuple-element.90), channel_id=1, source_target_pairs={{2,24},{0,8},{31,15}} | collective-permute-start | bytes 786440 | tf_op jit(solution)/shard_map/ppermute | solution.py:229
  13.2 2.0 %collective-permute-start = (bf16[4,256,128]{2,1,0:T(8,128)(2,1)S(1)}, bf16[4,256,128]{2,1,0:T(8,128)(2,1)}, u32[]{:S(2)}, u32[]{:S(2)}) collective-permute-start(bf16[4,256,128]{2,1,0:T(8,128)(2,1)S(1)} %get-tuple-element.89), channel_id=1, source_target_pairs={{2,20},{0,4},{31,23}} | collective-permute-start | bytes 786440 | tf_op jit(solution)/shard_map/ppermute | solution.py:229
  15.2 0.1 pad_add_fusion
  15.3 0.7 slice_reduce_fusion
  16.0 0.1 collective-permute-start.8
  16.1 1.3 %collective-permute-done.2 = bf16[4,256,128]{2,1,0:T(8,128)(2,1)} collective-permute-done((bf16[4,256,128]{2,1,0:T(8,128)(2,1)}, bf16[4,256,128]{2,1,0:T(8,128)(2,1)}, u32[]{:S(2)}, u32[]{:S(2)}) %collective-permute-start.2) | collective-permute-done | bytes 262176 | tf_op jit(solution)/shard_map/ppermute | solution.py:229
  17.4 5.6 %collective-permute-done.1 = bf16[4,256,128]{2,1,0:T(8,128)(2,1)} collective-permute-done((bf16[4,256,128]{2,1,0:T(8,128)(2,1)}, bf16[4,256,128]{2,1,0:T(8,128)(2,1)}, u32[]{:S(2)}, u32[]{:S(2)}) %collective-permute-start.1) | collective-permute-done | bytes 262176 | tf_op jit(solution)/shard_map/ppermute | solution.py:229
  23.0 0.0 collective-permute-done
  23.1 1.3 fusion.4
  24.4 7.3 %collective-permute-start.5 = (bf16[2,256,128]{2,1,0:T(8,128)(2,1)S(1)}, bf16[2,256,128]{2,1,0:T(8,128)(2,1)S(1)}, u32[]{:S(2)}, u32[]{:S(2)}) collective-permute-start(bf16[2,256,128]{2,1,0:T(8,128)(2,1)S(1)} %slice_select_fusion), channel_id=1, source_target_pairs={{0,2},{2,0},{4,6},{6,4},{8,10},{10,8},{12,14},{14,12},{16,18},{18,... | collective-permute-start | bytes 393224 | tf_op jit(solution)/shard_map/ppermute | solution.py:232
  31.7 0.7 dynamic-slice_bitcast_fusion
  32.4 0.1 collective-permute-start.10
  32.5 0.2 collective-permute-done.5
  32.7 0.1 collective-permute-start.6
  32.8 0.1 pad_add_fusion.1.sc
  32.9 1.0 convert_element_type.21.w
  33.9 0.6 reshape.44.sc
  34.5 0.6 add_convert_fusion.pick
  35.1 3.4 %collective-permute-done.6.slab_a = bf16[2,256,128]{2,1,0:T(8,128)(2,1)S(1)} collective-permute-done((bf16[2,256,128]{2,1,0:T(8,128)(2,1)S(1)}, bf16[2,256,128]{2,1,0:T(8,128)(2,1)S(1)}, u32[]{:S(2)}, u32[]{:S(2)}) %collective-permute-start.6) | collective-permute-done | bytes 131104 | tf_op jit(solution)/shard_map/ppermute | solution.py:237
  38.6 0.1 collective-permute-start.7
  38.6 0.6 slice_bitcast_fusion.w_b
  39.2 0.7 collective-permute-done.7.panel_b
  39.9 0.6 copy-done.10
  40.5 2.1 %shard_map.64 = (bf16[3,128,256]{2,1,0:T(8,128)(2,1)}, f32[256,128]{1,0:T(8,128)}) custom-call(s32[3]{0:T(128)} %add_convert_fusion.pick, bf16[2,256,128]{2,1,0:T(8,128)(2,1)} %copy-done.7, bf16[2,256,128]{2,1,0:T(8,128)(2,1)} %copy-done.6, bf16[256,128]{1,0:T(8,128)(2,1)} %copy-done.8, bf16[256,128]{1,0:T(8,128)(2,1)} %copy-done.10, ...), custom_call_target="tpu_custom_call" | custom-call | tf_op jit(solution)/shard_map/pallas_call | solution.py:41
  42.7 0.0 collective-permute-done.8.refs_0_
  42.7 0.2 collective-permute-start.9
  42.8 0.0 collective-permute-start.12
  42.8 0.0 copy-start.1
  42.8 0.9 copy-done.1
  43.8 0.9 copy-done.2
  44.7 1.2 copy-done.4
  45.9 7.0 %shard_map.65 = (f32[256,32768]{1,0:T(8,128)}, f32[128,256]{1,0:T(8,128)S(1)}, f32[8,128]{1,0:T(8,128)S(1)}) custom-call(s32[35]{0:T(128)S(1)} %pad_add_fusion.1.sc, f32[2,256,256]{2,1,0:T(8,128)S(1)} %convert_element_type.21.w, bf16[3,128,256]{2,1,0:T(8,128)(2,1)S(1)} %copy-done.1, f32[256,128]{1,0:T(8,128)S(1)} %copy-done.2, ...), custom_call_target="tpu_custom_call", output_to_operand_aliasing={{1}: (4, {})} | custom-call | flops 1879048192 | bytes 6291456 | tf_op jit(solution)/shard_map/pallas_call | solution.py:149
  52.9 0.0 collective-permute-done.10.refs_0_
  52.9 1.2 collective-permute-start.11
  54.1 1.0 collective-permute-start.14
  55.0 0.0 collective-permute-done.9.refs_1_
  55.0 6.1 %shard_map.66 = (f32[256,32768]{1,0:T(8,128)}, f32[128,256]{1,0:T(8,128)S(1)}, f32[8,128]{1,0:T(8,128)S(1)}) custom-call(s32[35]{0:T(128)S(1)} %pad_add_fusion.1.sc, f32[2,256,256]{2,1,0:T(8,128)S(1)} %convert_element_type.21.w, bf16[3,128,256]{2,1,0:T(8,128)(2,1)S(1)} %copy-done.1, ...), custom_call_target="tpu_custom_call", output_to_operand_aliasing={{1}: (4, {}), {0}: (7, {})} | custom-call | flops 1879048192 | bytes 6291456 | tf_op jit(solution)/shard_map/pallas_call | solution.py:149
  61.2 1.3 collective-permute-start.13
  62.5 0.6 collective-permute-start.16
  63.0 0.0 collective-permute-done.11.refs_1_
  63.0 6.1 %shard_map.67 = (f32[256,32768]{1,0:T(8,128)}, f32[128,256]{1,0:T(8,128)S(1)}, f32[8,128]{1,0:T(8,128)S(1)}) custom-call(s32[35]{0:T(128)S(1)} %pad_add_fusion.1.sc, f32[2,256,256]{2,1,0:T(8,128)S(1)} %convert_element_type.21.w, bf16[3,128,256]{2,1,0:T(8,128)(2,1)S(1)} %copy-done.1, ...), custom_call_target="tpu_custom_call", output_to_operand_aliasing={{1}: (4, {}), {0}: (8, {})} | custom-call | flops 1879048192 | bytes 6291456 | tf_op jit(solution)/shard_map/pallas_call | solution.py:149
  69.1 2.7 %collective-permute-done.14.refs_0_ = bf16[4128,128]{1,0:T(8,128)(2,1)S(1)} collective-permute-done((bf16[4128,128]{1,0:T(8,128)(2,1)S(1)}, bf16[4128,128]{1,0:T(8,128)(2,1)S(1)}, u32[]{:S(2)}, u32[]{:S(2)}) %collective-permute-start.14) | collective-permute-done | bytes 1056800 | tf_op jit(solution)/shard_map/ppermute | solution.py:295
  71.9 2.5 %collective-permute-start.18 = (bf16[4128,128]{1,0:T(8,128)(2,1)S(1)}, bf16[4128,128]{1,0:T(8,128)(2,1)S(1)}, u32[]{:S(2)}, u32[]{:S(2)}) collective-permute-start(bf16[4128,128]{1,0:T(8,128)(2,1)S(1)} %collective-permute-done.14.refs_0_), channel_id=1, source_target_pairs={{0,8},{8,16},{16,24},{24,28},{28,20},{20,12},{12,4},{4,0},{2,6},{1... | collective-permute-start | bytes 3170312 | tf_op jit(solution)/shard_map/ppermute | solution.py:295
  74.3 6.1 %shard_map.68 = (f32[256,32768]{1,0:T(8,128)}, f32[128,256]{1,0:T(8,128)S(1)}, f32[8,128]{1,0:T(8,128)S(1)}) custom-call(s32[35]{0:T(128)S(1)} %pad_add_fusion.1.sc, f32[2,256,256]{2,1,0:T(8,128)S(1)} %convert_element_type.21.w, bf16[3,128,256]{2,1,0:T(8,128)(2,1)S(1)} %copy-done.1, ...), custom_call_target="tpu_custom_call", output_to_operand_aliasing={{1}: (4, {}), {0}: (8, {})} | custom-call | flops 1879048192 | bytes 6291456 | tf_op jit(solution)/shard_map/pallas_call | solution.py:149
  80.5 2.7 %collective-permute-done.16.refs_0_ = bf16[4128,128]{1,0:T(8,128)(2,1)S(1)} collective-permute-done((bf16[4128,128]{1,0:T(8,128)(2,1)S(1)}, bf16[4128,128]{1,0:T(8,128)(2,1)S(1)}, u32[]{:S(2)}, u32[]{:S(2)}) %collective-permute-start.16) | collective-permute-done | bytes 1056800 | tf_op jit(solution)/shard_map/ppermute | solution.py:295
  83.2 0.0 collective-permute-done.15.refs_1_
  83.2 6.1 %shard_map.69 = (f32[256,32768]{1,0:T(8,128)}, f32[128,256]{1,0:T(8,128)S(1)}, f32[8,128]{1,0:T(8,128)S(1)}) custom-call(s32[35]{0:T(128)S(1)} %pad_add_fusion.1.sc, f32[2,256,256]{2,1,0:T(8,128)S(1)} %convert_element_type.21.w, bf16[3,128,256]{2,1,0:T(8,128)(2,1)S(1)} %copy-done.1, ...), custom_call_target="tpu_custom_call", output_to_operand_aliasing={{1}: (4, {}), {0}: (8, {})} | custom-call | flops 1879048192 | bytes 6291456 | tf_op jit(solution)/shard_map/pallas_call | solution.py:149
  89.3 5.2 %collective-permute-done.18.refs_0_ = bf16[4128,128]{1,0:T(8,128)(2,1)S(1)} collective-permute-done((bf16[4128,128]{1,0:T(8,128)(2,1)S(1)}, bf16[4128,128]{1,0:T(8,128)(2,1)S(1)}, u32[]{:S(2)}, u32[]{:S(2)}) %collective-permute-start.18) | collective-permute-done | bytes 1056800 | tf_op jit(solution)/shard_map/ppermute | solution.py:295
  94.5 0.0 collective-permute-start.19
  94.5 2.5 %collective-permute-start.20 = (bf16[4128,128]{1,0:T(8,128)(2,1)S(1)}, bf16[4128,128]{1,0:T(8,128)(2,1)S(1)}, u32[]{:S(2)}, u32[]{:S(2)}) collective-permute-start(bf16[4128,128]{1,0:T(8,128)(2,1)S(1)} %collective-permute-done.16.refs_0_), channel_id=1, source_target_pairs={{0,8},{8,16},{16,24},{24,28},{28,20},{20,12},{12,4},{4,0},{2,6},{1... | collective-permute-start | bytes 3170312 | tf_op jit(solution)/shard_map/ppermute | solution.py:295
  97.0 6.7 %shard_map.70 = (f32[256,32768]{1,0:T(8,128)}, f32[128,256]{1,0:T(8,128)S(1)}, f32[8,128]{1,0:T(8,128)}) custom-call(s32[35]{0:T(128)S(1)} %pad_add_fusion.1.sc, f32[2,256,256]{2,1,0:T(8,128)S(1)} %convert_element_type.21.w, bf16[3,128,256]{2,1,0:T(8,128)(2,1)S(1)} %copy-done.1, ...), custom_call_target="tpu_custom_call", output_to_operand_aliasing={{1}: (4, {}), {0}: (8, {})} | custom-call | flops 1879048192 | bytes 6291456 | tf_op jit(solution)/shard_map/pallas_call | solution.py:149
  103.7 6.1 %shard_map.71 = (f32[256,32768]{1,0:T(8,128)}, f32[128,256]{1,0:T(8,128)S(1)}, f32[8,128]{1,0:T(8,128)S(1)}) custom-call(s32[35]{0:T(128)S(1)} %pad_add_fusion.1.sc, f32[2,256,256]{2,1,0:T(8,128)S(1)} %convert_element_type.21.w, bf16[3,128,256]{2,1,0:T(8,128)(2,1)S(1)} %copy-done.1, ...), custom_call_target="tpu_custom_call", output_to_operand_aliasing={{1}: (4, {}), {0}: (8, {})} | custom-call | flops 1879048192 | bytes 6291456 | tf_op jit(solution)/shard_map/pallas_call | solution.py:149
  109.9 0.1 collective-permute-start.21
  109.9 2.7 %collective-permute-done.21.refs_1_ = bf16[4128,128]{1,0:T(8,128)(2,1)S(1)} collective-permute-done((bf16[4128,128]{1,0:T(8,128)(2,1)S(1)}, bf16[4128,128]{1,0:T(8,128)(2,1)S(1)}, u32[]{:S(2)}, u32[]{:S(2)}) %collective-permute-start.21) | collective-permute-done | bytes 1056800 | tf_op jit(solution)/shard_map/ppermute | solution.py:295
  112.6 6.7 %shard_map.72 = (f32[256,32768]{1,0:T(8,128)}, f32[128,256]{1,0:T(8,128)S(1)}, f32[8,128]{1,0:T(8,128)}) custom-call(s32[35]{0:T(128)S(1)} %pad_add_fusion.1.sc, f32[2,256,256]{2,1,0:T(8,128)S(1)} %convert_element_type.21.w, bf16[3,128,256]{2,1,0:T(8,128)(2,1)S(1)} %copy-done.1, ...), custom_call_target="tpu_custom_call", output_to_operand_aliasing={{1}: (4, {}), {0}: (8, {})} | custom-call | flops 1879048192 | bytes 6291456 | tf_op jit(solution)/shard_map/pallas_call | solution.py:149
  119.3 0.1 collective-permute-start.22
  119.4 5.5 %collective-permute-done.22.other = f32[128,256]{1,0:T(8,128)S(1)} collective-permute-done((f32[128,256]{1,0:T(8,128)S(1)}, f32[128,256]{1,0:T(8,128)S(1)}, u32[]{:S(2)}, u32[]{:S(2)}) %collective-permute-start.22) | collective-permute-done | bytes 131104 | tf_op jit(solution)/shard_map/ppermute | solution.py:361
  124.9 0.6 copy-done.9
  125.6 2.5 %shard_map.73 = f32[256,32768]{1,0:T(8,128)} custom-call(s32[4]{0:T(128)} %reshape.44.sc, f32[128,256]{1,0:T(8,128)} %copy-done, f32[128,256]{1,0:T(8,128)} %copy-done.9, f32[2,128]{1,0:T(2,128)} %damp.1, f32[256,32768]{1,0:T(8,128)} %get-tuple-element.88.tile), custom_call_target="tpu_custom_call", output_to_operand_aliasing={{}: (4, {})} | custom-call | tf_op jit(solution)/shard_map/pallas_call | solution.py:190
  (39 shorter events, 0.2 us)
Async XLA Ops:
  0.0 2.9 %copy-start.5 = (bf16[16,256,128]{2,1,0:T(8,128)(2,1)S(1)}, bf16[16,256,128]{2,1,0:T(8,128)(2,1)}, u32[]{:S(2)}) copy-start(bf16[16,256,128]{2,1,0:T(8,128)(2,1)} %param.6) | copy-start | bytes 3145732
  2.4 21.9 %collective-permute-start.4 = (bf16[4128,128]{1,0:T(8,128)(2,1)}, bf16[4128,128]{1,0:T(8,128)(2,1)S(1)}, u32[]{:S(2)}, u32[]{:S(2)}) collective-permute-start(bf16[4128,128]{1,0:T(8,128)(2,1)} %pad_maximum_fusion.refs_0_), channel_id=1, source_target_pairs={{0,2},{2,0},{4,6},{6,4},{8,10},{10,8},{12,14},{14,12},{16,18},{18,... | collective-permute-start | bytes 3170312 | tf_op jit(solution)/shard_map/ppermute | solution.py:295
  3.7 12.3 %collective-permute-start.3 = (bf16[4,256,128]{2,1,0:T(8,128)(2,1)S(1)}, bf16[4,256,128]{2,1,0:T(8,128)(2,1)}, u32[]{:S(2)}, u32[]{:S(2)}) collective-permute-start(bf16[4,256,128]{2,1,0:T(8,128)(2,1)S(1)} %get-tuple-element.92), channel_id=1, source_target_pairs={{2,16}} | collective-permute-start | bytes 786440 | tf_op jit(solution)/shard_map/ppermute | solution.py:229
  5.1 12.3 %collective-permute-start.2 = (bf16[4,256,128]{2,1,0:T(8,128)(2,1)}, bf16[4,256,128]{2,1,0:T(8,128)(2,1)}, u32[]{:S(2)}, u32[]{:S(2)}) collective-permute-start(bf16[4,256,128]{2,1,0:T(8,128)(2,1)} %get-tuple-element.91), channel_id=1, source_target_pairs={{2,28},{0,12},{31,7}} | collective-permute-start | bytes 786440 | tf_op jit(solution)/shard_map/ppermute | solution.py:229
  11.2 11.8 %collective-permute-start.1 = (bf16[4,256,128]{2,1,0:T(8,128)(2,1)}, bf16[4,256,128]{2,1,0:T(8,128)(2,1)}, u32[]{:S(2)}, u32[]{:S(2)}) collective-permute-start(bf16[4,256,128]{2,1,0:T(8,128)(2,1)} %get-tuple-element.90), channel_id=1, source_target_pairs={{2,24},{0,8},{31,15}} | collective-permute-start | bytes 786440 | tf_op jit(solution)/shard_map/ppermute | solution.py:229
  13.2 9.8 %collective-permute-start = (bf16[4,256,128]{2,1,0:T(8,128)(2,1)S(1)}, bf16[4,256,128]{2,1,0:T(8,128)(2,1)}, u32[]{:S(2)}, u32[]{:S(2)}) collective-permute-start(bf16[4,256,128]{2,1,0:T(8,128)(2,1)S(1)} %get-tuple-element.89), channel_id=1, source_target_pairs={{2,20},{0,4},{31,23}} | collective-permute-start | bytes 786440 | tf_op jit(solution)/shard_map/ppermute | solution.py:229
  16.0 26.6 %collective-permute-start.8 = (bf16[4128,128]{1,0:T(8,128)(2,1)}, bf16[4128,128]{1,0:T(8,128)(2,1)S(1)}, u32[]{:S(2)}, u32[]{:S(2)}) collective-permute-start(bf16[4128,128]{1,0:T(8,128)(2,1)} %pad_maximum_fusion.refs_0_), channel_id=1, source_target_pairs={{0,8},{8,16},{16,24},{24,28},{28,20},{20,12},{12,4},{4,0},{2,6},{1... | collective-permute-start | bytes 3170312 | tf_op jit(solution)/shard_map/ppermute | solution.py:295
  24.3 8.1 %copy-start.3 = (bf16[4128,128]{1,0:T(8,128)(2,1)}, bf16[4128,128]{1,0:T(8,128)(2,1)S(1)}, u32[]{:S(2)}) copy-start(bf16[4128,128]{1,0:T(8,128)(2,1)S(1)} %collective-permute-done.4.refs_1_) | copy-start | bytes 3170308
  24.4 8.3 %collective-permute-start.5 = (bf16[2,256,128]{2,1,0:T(8,128)(2,1)S(1)}, bf16[2,256,128]{2,1,0:T(8,128)(2,1)S(1)}, u32[]{:S(2)}, u32[]{:S(2)}) collective-permute-start(bf16[2,256,128]{2,1,0:T(8,128)(2,1)S(1)} %slice_select_fusion), channel_id=1, source_target_pairs={{0,2},{2,0},{4,6},{6,4},{8,10},{10,8},{12,14},{14,12},{16,18},{18,... | collective-permute-start | bytes 393224 | tf_op jit(solution)/shard_map/ppermute | solution.py:232
  32.4 7.5 %copy-start.11 = (bf16[16,128]{1,0:T(8,128)(2,1)}, bf16[16,128]{1,0:T(8,128)(2,1)S(1)}, u32[]{:S(2)}) copy-start(bf16[16,128]{1,0:T(8,128)(2,1)S(1)} %pad.9.w_a) | copy-start | bytes 12292
  32.4 20.4 %collective-permute-start.10 = (bf16[4128,128]{1,0:T(8,128)(2,1)}, bf16[4128,128]{1,0:T(8,128)(2,1)S(1)}, u32[]{:S(2)}, u32[]{:S(2)}) collective-permute-start(bf16[4128,128]{1,0:T(8,128)(2,1)} %copy-done.3), channel_id=1, source_target_pairs={{0,8},{8,16},{16,24},{24,28},{28,20},{20,12},{12,4},{4,0},{2,6},{1... | collective-permute-start | bytes 3170312 | tf_op jit(solution)/shard_map/ppermute | solution.py:295
  32.7 7.2 %copy-start.6 = (bf16[2,256,128]{2,1,0:T(8,128)(2,1)}, bf16[2,256,128]{2,1,0:T(8,128)(2,1)S(1)}, u32[]{:S(2)}) copy-start(bf16[2,256,128]{2,1,0:T(8,128)(2,1)S(1)} %maximum_select_fusion.slab_b) | copy-start | bytes 393220
  32.7 5.8 %collective-permute-start.6 = (bf16[2,256,128]{2,1,0:T(8,128)(2,1)S(1)}, bf16[2,256,128]{2,1,0:T(8,128)(2,1)S(1)}, u32[]{:S(2)}, u32[]{:S(2)}) collective-permute-start(bf16[2,256,128]{2,1,0:T(8,128)(2,1)S(1)} %maximum_select_fusion.slab_b), channel_id=1, source_target_pairs={{0,1},{1,0},{2,3},{3,2},{4,5},{5,4},{6,7},{7,6},{8,9},{9,8},{10,11... | collective-permute-start | bytes 393224 | tf_op jit(solution)/shard_map/ppermute | solution.py:237
  38.5 1.4 %copy-start.7 = (bf16[2,256,128]{2,1,0:T(8,128)(2,1)}, bf16[2,256,128]{2,1,0:T(8,128)(2,1)S(1)}, u32[]{:S(2)}) copy-start(bf16[2,256,128]{2,1,0:T(8,128)(2,1)S(1)} %collective-permute-done.6.slab_a) | copy-start | bytes 393220
  38.5 1.3 %copy-start.8 = (bf16[256,128]{1,0:T(8,128)(2,1)}, bf16[256,128]{1,0:T(8,128)(2,1)S(1)}, u32[]{:S(2)}) copy-start(bf16[256,128]{1,0:T(8,128)(2,1)S(1)} %fusion.5.panel_a) | copy-start | bytes 196612
  38.6 1.3 %collective-permute-start.7 = (bf16[256,128]{1,0:T(8,128)(2,1)S(1)}, bf16[256,128]{1,0:T(8,128)(2,1)S(1)}, u32[]{:S(2)}, u32[]{:S(2)}) collective-permute-start(bf16[256,128]{1,0:T(8,128)(2,1)S(1)} %fusion.5.panel_a), channel_id=1, source_target_pairs={{0,2},{2,0},{4,6},{6,4},{8,10},{10,8},{12,14},{14,12},{16,18},{18,... | collective-permute-start | bytes 196616 | tf_op jit(solution)/shard_map/ppermute | solution.py:239
  39.9 0.6 copy-start.10
  42.7 12.4 %collective-permute-start.9 = (bf16[4128,128]{1,0:T(8,128)(2,1)S(1)}, bf16[4128,128]{1,0:T(8,128)(2,1)S(1)}, u32[]{:S(2)}, u32[]{:S(2)}) collective-permute-start(bf16[4128,128]{1,0:T(8,128)(2,1)S(1)} %collective-permute-done.8.refs_0_), channel_id=1, source_target_pairs={{0,2},{2,0},{4,6},{6,4},{8,10},{10,8},{12,14},{14,12},{16,18},{18,... | collective-permute-start | bytes 3170312 | tf_op jit(solution)/shard_map/ppermute | solution.py:295
  42.8 18.4 %collective-permute-start.12 = (bf16[4128,128]{1,0:T(8,128)(2,1)S(1)}, bf16[4128,128]{1,0:T(8,128)(2,1)S(1)}, u32[]{:S(2)}, u32[]{:S(2)}) collective-permute-start(bf16[4128,128]{1,0:T(8,128)(2,1)S(1)} %collective-permute-done.8.refs_0_), channel_id=1, source_target_pairs={{0,8},{8,16},{16,24},{24,28},{28,20},{20,12},{12,4},{4,0},{2,6},{1... | collective-permute-start | bytes 3170312 | tf_op jit(solution)/shard_map/ppermute | solution.py:295
  42.8 0.9 copy-start.1
  43.8 0.9 copy-start.2
  44.7 1.2 copy-start.4
  52.9 10.1 %collective-permute-start.11 = (bf16[4128,128]{1,0:T(8,128)(2,1)S(1)}, bf16[4128,128]{1,0:T(8,128)(2,1)S(1)}, u32[]{:S(2)}, u32[]{:S(2)}) collective-permute-start(bf16[4128,128]{1,0:T(8,128)(2,1)S(1)} %collective-permute-done.10.refs_0_), channel_id=1, source_target_pairs={{0,2},{2,0},{4,6},{6,4},{8,10},{10,8},{12,14},{14,12},{16,18},{18,... | collective-permute-start | bytes 3170312 | tf_op jit(solution)/shard_map/ppermute | solution.py:295
  54.1 17.8 %collective-permute-start.14 = (bf16[4128,128]{1,0:T(8,128)(2,1)S(1)}, bf16[4128,128]{1,0:T(8,128)(2,1)S(1)}, u32[]{:S(2)}, u32[]{:S(2)}) collective-permute-start(bf16[4128,128]{1,0:T(8,128)(2,1)S(1)} %collective-permute-done.10.refs_0_), channel_id=1, source_target_pairs={{0,8},{8,16},{16,24},{24,28},{28,20},{20,12},{12,4},{4,0},{2,6},{1... | collective-permute-start | bytes 3170312 | tf_op jit(solution)/shard_map/ppermute | solution.py:295
  61.2 13.2 %collective-permute-start.13 = (bf16[4128,128]{1,0:T(8,128)(2,1)S(1)}, bf16[4128,128]{1,0:T(8,128)(2,1)S(1)}, u32[]{:S(2)}, u32[]{:S(2)}) collective-permute-start(bf16[4128,128]{1,0:T(8,128)(2,1)S(1)} %collective-permute-done.12.refs_0_), channel_id=1, source_target_pairs={{0,2},{2,0},{4,6},{6,4},{8,10},{10,8},{12,14},{14,12},{16,18},{18,... | collective-permute-start | bytes 3170312 | tf_op jit(solution)/shard_map/ppermute | solution.py:295
  62.5 20.7 %collective-permute-start.16 = (bf16[4128,128]{1,0:T(8,128)(2,1)S(1)}, bf16[4128,128]{1,0:T(8,128)(2,1)S(1)}, u32[]{:S(2)}, u32[]{:S(2)}) collective-permute-start(bf16[4128,128]{1,0:T(8,128)(2,1)S(1)} %collective-permute-done.12.refs_0_), channel_id=1, source_target_pairs={{0,8},{8,16},{16,24},{24,28},{28,20},{20,12},{12,4},{4,0},{2,6},{1... | collective-permute-start | bytes 3170312 | tf_op jit(solution)/shard_map/ppermute | solution.py:295
  71.9 11.3 %collective-permute-start.15 = (bf16[4128,128]{1,0:T(8,128)(2,1)S(1)}, bf16[4128,128]{1,0:T(8,128)(2,1)S(1)}, u32[]{:S(2)}, u32[]{:S(2)}) collective-permute-start(bf16[4128,128]{1,0:T(8,128)(2,1)S(1)} %collective-permute-done.14.refs_0_), channel_id=1, source_target_pairs={{0,2},{2,0},{4,6},{6,4},{8,10},{10,8},{12,14},{14,12},{16,18},{18,... | collective-permute-start | bytes 3170312 | tf_op jit(solution)/shard_map/ppermute | solution.py:295
  71.9 22.6 %collective-permute-start.18 = (bf16[4128,128]{1,0:T(8,128)(2,1)S(1)}, bf16[4128,128]{1,0:T(8,128)(2,1)S(1)}, u32[]{:S(2)}, u32[]{:S(2)}) collective-permute-start(bf16[4128,128]{1,0:T(8,128)(2,1)S(1)} %collective-permute-done.14.refs_0_), channel_id=1, source_target_pairs={{0,8},{8,16},{16,24},{24,28},{28,20},{20,12},{12,4},{4,0},{2,6},{1... | collective-permute-start | bytes 3170312 | tf_op jit(solution)/shard_map/ppermute | solution.py:295
  83.2 13.8 %collective-permute-start.17 = (bf16[4128,128]{1,0:T(8,128)(2,1)S(1)}, bf16[4128,128]{1,0:T(8,128)(2,1)S(1)}, u32[]{:S(2)}, u32[]{:S(2)}) collective-permute-start(bf16[4128,128]{1,0:T(8,128)(2,1)S(1)} %collective-permute-done.16.refs_0_), channel_id=1, source_target_pairs={{0,2},{2,0},{4,6},{6,4},{8,10},{10,8},{12,14},{14,12},{16,18},{18,... | collective-permute-start | bytes 3170312 | tf_op jit(solution)/shard_map/ppermute | solution.py:295
  94.5 9.2 %collective-permute-start.19 = (bf16[4128,128]{1,0:T(8,128)(2,1)S(1)}, bf16[4128,128]{1,0:T(8,128)(2,1)S(1)}, u32[]{:S(2)}, u32[]{:S(2)}) collective-permute-start(bf16[4128,128]{1,0:T(8,128)(2,1)S(1)} %collective-permute-done.18.refs_0_), channel_id=1, source_target_pairs={{0,2},{2,0},{4,6},{6,4},{8,10},{10,8},{12,14},{14,12},{16,18},{18,... | collective-permute-start | bytes 3170312 | tf_op jit(solution)/shard_map/ppermute | solution.py:295
  94.5 15.3 %collective-permute-start.20 = (bf16[4128,128]{1,0:T(8,128)(2,1)S(1)}, bf16[4128,128]{1,0:T(8,128)(2,1)S(1)}, u32[]{:S(2)}, u32[]{:S(2)}) collective-permute-start(bf16[4128,128]{1,0:T(8,128)(2,1)S(1)} %collective-permute-done.16.refs_0_), channel_id=1, source_target_pairs={{0,8},{8,16},{16,24},{24,28},{28,20},{20,12},{12,4},{4,0},{2,6},{1... | collective-permute-start | bytes 3170312 | tf_op jit(solution)/shard_map/ppermute | solution.py:295
  109.9 2.7 %collective-permute-start.21 = (bf16[4128,128]{1,0:T(8,128)(2,1)S(1)}, bf16[4128,128]{1,0:T(8,128)(2,1)S(1)}, u32[]{:S(2)}, u32[]{:S(2)}) collective-permute-start(bf16[4128,128]{1,0:T(8,128)(2,1)S(1)} %collective-permute-done.20.refs_0_), channel_id=1, source_target_pairs={{0,2},{2,0},{4,6},{6,4},{8,10},{10,8},{12,14},{14,12},{16,18},{18,... | collective-permute-start | bytes 3170312 | tf_op jit(solution)/shard_map/ppermute | solution.py:295
  119.3 5.6 %copy-start = (f32[128,256]{1,0:T(8,128)}, f32[128,256]{1,0:T(8,128)S(1)}, u32[]{:S(2)}) copy-start(f32[128,256]{1,0:T(8,128)S(1)} %get-tuple-element.87.gram) | copy-start | bytes 393220
  119.3 5.6 %collective-permute-start.22 = (f32[128,256]{1,0:T(8,128)S(1)}, f32[128,256]{1,0:T(8,128)S(1)}, u32[]{:S(2)}, u32[]{:S(2)}) collective-permute-start(f32[128,256]{1,0:T(8,128)S(1)} %get-tuple-element.87.gram), channel_id=1, source_target_pairs={{0,1},{1,0},{2,3},{3,2},{4,5},{5,4},{6,7},{7,6},{8,9},{9,8},{10,11... | collective-permute-start | bytes 393224 | tf_op jit(solution)/shard_map/ppermute | solution.py:361
  124.9 0.6 copy-start.9

commit v2 on v1

--- a/solution.py
+++ b/solution.py
@@ -47,32 +47,45 @@
             jax.ShapeDtypeStruct((slabs + 1, width, rows), BF16),
             jax.ShapeDtypeStruct((slabs * width, width), F32),
         ],
+        compiler_params=pltpu.CompilerParams(vmem_limit_bytes=8 << 20),
     )(pick, slab_a, slab_b, panel_a, panel_b, w_a, w_b, inverse)
 
 
-def block_kernel(slot, half, count, skip, sc, w, turned, fac, gin, *refs):
-    units = refs[: count // 2]
-    out, gout, token, jbuf, pbuf, obuf, in_sem, out_sem = refs[count // 2 + skip :]
-    slabs = w.shape[0]
-    _, width, rows = turned.shape
+def block_kernel(slot, half, shape, do_gram, do_rest, count, skip, sc, w, *refs):
+    slabs, width, rows = shape
+    refs = list(refs)
+    if do_rest:
+        turned, fac = refs.pop(0), refs.pop(0)
+    if do_gram:
+        gin = refs.pop(0)
+    units, refs = refs[: count // 2], refs[count // 2 + skip :]
+    if do_rest:
+        out = refs.pop(0)
+    if do_gram:
+        gout = refs.pop(0)
+    token, jbuf, in_sem = refs[:3]
+    if do_rest:
+        pbuf, obuf, tail_sem, out_sem = refs[3:]
     extra = sc.shape[0] - slabs - 1
-    size, tail = half * rows, pbuf.shape[1]
+    size = half * rows
 
     def fetch(b):
         unit, h = units[b // 2], b % 2
-        return (
-            pltpu.make_async_copy(unit.at[pl.ds(h * size, size)], jbuf.at[b], in_sem.at[0, b]),
-            pltpu.make_async_copy(
-                unit.at[pl.ds(2 * size + h * tail, tail)], pbuf.at[b], in_sem.at[1, b]
-            ),
-        )
+        copies = [pltpu.make_async_copy(unit.at[pl.ds(h * size, size)], jbuf.at[b], in_sem.at[b])]
+        if do_rest:
+            tail = pbuf.shape[1]
+            at = pl.ds(2 * size + h * tail, tail)
+            copies.append(pltpu.make_async_copy(unit.at[at], pbuf.at[b], tail_sem.at[b]))
+        return copies
 
     for b in range(count):
         for copy in fetch(b):
             copy.start()
     token[...] = jnp.zeros_like(token)
-    gout[...] = gin[...]
-    fac_b = fac[...].astype(BF16)
+    if do_gram:
+        gout[...] = gin[...]
+    if do_rest:
+        fac_b = fac[...].astype(BF16)
 
     def write(b):
         col = pl.multiple_of(sc[slot + b] * width, half * width)
@@ -81,15 +94,17 @@
         )
 
     def one(b, carry):
-        pltpu.make_async_copy(units[0].at[pl.ds(0, size)], jbuf.at[b], in_sem.at[0, b]).wait()
-        pltpu.make_async_copy(units[0].at[pl.ds(0, tail)], pbuf.at[b], in_sem.at[1, b]).wait()
-
-        @pl.when(b >= 2)
-        def _():
-            write(b - 2).wait()
-
+        pltpu.make_async_copy(units[0].at[pl.ds(0, size)], jbuf.at[b], in_sem.at[b]).wait()
+        if do_rest:
+            tail = pbuf.shape[1]
+            pltpu.make_async_copy(units[0].at[pl.ds(0, tail)], pbuf.at[b], tail_sem.at[b]).wait()
+
+            @pl.when(b >= 2)
+            def _():
+                write(b - 2).wait()
+
+            pw = pbuf[b].astype(F32)
         first = sc[slot + b]
-        pw = pbuf[b].astype(F32)
         acc = None
         parts, panels = [], []
         for k in range(half):
@@ -99,77 +114,104 @@
                 jnp.where(j == sc[extra + 1 + i], 0.0, w[i, pl.ds(j, 1), :]).astype(BF16)
                 for i in range(slabs)
             ]
-            row_p = jnp.concatenate([pw[k : k + 1], pw[half + k : half + k + 1]], 1).astype(BF16)
-            parts.append(
-                dot_nt(jac_t, jnp.concatenate([turned[i] * ws[i] for i in range(slabs)], 0))
-            )
-            panels.append(dot_nt(jac_t, turned[slabs] * row_p).astype(BF16))
-            part = dot_nt(jac_t, jnp.concatenate([jac_t * ws[i] for i in range(slabs)], 0))
-            acc = part if acc is None else acc + part
-        corr = jnp.dot(fac_b, jnp.concatenate(panels, 1), preferred_element_type=F32)
-        o = obuf.at[b % 2]
-        for k in range(half):
-            for i in range(slabs):
-                here = (slice(i * width, (i + 1) * width), slice(k * width, (k + 1) * width))
-                o[here] = parts[k][:, i * width : (i + 1) * width] - corr[here]
-        gout[...] += acc
-        where_p = sc[extra] - first
-
-        @pl.when((where_p >= 0) & (where_p < half))
-        def _():
+            if do_rest:
+                row_p = jnp.concatenate([pw[k : k + 1], pw[half + k : half + k + 1]], 1)
+                row_p = row_p.astype(BF16)
+                parts.append(
+                    dot_nt(jac_t, jnp.concatenate([turned[i] * ws[i] for i in range(slabs)], 0))
+                )
+                panels.append(dot_nt(jac_t, turned[slabs] * row_p).astype(BF16))
+            if do_gram:
+                part = dot_nt(jac_t, jnp.concatenate([jac_t * ws[i] for i in range(slabs)], 0))
+                acc = part if acc is None else acc + part
+        if do_gram:
+            gout[...] += acc
+        if do_rest:
+            corr = jnp.dot(fac_b, jnp.concatenate(panels, 1), preferred_element_type=F32)
+            o = obuf.at[b % 2]
             for k in range(half):
-
-                @pl.when(where_p == k)
-                def _():
-                    o[:, k * width : (k + 1) * width] = fac[...]
-
-        write(b).start()
+                for i in range(slabs):
+                    here = (slice(i * width, (i + 1) * width), slice(k * width, (k + 1) * width))
+                    o[here] = parts[k][:, i * width : (i + 1) * width] - corr[here]
+            where_p = sc[extra] - first
+
+            @pl.when((where_p >= 0) & (where_p < half))
+            def _():
+                for k in range(half):
+
+                    @pl.when(where_p == k)
+                    def _():
+                        o[:, k * width : (k + 1) * width] = fac[...]
+
+            write(b).start()
         return carry
 
     lax.fori_loop(0, count, one, 0)
-    for b in range(max(count - 2, 0), count):
-        write(b).wait()
+    if do_rest:
+        for b in range(max(count - 2, 0), count):
+            write(b).wait()
 
 
 def block_call(slot, half, sc, units, w, turned, fac, gram, after, out, shape):
-    slabs = w.shape[0]
-    _, width, rows = turned.shape
+    do_rest, do_gram = turned is not None, gram is not None
+    slabs, _, rows = w.shape
+    width = units[0].shape[1]
     count = 2 * len(units)
-    args = [w, turned, fac, gram] + list(units) + list(after)
-    specs = [pl.BlockSpec(memory_space=pltpu.VMEM)] * 4
-    specs += [pl.BlockSpec(memory_space=pltpu.HBM)] * len(units)
-    specs += [pl.BlockSpec(memory_space=pl.ANY)] * len(after)
-    aliases = {4: 1}
-    if out is not None:
+    vmem, anywhere = pl.BlockSpec(memory_space=pltpu.VMEM), pl.BlockSpec(memory_space=pl.ANY)
+    args, outs, specs, aliases = [w], [], [], {}
+    if do_rest:
+        args += [turned, fac]
+        outs.append(jax.ShapeDtypeStruct(shape, F32))
+        specs.append(anywhere)
+    if do_gram:
+        aliases[1 + len(args)] = len(outs)
+        args.append(gram)
+        outs.append(jax.ShapeDtypeStruct(gram.shape, F32))
+        specs.append(vmem)
+    outs.append(jax.ShapeDtypeStruct((8, 128), F32))
+    specs.append(vmem)
+    in_specs = [pl.BlockSpec(memory_space=pltpu.SMEM)] + [vmem] * len(args)
+    args += list(units) + list(after)
+    in_specs += [pl.BlockSpec(memory_space=pltpu.HBM)] * len(units) + [anywhere] * len(after)
+    skip = len(after)
+    if do_rest and out is not None:
         aliases[1 + len(args)] = 0
         args.append(out)
-        specs.append(pl.BlockSpec(memory_space=pl.ANY))
+        in_specs.append(anywhere)
+        skip += 1
     stations = half * count
     tail = units[0].shape[0] // 2 - half * rows
-    return pl.pallas_call(
-        functools.partial(block_kernel, slot, half, count, len(after) + (out is not None)),
-        in_specs=[pl.BlockSpec(memory_space=pltpu.SMEM)] + specs,
-        out_specs=[pl.BlockSpec(memory_space=pl.ANY)] + [pl.BlockSpec(memory_space=pltpu.VMEM)] * 2,
-        out_shape=[
-            jax.ShapeDtypeStruct(shape, F32),
-            jax.ShapeDtypeStruct(gram.shape, F32),
-            jax.ShapeDtypeStruct((8, 128), F32),
-        ],
-        scratch_shapes=[
-            pltpu.VMEM((count, half * rows, width), BF16),
+    scratch = [
+        pltpu.VMEM((count, half * rows, width), BF16),
+        pltpu.SemaphoreType.DMA((count,)),
+    ]
+    if do_rest:
+        scratch += [
             pltpu.VMEM((count, tail, width), BF16),
             pltpu.VMEM((2, slabs * width, half * width), F32),
-            pltpu.SemaphoreType.DMA((2, count)),
+            pltpu.SemaphoreType.DMA((count,)),
             pltpu.SemaphoreType.DMA((2,)),
-        ],
+        ]
+    results = pl.pallas_call(
+        functools.partial(
+            block_kernel, slot, half, (slabs, width, rows), do_gram, do_rest, count, skip
+        ),
+        in_specs=in_specs,
+        out_specs=specs,
+        out_shape=outs,
+        scratch_shapes=scratch,
         input_output_aliases=aliases,
         compiler_params=pltpu.CompilerParams(vmem_limit_bytes=24 << 20),
         cost_estimate=pl.CostEstimate(
-            flops=stations * 14 * width * width * rows,
-            bytes_accessed=stations * (slabs * width * width * 4 + rows * width * 2),
+            flops=stations * (4 * do_gram + 10 * do_rest) * width * width * rows // 8,
+            bytes_accessed=stations * (do_rest * slabs * width * width * 4 + rows * width * 2) // 8,
             transcendentals=0,
         ),
     )(sc, *args)
+    results = list(results)
+    out = results.pop(0) if do_rest else out
+    gram = results.pop(0) if do_gram else gram
+    return out, gram, results[0]
 
 
 def patch_kernel(sc, gram, other, damp, tile, out):
@@ -197,6 +239,7 @@
         ),
         out_shape=jax.ShapeDtypeStruct(out.shape, F32),
         input_output_aliases={4: 0},
+        compiler_params=pltpu.CompilerParams(vmem_limit_bytes=8 << 20),
     )(sc, gram, other, damping, out)
 
 
@@ -298,15 +341,7 @@
     tail = tail.reshape(2, per_dev, width)
     tail = jnp.pad(tail, ((0, 0), (0, -per_dev % 16), (0, 0))).reshape(-1, width)
     own = jnp.concatenate([jacobian.reshape(per_dev * samples, width), tail], 0)
-    other_core = over(own, swap)
-    if (rows, cols, per_dev) == (16, 2, 8 * slabs):
-        small, other_core = spread_direct(jacobian, weights, row, col, other_core)
-    else:
-        small = spread_general(jacobian, weights, row, col, rows, cols)
-    hops = [over(own, ring), over(other_core, ring)]
-    turned, factor = prep_call(*small, panel_inverse)
     w32 = weights.astype(F32)
-
     far = chips // 2
     order = [None] + [(d, s) for d in range(1, far) for s in (0, 1)] + [(far, 0)]
     table = np.zeros((rows, len(order), 2, 2), np.int32)
@@ -333,30 +368,51 @@
     sc = jnp.concatenate([starts, (panel_id - base)[None].astype(jnp.int32), ids])
     sc, spots = lax.optimization_barrier((sc, spots))
 
-    tokens, after = [], []
+    after, hops = [], [over(own, ring)]
     gram = jnp.zeros((width, slabs * width), F32)
     shape = (slabs * width, col_block * width)
     out = None
 
-    def compute(units):
+    def compute(slot, units, do_gram=True, do_rest=True):
         nonlocal out, gram
-        out, gram, token = block_call(
-            4 * len(tokens), half, sc, units, w32, turned, factor, gram, tuple(after), out, shape
+        out, g, token = block_call(
+            slot, half, sc, units, w32, turned if do_rest else None, factor if do_rest else None,
+            gram if do_gram else None, tuple(after), out, shape,
         )
+        gram = g if do_gram else gram
         after.clear()
-        tokens.append(token)
-
-    for q in range(len(order) - 1):
-        x = hops[q]
-        if q == 0:
-            x, factor = lax.optimization_barrier((x, factor))
-            compute([own, other_core])
+        return token
+
+    def hold(x, ready):
+        x, ready = lax.optimization_barrier((x, ready))
+        after.append(ready)
+        return x
+
+    other_core = late = over(own, swap)
+    if (rows, cols, per_dev) == (16, 2, 8 * slabs):
+        small, late = spread_direct(jacobian, weights, row, col, other_core)
+    else:
+        small = spread_general(jacobian, weights, row, col, rows, cols)
+    turned, factor = prep_call(*small, panel_inverse)
+    hops[0], factor = lax.optimization_barrier((hops[0], factor))
+    hops += [over(late, ring), over(hops[0], ring)]
+    last = len(order) - 2
+    pending = [hops[0], over(hops[0], swap)]
+    token = compute(0, [own, other_core])
+    for q in range(1, last + 1):
+        if q < last:
+            x = hold(hops[q], token)
+            if q + 2 <= last:
+                hops.append(over(x, ring))
+            units = [x, over(x, swap)]
+            token = compute(4 * q, pending)
+            pending = units
         else:
-            x, ready = lax.optimization_barrier((x, tokens[q - 1 if q < len(order) - 2 else q]))
-            after.append(ready)
-        if q + 2 < len(order) - 1:
-            hops.append(over(x, ring))
-        compute([x, over(x, swap)])
+            token = compute(4 * q, pending)
+            x = hold(hops[q], token)
+            units = [x, over(x, swap)]
+    after.append(compute(4 * last + 4, units, do_rest=False))
+    compute(4 * last + 4, units, do_gram=False)
     if cols == 2:
         other = lax.ppermute(gram, "col", [(0, 1), (1, 0)])
     else:

time: 129 us -> 123 us (0.953)
  local copies, waits for them, and re-layouts: 7.02 us -> 1.55 us
  other arithmetic: 6.33 us -> 4.83 us
    ppermute x1, waiting for transfers between devices: 5.52 us -> 0.01 us  [shards(): other = lax.ppermute(gram, 'col', [(0, 1), (1, 0)])]
    unnamed x24 -> x6, local copies, waits for them, and re-layouts: 4.34 us -> 0.02 us
    ppermute x15, waiting for transfers between devices: 13.3 us -> 17.4 us  [over(): return lax.ppermute(value, 'row', perm)]
    pallas_call x8 -> x9, Pallas kernels: 51 us -> 52.8 us  [block_call(): pl.pallas_call(functools.partial(block_kernel, slot, half, (slabs, width,...]
  transfers between devices with their start and end apart: 23 -> 23, of which waited for: 10 -> 11; matrix products, arithmetic and copies ran while one was open for 5% -> 4% of each run, Pallas kernels for 36% -> 41%
where the time goes in v2:
time: 123 us
  Pallas kernels  56 us (46%)
  waiting for transfers between devices  30.2 us (25%)
  starting transfers between devices  29.8 us (24%)
  other arithmetic  4.83 us (4%)
  local copies, waits for them, and re-layouts  1.55 us (1%)
    pallas_call x9, Pallas kernels, block_call(): pl.pallas_call(functools.partial(block_kernel, slot, half, (slabs, width,...  52.8 us
    ppermute x15, waiting for transfers between devices, over(): return lax.ppermute(value, 'row', perm)  17.4 us
    ppermute x4, starting transfers between devices, spread_direct(): total = total + lax.ppermute(pay, both, pairs)  11.6 us
    ppermute x15, starting transfers between devices, over(): return lax.ppermute(value, 'row', perm)  10.8 us
    ppermute x1, starting transfers between devices, spread_direct(): lax.ppermute(jnp.where(is_panel, total[:slabs], total[slabs:]), both, hop)  7.28 us
    ppermute x4, waiting for transfers between devices, spread_direct(): total = total + lax.ppermute(pay, both, pairs)  6.94 us
    ppermute x1, waiting for transfers between devices, spread_direct(): second = lax.ppermute(send, 'col', [(0, 1), (1, 0)])  4.52 us
  transfers between devices with their start and end apart: 23, of which 11 were waited for; matrix products, arithmetic and copies ran while one was open for 4% of the time, Pallas kernels for 41%

profile of v2, /device:TPU:0, one launch (start us, length us, event | category | flops | bytes accessed | tf_op | source)
XLA Modules:
  0.0 122.8 jit_solution(10718151009563335621)
XLA Ops:
  0.0 1.4 %pad_maximum_fusion.refs_3_ = bf16[4128,128]{1,0:T(8,128)(2,1)S(1)} fusion(bf16[32,128]{1,0:T(8,128)(2,1)} %bitcast.18, bf16[4096,128]{1,0:T(8,128)(2,1)} %bitcast.17), kind=kLoop, calls=%fused_computation | loop fusion | flops 2113536 | bytes 2113536 | tf_op jit(solution)/shard_map/concatenate | solution.py:343
  1.4 0.5 collective-permute-start.4
  1.9 0.9 pad_select_fusion.3
  2.8 1.4 %collective-permute-start.3 = (bf16[4,256,128]{2,1,0:T(8,128)(2,1)S(1)}, bf16[4,256,128]{2,1,0:T(8,128)(2,1)}, u32[]{:S(2)}, u32[]{:S(2)}) collective-permute-start(bf16[4,256,128]{2,1,0:T(8,128)(2,1)S(1)} %get-tuple-element.94), channel_id=1, source_target_pairs={{2,16}} | collective-permute-start | bytes 786440 | tf_op jit(solution)/shard_map/ppermute | solution.py:272
  4.2 6.2 %collective-permute-start.2 = (bf16[4,256,128]{2,1,0:T(8,128)(2,1)}, bf16[4,256,128]{2,1,0:T(8,128)(2,1)}, u32[]{:S(2)}, u32[]{:S(2)}) collective-permute-start(bf16[4,256,128]{2,1,0:T(8,128)(2,1)} %get-tuple-element.93), channel_id=1, source_target_pairs={{2,28},{0,12},{31,7}} | collective-permute-start | bytes 786440 | tf_op jit(solution)/shard_map/ppermute | solution.py:272
  10.4 2.0 %collective-permute-start.1 = (bf16[4,256,128]{2,1,0:T(8,128)(2,1)}, bf16[4,256,128]{2,1,0:T(8,128)(2,1)}, u32[]{:S(2)}, u32[]{:S(2)}) collective-permute-start(bf16[4,256,128]{2,1,0:T(8,128)(2,1)} %get-tuple-element.92), channel_id=1, source_target_pairs={{2,24},{0,8},{31,15}} | collective-permute-start | bytes 786440 | tf_op jit(solution)/shard_map/ppermute | solution.py:272
  12.4 2.0 %collective-permute-start = (bf16[4,256,128]{2,1,0:T(8,128)(2,1)S(1)}, bf16[4,256,128]{2,1,0:T(8,128)(2,1)}, u32[]{:S(2)}, u32[]{:S(2)}) collective-permute-start(bf16[4,256,128]{2,1,0:T(8,128)(2,1)S(1)} %get-tuple-element.91), channel_id=1, source_target_pairs={{2,20},{0,4},{31,23}} | collective-permute-start | bytes 786440 | tf_op jit(solution)/shard_map/ppermute | solution.py:272
  14.4 0.1 pad_add_fusion
  14.5 0.7 slice_reduce_fusion
  15.2 0.0 collective-permute-done.3
  15.2 0.1 collective-permute-start.8
  15.3 1.3 %collective-permute-done.2 = bf16[4,256,128]{2,1,0:T(8,128)(2,1)} collective-permute-done((bf16[4,256,128]{2,1,0:T(8,128)(2,1)}, bf16[4,256,128]{2,1,0:T(8,128)(2,1)}, u32[]{:S(2)}, u32[]{:S(2)}) %collective-permute-start.2) | collective-permute-done | bytes 262176 | tf_op jit(solution)/shard_map/ppermute | solution.py:272
  16.6 5.6 %collective-permute-done.1 = bf16[4,256,128]{2,1,0:T(8,128)(2,1)} collective-permute-done((bf16[4,256,128]{2,1,0:T(8,128)(2,1)}, bf16[4,256,128]{2,1,0:T(8,128)(2,1)}, u32[]{:S(2)}, u32[]{:S(2)}) %collective-permute-start.1) | collective-permute-done | bytes 262176 | tf_op jit(solution)/shard_map/ppermute | solution.py:272
  22.2 0.0 collective-permute-done
  22.2 1.3 %fusion.4 = bf16[4,256,128]{2,1,0:T(8,128)(2,1)S(1)} fusion(bf16[4,256,128]{2,1,0:T(8,128)(2,1)} %collective-permute-done.3, bf16[4,256,128]{2,1,0:T(8,128)(2,1)} %collective-permute-done.2, bf16[4,256,128]{2,1,0:T(8,128)(2,1)} %collective-permute-done.1, bf16[4,256,128]{2,1,0:T(8,128)(2,1)} %collective-permute-done, bf16[1,256,128]{2,1,0:T(8,128)(2,1)S(1)} %slice.38, ...), kind=kLoop, calls=%fused_computation.10 | loop fusion | flops 917504 | bytes 1638402 | tf_op jit(solution)/shard_map/add | solution.py:272
  23.5 0.0 copy-start
  23.5 0.0 collective-permute-done.4.refs_4_
  23.5 7.3 %collective-permute-start.5 = (bf16[2,256,128]{2,1,0:T(8,128)(2,1)S(1)}, bf16[2,256,128]{2,1,0:T(8,128)(2,1)S(1)}, u32[]{:S(2)}, u32[]{:S(2)}) collective-permute-start(bf16[2,256,128]{2,1,0:T(8,128)(2,1)S(1)} %slice_select_fusion), channel_id=1, source_target_pairs={{0,2},{2,0},{4,6},{6,4},{8,10},{10,8},{12,14},{14,12},{16,18},{18,... | collective-permute-start | bytes 393224 | tf_op jit(solution)/shard_map/ppermute | solution.py:275
  30.8 0.7 dynamic-slice_bitcast_fusion
  31.5 0.1 collective-permute-start.10
  31.6 0.2 collective-permute-done.5
  31.8 0.1 collective-permute-start.6
  31.9 0.1 pad_add_fusion.1.sc
  32.0 1.0 convert_element_type.21.w
  33.0 0.1 reshape.44.sc
  33.1 0.1 add_convert_fusion.pick
  33.1 4.5 %collective-permute-done.6.slab_a = bf16[2,256,128]{2,1,0:T(8,128)(2,1)S(1)} collective-permute-done((bf16[2,256,128]{2,1,0:T(8,128)(2,1)S(1)}, bf16[2,256,128]{2,1,0:T(8,128)(2,1)S(1)}, u32[]{:S(2)}, u32[]{:S(2)}) %collective-permute-start.6) | collective-permute-done | bytes 131104 | tf_op jit(solution)/shard_map/ppermute | solution.py:280
  37.7 0.1 collective-permute-start.7
  37.8 1.2 %collective-permute-done.7.panel_b = bf16[256,128]{1,0:T(8,128)(2,1)S(1)} collective-permute-done((bf16[256,128]{1,0:T(8,128)(2,1)S(1)}, bf16[256,128]{1,0:T(8,128)(2,1)S(1)}, u32[]{:S(2)}, u32[]{:S(2)}) %collective-permute-start.7) | collective-permute-done | bytes 65568 | tf_op jit(solution)/shard_map/ppermute | solution.py:282
  39.0 1.0 shard_map.64
  40.0 0.0 collective-permute-done.8.refs_3_
  40.0 0.2 collective-permute-start.9
  40.2 0.0 collective-permute-start.12
  40.2 6.0 %shard_map.65 = (f32[256,32768]{1,0:T(8,128)}, f32[128,256]{1,0:T(8,128)S(1)}, f32[8,128]{1,0:T(8,128)S(1)}) custom-call(s32[35]{0:T(128)S(1)} %pad_add_fusion.1.sc, f32[2,256,256]{2,1,0:T(8,128)S(1)} %convert_element_type.21.w, bf16[3,128,256]{2,1,0:T(8,128)(2,1)S(1)} %get-tuple-element.51.refs_0_, ...), custom_call_target="tpu_custom_call", output_to_operand_aliasing={{1}: (4, {})} | custom-call | flops 234881024 | bytes 786432 | tf_op jit(solution)/shard_map/pallas_call | solution.py:195
  46.3 2.2 %collective-permute-done.10.refs_3_ = bf16[4128,128]{1,0:T(8,128)(2,1)} collective-permute-done((bf16[4128,128]{1,0:T(8,128)(2,1)}, bf16[4128,128]{1,0:T(8,128)(2,1)}, u32[]{:S(2)}, u32[]{:S(2)}) %collective-permute-start.10) | collective-permute-done | bytes 1056800 | tf_op jit(solution)/shard_map/ppermute | solution.py:338
  48.5 2.5 %collective-permute-start.14 = (bf16[4128,128]{1,0:T(8,128)(2,1)}, bf16[4128,128]{1,0:T(8,128)(2,1)S(1)}, u32[]{:S(2)}, u32[]{:S(2)}) collective-permute-start(bf16[4128,128]{1,0:T(8,128)(2,1)} %collective-permute-done.10.refs_3_), channel_id=1, source_target_pairs={{0,8},{8,16},{16,24},{24,28},{28,20},{20,12},{12,4},{4,0},{2,6},{1... | collective-permute-start | bytes 3170312 | tf_op jit(solution)/shard_map/ppermute | solution.py:338
  50.9 6.1 %shard_map.66 = (f32[256,32768]{1,0:T(8,128)}, f32[128,256]{1,0:T(8,128)S(1)}, f32[8,128]{1,0:T(8,128)S(1)}) custom-call(s32[35]{0:T(128)S(1)} %pad_add_fusion.1.sc, f32[2,256,256]{2,1,0:T(8,128)S(1)} %convert_element_type.21.w, bf16[3,128,256]{2,1,0:T(8,128)(2,1)S(1)} %get-tuple-element.51.refs_0_, ...), custom_call_target="tpu_custom_call", output_to_operand_aliasing={{1}: (4, {}), {0}: (8, {})} | custom-call | flops 234881024 | bytes 786432 | tf_op jit(solution)/shard_map/pallas_call | solution.py:195
  57.1 2.6 %collective-permute-done.12.refs_3_ = bf16[4128,128]{1,0:T(8,128)(2,1)S(1)} collective-permute-done((bf16[4128,128]{1,0:T(8,128)(2,1)S(1)}, bf16[4128,128]{1,0:T(8,128)(2,1)S(1)}, u32[]{:S(2)}, u32[]{:S(2)}) %collective-permute-start.12) | collective-permute-done | bytes 1056800 | tf_op jit(solution)/shard_map/ppermute | solution.py:338
  59.7 0.0 collective-permute-start.13
  59.7 2.5 %collective-permute-start.16 = (bf16[4128,128]{1,0:T(8,128)(2,1)S(1)}, bf16[4128,128]{1,0:T(8,128)(2,1)S(1)}, u32[]{:S(2)}, u32[]{:S(2)}) collective-permute-start(bf16[4128,128]{1,0:T(8,128)(2,1)S(1)} %collective-permute-done.12.refs_3_), channel_id=1, source_target_pairs={{0,8},{8,16},{16,24},{24,28},{28,20},{20,12},{12,4},{4,0},{2,6},{1... | collective-permute-start | bytes 3170312 | tf_op jit(solution)/shard_map/ppermute | solution.py:338
  62.2 7.0 %shard_map.67 = (f32[256,32768]{1,0:T(8,128)}, f32[128,256]{1,0:T(8,128)S(1)}, f32[8,128]{1,0:T(8,128)S(1)}) custom-call(s32[35]{0:T(128)S(1)} %pad_add_fusion.1.sc, f32[2,256,256]{2,1,0:T(8,128)S(1)} %convert_element_type.21.w, bf16[3,128,256]{2,1,0:T(8,128)(2,1)S(1)} %get-tuple-element.51.refs_0_, ...), custom_call_target="tpu_custom_call", output_to_operand_aliasing={{1}: (4, {}), {0}: (8, {})} | custom-call | flops 234881024 | bytes 786432 | tf_op jit(solution)/shard_map/pallas_call | solution.py:195
  69.1 2.0 %collective-permute-done.14.refs_3_ = bf16[4128,128]{1,0:T(8,128)(2,1)S(1)} collective-permute-done((bf16[4128,128]{1,0:T(8,128)(2,1)}, bf16[4128,128]{1,0:T(8,128)(2,1)S(1)}, u32[]{:S(2)}, u32[]{:S(2)}) %collective-permute-start.14) | collective-permute-done | bytes 1056800 | tf_op jit(solution)/shard_map/ppermute | solution.py:338
  71.1 0.0 collective-permute-start.15
  71.1 2.4 %collective-permute-start.18 = (bf16[4128,128]{1,0:T(8,128)(2,1)S(1)}, bf16[4128,128]{1,0:T(8,128)(2,1)S(1)}, u32[]{:S(2)}, u32[]{:S(2)}) collective-permute-start(bf16[4128,128]{1,0:T(8,128)(2,1)S(1)} %collective-permute-done.14.refs_3_), channel_id=1, source_target_pairs={{0,8},{8,16},{16,24},{24,28},{28,20},{20,12},{12,4},{4,0},{2,6},{1... | collective-permute-start | bytes 3170312 | tf_op jit(solution)/shard_map/ppermute | solution.py:338
  73.5 0.0 collective-permute-done.13.refs_4_
  73.5 6.1 %shard_map.68 = (f32[256,32768]{1,0:T(8,128)}, f32[128,256]{1,0:T(8,128)S(1)}, f32[8,128]{1,0:T(8,128)S(1)}) custom-call(s32[35]{0:T(128)S(1)} %pad_add_fusion.1.sc, f32[2,256,256]{2,1,0:T(8,128)S(1)} %convert_element_type.21.w, bf16[3,128,256]{2,1,0:T(8,128)(2,1)S(1)} %get-tuple-element.51.refs_0_, ...), custom_call_target="tpu_custom_call", output_to_operand_aliasing={{1}: (4, {}), {0}: (8, {})} | custom-call | flops 234881024 | bytes 786432 | tf_op jit(solution)/shard_map/pallas_call | solution.py:195
  79.6 2.7 %collective-permute-done.16.refs_3_ = bf16[4128,128]{1,0:T(8,128)(2,1)S(1)} collective-permute-done((bf16[4128,128]{1,0:T(8,128)(2,1)S(1)}, bf16[4128,128]{1,0:T(8,128)(2,1)S(1)}, u32[]{:S(2)}, u32[]{:S(2)}) %collective-permute-start.16) | collective-permute-done | bytes 1056800 | tf_op jit(solution)/shard_map/ppermute | solution.py:338
  82.3 0.0 collective-permute-start.17
  82.3 0.0 collective-permute-done.15.refs_4_
  82.3 6.1 %shard_map.69 = (f32[256,32768]{1,0:T(8,128)}, f32[128,256]{1,0:T(8,128)S(1)}, f32[8,128]{1,0:T(8,128)S(1)}) custom-call(s32[35]{0:T(128)S(1)} %pad_add_fusion.1.sc, f32[2,256,256]{2,1,0:T(8,128)S(1)} %convert_element_type.21.w, bf16[3,128,256]{2,1,0:T(8,128)(2,1)S(1)} %get-tuple-element.51.refs_0_, ...), custom_call_target="tpu_custom_call", output_to_operand_aliasing={{1}: (4, {}), {0}: (8, {})} | custom-call | flops 234881024 | bytes 786432 | tf_op jit(solution)/shard_map/pallas_call | solution.py:195
  88.5 5.2 %collective-permute-done.18.refs_3_ = bf16[4128,128]{1,0:T(8,128)(2,1)S(1)} collective-permute-done((bf16[4128,128]{1,0:T(8,128)(2,1)S(1)}, bf16[4128,128]{1,0:T(8,128)(2,1)S(1)}, u32[]{:S(2)}, u32[]{:S(2)}) %collective-permute-start.18) | collective-permute-done | bytes 1056800 | tf_op jit(solution)/shard_map/ppermute | solution.py:338
  93.6 0.0 collective-permute-start.19
  93.7 2.5 %collective-permute-start.20 = (bf16[4128,128]{1,0:T(8,128)(2,1)S(1)}, bf16[4128,128]{1,0:T(8,128)(2,1)S(1)}, u32[]{:S(2)}, u32[]{:S(2)}) collective-permute-start(bf16[4128,128]{1,0:T(8,128)(2,1)S(1)} %collective-permute-done.16.refs_3_), channel_id=1, source_target_pairs={{0,8},{8,16},{16,24},{24,28},{28,20},{20,12},{12,4},{4,0},{2,6},{1... | collective-permute-start | bytes 3170312 | tf_op jit(solution)/shard_map/ppermute | solution.py:338
  96.1 6.7 %shard_map.70 = (f32[256,32768]{1,0:T(8,128)}, f32[128,256]{1,0:T(8,128)S(1)}, f32[8,128]{1,0:T(8,128)}) custom-call(s32[35]{0:T(128)S(1)} %pad_add_fusion.1.sc, f32[2,256,256]{2,1,0:T(8,128)S(1)} %convert_element_type.21.w, bf16[3,128,256]{2,1,0:T(8,128)(2,1)S(1)} %get-tuple-element.51.refs_0_, ...), custom_call_target="tpu_custom_call", output_to_operand_aliasing={{1}: (4, {}), {0}: (8, {})} | custom-call | flops 234881024 | bytes 786432 | tf_op jit(solution)/shard_map/pallas_call | solution.py:195
  102.8 0.0 collective-permute-done.19.refs_4_
  102.9 6.1 %shard_map.71 = (f32[256,32768]{1,0:T(8,128)}, f32[128,256]{1,0:T(8,128)S(1)}, f32[8,128]{1,0:T(8,128)S(1)}) custom-call(s32[35]{0:T(128)S(1)} %pad_add_fusion.1.sc, f32[2,256,256]{2,1,0:T(8,128)S(1)} %convert_element_type.21.w, bf16[3,128,256]{2,1,0:T(8,128)(2,1)S(1)} %get-tuple-element.51.refs_0_, ...), custom_call_target="tpu_custom_call", output_to_operand_aliasing={{1}: (4, {}), {0}: (7, {})} | custom-call | flops 234881024 | bytes 786432 | tf_op jit(solution)/shard_map/pallas_call | solution.py:195
  109.0 0.1 collective-permute-start.21
  109.1 2.7 %collective-permute-done.21.refs_2_.refs_3_ = bf16[4128,128]{1,0:T(8,128)(2,1)S(1)} collective-permute-done((bf16[4128,128]{1,0:T(8,128)(2,1)S(1)}, bf16[4128,128]{1,0:T(8,128)(2,1)S(1)}, u32[]{:S(2)}, u32[]{:S(2)}) %collective-permute-start.21) | collective-permute-done | bytes 1056800 | tf_op jit(solution)/shard_map/ppermute | solution.py:338
  111.7 2.9 %shard_map.72 = (f32[128,256]{1,0:T(8,128)S(1)}, f32[8,128]{1,0:T(8,128)S(1)}) custom-call(s32[35]{0:T(128)S(1)} %pad_add_fusion.1.sc, f32[2,256,256]{2,1,0:T(8,128)S(1)} %convert_element_type.21.w, f32[128,256]{1,0:T(8,128)S(1)} %get-tuple-element.83.refs_0_, ...), custom_call_target="tpu_custom_call", output_to_operand_aliasing={{0}: (2, {})} | custom-call | flops 67108864 | bytes 262144 | tf_op jit(solution)/shard_map/pallas_call | solution.py:195
  114.7 0.1 collective-permute-start.22
  114.8 0.0 copy-start.1
  114.8 5.7 %shard_map.73 = (f32[256,32768]{1,0:T(8,128)}, f32[8,128]{1,0:T(8,128)}) custom-call(s32[35]{0:T(128)S(1)} %pad_add_fusion.1.sc, f32[2,256,256]{2,1,0:T(8,128)S(1)} %convert_element_type.21.w, bf16[3,128,256]{2,1,0:T(8,128)(2,1)S(1)} %get-tuple-element.51.refs_0_, f32[256,128]{1,0:T(8,128)S(1)} %get-tuple-element.53.refs_1_, ...), custom_call_target="tpu_custom_call", output_to_operand_aliasing={{0}: (7, {})} | custom-call | flops 167772160 | bytes 786432 | tf_op jit(solution)/shard_map/pallas_call | solution.py:195
  120.5 0.0 collective-permute-done.22.other
  120.5 2.3 %shard_map.74 = f32[256,32768]{1,0:T(8,128)} custom-call(s32[4]{0:T(128)S(1)} %reshape.44.sc, f32[128,256]{1,0:T(8,128)S(1)} %get-tuple-element.87.gram, f32[128,256]{1,0:T(8,128)S(1)} %collective-permute-done.22.other, f32[2,128]{1,0:T(2,128)S(1)} %copy-done.1, f32[256,32768]{1,0:T(8,128)} %get-tuple-element.90.tile), custom_call_target="tpu_custom_call", output_to_operand_aliasing={{}: (4, {})} | custom-call | tf_op jit(solution)/shard_map/pallas_call | solution.py:232
  (22 shorter events, 0.2 us)
Async XLA Ops:
  0.0 1.9 %copy-start.2 = (bf16[16,256,128]{2,1,0:T(8,128)(2,1)S(1)}, bf16[16,256,128]{2,1,0:T(8,128)(2,1)}, u32[]{:S(2)}) copy-start(bf16[16,256,128]{2,1,0:T(8,128)(2,1)} %param.6) | copy-start | bytes 3145732
  1.4 22.1 %collective-permute-start.4 = (bf16[4128,128]{1,0:T(8,128)(2,1)S(1)}, bf16[4128,128]{1,0:T(8,128)(2,1)}, u32[]{:S(2)}, u32[]{:S(2)}) collective-permute-start(bf16[4128,128]{1,0:T(8,128)(2,1)S(1)} %pad_maximum_fusion.refs_3_), channel_id=1, source_target_pairs={{0,2},{2,0},{4,6},{6,4},{8,10},{10,8},{12,14},{14,12},{16,18},{18,... | collective-permute-start | bytes 3170312 | tf_op jit(solution)/shard_map/ppermute | solution.py:338
  2.8 12.4 %collective-permute-start.3 = (bf16[4,256,128]{2,1,0:T(8,128)(2,1)S(1)}, bf16[4,256,128]{2,1,0:T(8,128)(2,1)}, u32[]{:S(2)}, u32[]{:S(2)}) collective-permute-start(bf16[4,256,128]{2,1,0:T(8,128)(2,1)S(1)} %get-tuple-element.94), channel_id=1, source_target_pairs={{2,16}} | collective-permute-start | bytes 786440 | tf_op jit(solution)/shard_map/ppermute | solution.py:272
  4.2 12.4 %collective-permute-start.2 = (bf16[4,256,128]{2,1,0:T(8,128)(2,1)}, bf16[4,256,128]{2,1,0:T(8,128)(2,1)}, u32[]{:S(2)}, u32[]{:S(2)}) collective-permute-start(bf16[4,256,128]{2,1,0:T(8,128)(2,1)} %get-tuple-element.93), channel_id=1, source_target_pairs={{2,28},{0,12},{31,7}} | collective-permute-start | bytes 786440 | tf_op jit(solution)/shard_map/ppermute | solution.py:272
  10.4 11.8 %collective-permute-start.1 = (bf16[4,256,128]{2,1,0:T(8,128)(2,1)}, bf16[4,256,128]{2,1,0:T(8,128)(2,1)}, u32[]{:S(2)}, u32[]{:S(2)}) collective-permute-start(bf16[4,256,128]{2,1,0:T(8,128)(2,1)} %get-tuple-element.92), channel_id=1, source_target_pairs={{2,24},{0,8},{31,15}} | collective-permute-start | bytes 786440 | tf_op jit(solution)/shard_map/ppermute | solution.py:272
  12.4 9.8 %collective-permute-start = (bf16[4,256,128]{2,1,0:T(8,128)(2,1)S(1)}, bf16[4,256,128]{2,1,0:T(8,128)(2,1)}, u32[]{:S(2)}, u32[]{:S(2)}) collective-permute-start(bf16[4,256,128]{2,1,0:T(8,128)(2,1)S(1)} %get-tuple-element.91), channel_id=1, source_target_pairs={{2,20},{0,4},{31,23}} | collective-permute-start | bytes 786440 | tf_op jit(solution)/shard_map/ppermute | solution.py:272
  15.2 24.8 %collective-permute-start.8 = (bf16[4128,128]{1,0:T(8,128)(2,1)S(1)}, bf16[4128,128]{1,0:T(8,128)(2,1)S(1)}, u32[]{:S(2)}, u32[]{:S(2)}) collective-permute-start(bf16[4128,128]{1,0:T(8,128)(2,1)S(1)} %pad_maximum_fusion.refs_3_), channel_id=1, source_target_pairs={{0,8},{8,16},{16,24},{24,28},{28,20},{20,12},{12,4},{4,0},{2,6},{1... | collective-permute-start | bytes 3170312 | tf_op jit(solution)/shard_map/ppermute | solution.py:338
  23.5 15.5 %copy-start = (f32[128,128]{1,0:T(8,128)S(1)}, f32[128,128]{1,0:T(8,128)}, u32[]{:S(2)}) copy-start(f32[128,128]{1,0:T(8,128)} %inverse.1) | copy-start | bytes 196612
  23.5 8.3 %collective-permute-start.5 = (bf16[2,256,128]{2,1,0:T(8,128)(2,1)S(1)}, bf16[2,256,128]{2,1,0:T(8,128)(2,1)S(1)}, u32[]{:S(2)}, u32[]{:S(2)}) collective-permute-start(bf16[2,256,128]{2,1,0:T(8,128)(2,1)S(1)} %slice_select_fusion), channel_id=1, source_target_pairs={{0,2},{2,0},{4,6},{6,4},{8,10},{10,8},{12,14},{14,12},{16,18},{18,... | collective-permute-start | bytes 393224 | tf_op jit(solution)/shard_map/ppermute | solution.py:275
  31.5 16.9 %collective-permute-start.10 = (bf16[4128,128]{1,0:T(8,128)(2,1)}, bf16[4128,128]{1,0:T(8,128)(2,1)}, u32[]{:S(2)}, u32[]{:S(2)}) collective-permute-start(bf16[4128,128]{1,0:T(8,128)(2,1)} %collective-permute-done.4.refs_4_), channel_id=1, source_target_pairs={{0,8},{8,16},{16,24},{24,28},{28,20},{20,12},{12,4},{4,0},{2,6},{1... | collective-permute-start | bytes 3170312 | tf_op jit(solution)/shard_map/ppermute | solution.py:338
  31.8 5.8 %collective-permute-start.6 = (bf16[2,256,128]{2,1,0:T(8,128)(2,1)S(1)}, bf16[2,256,128]{2,1,0:T(8,128)(2,1)S(1)}, u32[]{:S(2)}, u32[]{:S(2)}) collective-permute-start(bf16[2,256,128]{2,1,0:T(8,128)(2,1)S(1)} %maximum_select_fusion.slab_b), channel_id=1, source_target_pairs={{0,1},{1,0},{2,3},{3,2},{4,5},{5,4},{6,7},{7,6},{8,9},{9,8},{10,11... | collective-permute-start | bytes 393224 | tf_op jit(solution)/shard_map/ppermute | solution.py:280
  37.7 1.3 %collective-permute-start.7 = (bf16[256,128]{1,0:T(8,128)(2,1)S(1)}, bf16[256,128]{1,0:T(8,128)(2,1)S(1)}, u32[]{:S(2)}, u32[]{:S(2)}) collective-permute-start(bf16[256,128]{1,0:T(8,128)(2,1)S(1)} %fusion.5.panel_a), channel_id=1, source_target_pairs={{0,2},{2,0},{4,6},{6,4},{8,10},{10,8},{12,14},{14,12},{16,18},{18,... | collective-permute-start | bytes 196616 | tf_op jit(solution)/shard_map/ppermute | solution.py:282
  40.0 11.0 %collective-permute-start.9 = (bf16[4128,128]{1,0:T(8,128)(2,1)S(1)}, bf16[4128,128]{1,0:T(8,128)(2,1)S(1)}, u32[]{:S(2)}, u32[]{:S(2)}) collective-permute-start(bf16[4128,128]{1,0:T(8,128)(2,1)S(1)} %collective-permute-done.8.refs_3_), channel_id=1, source_target_pairs={{0,2},{2,0},{4,6},{6,4},{8,10},{10,8},{12,14},{14,12},{16,18},{18,... | collective-permute-start | bytes 3170312 | tf_op jit(solution)/shard_map/ppermute | solution.py:338
  40.2 19.5 %collective-permute-start.12 = (bf16[4128,128]{1,0:T(8,128)(2,1)S(1)}, bf16[4128,128]{1,0:T(8,128)(2,1)S(1)}, u32[]{:S(2)}, u32[]{:S(2)}) collective-permute-start(bf16[4128,128]{1,0:T(8,128)(2,1)S(1)} %collective-permute-done.8.refs_3_), channel_id=1, source_target_pairs={{0,8},{8,16},{16,24},{24,28},{28,20},{20,12},{12,4},{4,0},{2,6},{1... | collective-permute-start | bytes 3170312 | tf_op jit(solution)/shard_map/ppermute | solution.py:338
  48.5 13.7 %collective-permute-start.11 = (bf16[4128,128]{1,0:T(8,128)(2,1)}, bf16[4128,128]{1,0:T(8,128)(2,1)S(1)}, u32[]{:S(2)}, u32[]{:S(2)}) collective-permute-start(bf16[4128,128]{1,0:T(8,128)(2,1)} %collective-permute-done.10.refs_3_), channel_id=1, source_target_pairs={{0,2},{2,0},{4,6},{6,4},{8,10},{10,8},{12,14},{14,12},{16,18},{18,... | collective-permute-start | bytes 3170312 | tf_op jit(solution)/shard_map/ppermute | solution.py:338
  48.5 22.6 %collective-permute-start.14 = (bf16[4128,128]{1,0:T(8,128)(2,1)}, bf16[4128,128]{1,0:T(8,128)(2,1)S(1)}, u32[]{:S(2)}, u32[]{:S(2)}) collective-permute-start(bf16[4128,128]{1,0:T(8,128)(2,1)} %collective-permute-done.10.refs_3_), channel_id=1, source_target_pairs={{0,8},{8,16},{16,24},{24,28},{28,20},{20,12},{12,4},{4,0},{2,6},{1... | collective-permute-start | bytes 3170312 | tf_op jit(solution)/shard_map/ppermute | solution.py:338
  59.7 13.8 %collective-permute-start.13 = (bf16[4128,128]{1,0:T(8,128)(2,1)S(1)}, bf16[4128,128]{1,0:T(8,128)(2,1)S(1)}, u32[]{:S(2)}, u32[]{:S(2)}) collective-permute-start(bf16[4128,128]{1,0:T(8,128)(2,1)S(1)} %collective-permute-done.12.refs_3_), channel_id=1, source_target_pairs={{0,2},{2,0},{4,6},{6,4},{8,10},{10,8},{12,14},{14,12},{16,18},{18,... | collective-permute-start | bytes 3170312 | tf_op jit(solution)/shard_map/ppermute | solution.py:338
  59.7 22.6 %collective-permute-start.16 = (bf16[4128,128]{1,0:T(8,128)(2,1)S(1)}, bf16[4128,128]{1,0:T(8,128)(2,1)S(1)}, u32[]{:S(2)}, u32[]{:S(2)}) collective-permute-start(bf16[4128,128]{1,0:T(8,128)(2,1)S(1)} %collective-permute-done.12.refs_3_), channel_id=1, source_target_pairs={{0,8},{8,16},{16,24},{24,28},{28,20},{20,12},{12,4},{4,0},{2,6},{1... | collective-permute-start | bytes 3170312 | tf_op jit(solution)/shard_map/ppermute | solution.py:338
  71.1 11.2 %collective-permute-start.15 = (bf16[4128,128]{1,0:T(8,128)(2,1)S(1)}, bf16[4128,128]{1,0:T(8,128)(2,1)S(1)}, u32[]{:S(2)}, u32[]{:S(2)}) collective-permute-start(bf16[4128,128]{1,0:T(8,128)(2,1)S(1)} %collective-permute-done.14.refs_3_), channel_id=1, source_target_pairs={{0,2},{2,0},{4,6},{6,4},{8,10},{10,8},{12,14},{14,12},{16,18},{18,... | collective-permute-start | bytes 3170312 | tf_op jit(solution)/shard_map/ppermute | solution.py:338
  71.1 22.5 %collective-permute-start.18 = (bf16[4128,128]{1,0:T(8,128)(2,1)S(1)}, bf16[4128,128]{1,0:T(8,128)(2,1)S(1)}, u32[]{:S(2)}, u32[]{:S(2)}) collective-permute-start(bf16[4128,128]{1,0:T(8,128)(2,1)S(1)} %collective-permute-done.14.refs_3_), channel_id=1, source_target_pairs={{0,8},{8,16},{16,24},{24,28},{28,20},{20,12},{12,4},{4,0},{2,6},{1... | collective-permute-start | bytes 3170312 | tf_op jit(solution)/shard_map/ppermute | solution.py:338
  82.3 13.8 %collective-permute-start.17 = (bf16[4128,128]{1,0:T(8,128)(2,1)S(1)}, bf16[4128,128]{1,0:T(8,128)(2,1)S(1)}, u32[]{:S(2)}, u32[]{:S(2)}) collective-permute-start(bf16[4128,128]{1,0:T(8,128)(2,1)S(1)} %collective-permute-done.16.refs_3_), channel_id=1, source_target_pairs={{0,2},{2,0},{4,6},{6,4},{8,10},{10,8},{12,14},{14,12},{16,18},{18,... | collective-permute-start | bytes 3170312 | tf_op jit(solution)/shard_map/ppermute | solution.py:338
  93.6 9.2 %collective-permute-start.19 = (bf16[4128,128]{1,0:T(8,128)(2,1)S(1)}, bf16[4128,128]{1,0:T(8,128)(2,1)S(1)}, u32[]{:S(2)}, u32[]{:S(2)}) collective-permute-start(bf16[4128,128]{1,0:T(8,128)(2,1)S(1)} %collective-permute-done.18.refs_3_), channel_id=1, source_target_pairs={{0,2},{2,0},{4,6},{6,4},{8,10},{10,8},{12,14},{14,12},{16,18},{18,... | collective-permute-start | bytes 3170312 | tf_op jit(solution)/shard_map/ppermute | solution.py:338
  93.7 15.3 %collective-permute-start.20 = (bf16[4128,128]{1,0:T(8,128)(2,1)S(1)}, bf16[4128,128]{1,0:T(8,128)(2,1)S(1)}, u32[]{:S(2)}, u32[]{:S(2)}) collective-permute-start(bf16[4128,128]{1,0:T(8,128)(2,1)S(1)} %collective-permute-done.16.refs_3_), channel_id=1, source_target_pairs={{0,8},{8,16},{16,24},{24,28},{28,20},{20,12},{12,4},{4,0},{2,6},{1... | collective-permute-start | bytes 3170312 | tf_op jit(solution)/shard_map/ppermute | solution.py:338
  109.0 2.7 %collective-permute-start.21 = (bf16[4128,128]{1,0:T(8,128)(2,1)S(1)}, bf16[4128,128]{1,0:T(8,128)(2,1)S(1)}, u32[]{:S(2)}, u32[]{:S(2)}) collective-permute-start(bf16[4128,128]{1,0:T(8,128)(2,1)S(1)} %collective-permute-done.20.refs_1_.refs_2_), channel_id=1, source_target_pairs={{0,2},{2,0},{4,6},{6,4},{8,10},{10,8},{12,14},{14,12},{16,18},{18,... | collective-permute-start | bytes 3170312 | tf_op jit(solution)/shard_map/ppermute | solution.py:338
  114.7 5.8 %collective-permute-start.22 = (f32[128,256]{1,0:T(8,128)S(1)}, f32[128,256]{1,0:T(8,128)S(1)}, u32[]{:S(2)}, u32[]{:S(2)}) collective-permute-start(f32[128,256]{1,0:T(8,128)S(1)} %get-tuple-element.87.gram), channel_id=1, source_target_pairs={{0,1},{1,0},{2,3},{3,2},{4,5},{5,4},{6,7},{7,6},{8,9},{9,8},{10,11... | collective-permute-start | bytes 393224 | tf_op jit(solution)/shard_map/ppermute | solution.py:417
  114.8 5.7 %copy-start.1 = (f32[2,128]{1,0:T(2,128)S(1)}, f32[2,128]{1,0:T(2,128)}, u32[]{:S(2)}) copy-start(f32[2,128]{1,0:T(2,128)} %damp.1) | copy-start | bytes 3076

commit v3 on v2

--- a/solution.py
+++ b/solution.py
@@ -214,30 +214,44 @@
     return out, gram, results[0]
 
 
-def patch_kernel(sc, gram, other, damp, tile, out):
-    i = pl.program_id(0)
-    width = tile.shape[0]
-    g = (gram[...] + other[...]).T
+def patch_kernel(sc, gram, other, damp, tiles, out, buf, in_sem, out_sem):
+    slabs, width, _ = buf.shape
+
+    def spot(ref, i):
+        col = pl.multiple_of(sc[2 * i] * width, width)
+        return ref.at[pl.ds(i * width, width), pl.ds(col, width)]
+
+    reads = [pltpu.make_async_copy(spot(tiles, i), buf.at[i], in_sem.at[i]) for i in range(slabs)]
+    writes = [pltpu.make_async_copy(buf.at[i], spot(out, i), out_sem.at[i]) for i in range(slabs)]
+    for copy in reads:
+        copy.start()
     eye = lax.broadcasted_iota(jnp.int32, (width, width), 0) == lax.broadcasted_iota(
         jnp.int32, (width, width), 1
     )
-    full = jnp.where(eye, g * (1.0 + damp[pl.ds(i, 1), :]), g)
-    out[...] = jnp.where(sc[2 * i + 1] > 0, tile[...] + full, tile[...])
+    for i in range(slabs):
+        here = (slice(None), slice(i * width, (i + 1) * width))
+        g = (gram[here] + other[here]).T
+        full = jnp.where(eye, g * (1.0 + damp[i : i + 1, :]), g)
+        reads[i].wait()
+        buf[i] = jnp.where(sc[2 * i + 1] > 0, buf[i] + full, buf[i])
+        writes[i].start()
+    for copy in writes:
+        copy.wait()
 
 
 def patch_call(sc, gram, other, damping, out):
     slabs, width = damping.shape
-    tile = pl.BlockSpec((width, width), lambda i, s: (i, s[2 * i]))
-    part = pl.BlockSpec((width, width), lambda i, s: (0, i))
+    vmem, anywhere = pl.BlockSpec(memory_space=pltpu.VMEM), pl.BlockSpec(memory_space=pl.ANY)
     return pl.pallas_call(
         patch_kernel,
-        grid_spec=pltpu.PrefetchScalarGridSpec(
-            num_scalar_prefetch=1,
-            grid=(slabs,),
-            in_specs=[part, part, pl.BlockSpec((slabs, width), lambda i, s: (0, 0)), tile],
-            out_specs=tile,
-        ),
+        in_specs=[pl.BlockSpec(memory_space=pltpu.SMEM), vmem, vmem, vmem, anywhere],
+        out_specs=anywhere,
         out_shape=jax.ShapeDtypeStruct(out.shape, F32),
+        scratch_shapes=[
+            pltpu.VMEM((slabs, width, width), F32),
+            pltpu.SemaphoreType.DMA((slabs,)),
+            pltpu.SemaphoreType.DMA((slabs,)),
+        ],
         input_output_aliases={4: 0},
         compiler_params=pltpu.CompilerParams(vmem_limit_bytes=8 << 20),
     )(sc, gram, other, damping, out)

time: 123 us -> 123 us (level)
  no operation moved by 1% of the time
where the time goes in v3:
time: 123 us
  Pallas kernels  55.9 us (45%)
  waiting for transfers between devices  30.2 us (25%)
  starting transfers between devices  29.8 us (24%)
  other arithmetic  4.83 us (4%)
  local copies, waits for them, and re-layouts  1.55 us (1%)
    pallas_call x9, Pallas kernels, block_call(): pl.pallas_call(functools.partial(block_kernel, slot, half, (slabs, width,...  52.8 us
    ppermute x15, waiting for transfers between devices, over(): return lax.ppermute(value, 'row', perm)  17.4 us
    ppermute x4, starting transfers between devices, spread_direct(): total = total + lax.ppermute(pay, both, pairs)  11.6 us
    ppermute x15, starting transfers between devices, over(): return lax.ppermute(value, 'row', perm)  10.8 us
    ppermute x1, starting transfers between devices, spread_direct(): lax.ppermute(jnp.where(is_panel, total[:slabs], total[slabs:]), both, hop)  7.28 us
    ppermute x4, waiting for transfers between devices, spread_direct(): total = total + lax.ppermute(pay, both, pairs)  6.94 us
    ppermute x1, waiting for transfers between devices, spread_direct(): second = lax.ppermute(send, 'col', [(0, 1), (1, 0)])  4.52 us
  transfers between devices with their start and end apart: 23, of which 11 were waited for; matrix products, arithmetic and copies ran while one was open for 4% of the time, Pallas kernels for 41%

profile of v3, /device:TPU:0, one launch (start us, length us, event | category | flops | bytes accessed | tf_op | source)
XLA Modules:
  0.0 122.8 jit_solution(6137443452400097813)
XLA Ops:
  0.0 1.4 %pad_maximum_fusion.refs_3_ = bf16[4128,128]{1,0:T(8,128)(2,1)S(1)} fusion(bf16[32,128]{1,0:T(8,128)(2,1)} %bitcast.18, bf16[4096,128]{1,0:T(8,128)(2,1)} %bitcast.17), kind=kLoop, calls=%fused_computation | loop fusion | flops 2113536 | bytes 2113536 | tf_op jit(solution)/shard_map/concatenate | solution.py:357
  1.4 0.5 collective-permute-start.4
  1.9 0.9 pad_select_fusion.3
  2.8 1.4 %collective-permute-start.3 = (bf16[4,256,128]{2,1,0:T(8,128)(2,1)S(1)}, bf16[4,256,128]{2,1,0:T(8,128)(2,1)}, u32[]{:S(2)}, u32[]{:S(2)}) collective-permute-start(bf16[4,256,128]{2,1,0:T(8,128)(2,1)S(1)} %get-tuple-element.94), channel_id=1, source_target_pairs={{2,16}} | collective-permute-start | bytes 786440 | tf_op jit(solution)/shard_map/ppermute | solution.py:286
  4.2 6.2 %collective-permute-start.2 = (bf16[4,256,128]{2,1,0:T(8,128)(2,1)}, bf16[4,256,128]{2,1,0:T(8,128)(2,1)}, u32[]{:S(2)}, u32[]{:S(2)}) collective-permute-start(bf16[4,256,128]{2,1,0:T(8,128)(2,1)} %get-tuple-element.93), channel_id=1, source_target_pairs={{2,28},{0,12},{31,7}} | collective-permute-start | bytes 786440 | tf_op jit(solution)/shard_map/ppermute | solution.py:286
  10.4 2.0 %collective-permute-start.1 = (bf16[4,256,128]{2,1,0:T(8,128)(2,1)}, bf16[4,256,128]{2,1,0:T(8,128)(2,1)}, u32[]{:S(2)}, u32[]{:S(2)}) collective-permute-start(bf16[4,256,128]{2,1,0:T(8,128)(2,1)} %get-tuple-element.92), channel_id=1, source_target_pairs={{2,24},{0,8},{31,15}} | collective-permute-start | bytes 786440 | tf_op jit(solution)/shard_map/ppermute | solution.py:286
  12.4 2.0 %collective-permute-start = (bf16[4,256,128]{2,1,0:T(8,128)(2,1)S(1)}, bf16[4,256,128]{2,1,0:T(8,128)(2,1)}, u32[]{:S(2)}, u32[]{:S(2)}) collective-permute-start(bf16[4,256,128]{2,1,0:T(8,128)(2,1)S(1)} %get-tuple-element.91), channel_id=1, source_target_pairs={{2,20},{0,4},{31,23}} | collective-permute-start | bytes 786440 | tf_op jit(solution)/shard_map/ppermute | solution.py:286
  14.4 0.1 pad_add_fusion
  14.5 0.7 slice_reduce_fusion
  15.2 0.0 collective-permute-done.3
  15.2 0.1 collective-permute-start.8
  15.3 1.3 %collective-permute-done.2 = bf16[4,256,128]{2,1,0:T(8,128)(2,1)} collective-permute-done((bf16[4,256,128]{2,1,0:T(8,128)(2,1)}, bf16[4,256,128]{2,1,0:T(8,128)(2,1)}, u32[]{:S(2)}, u32[]{:S(2)}) %collective-permute-start.2) | collective-permute-done | bytes 262176 | tf_op jit(solution)/shard_map/ppermute | solution.py:286
  16.6 5.6 %collective-permute-done.1 = bf16[4,256,128]{2,1,0:T(8,128)(2,1)} collective-permute-done((bf16[4,256,128]{2,1,0:T(8,128)(2,1)}, bf16[4,256,128]{2,1,0:T(8,128)(2,1)}, u32[]{:S(2)}, u32[]{:S(2)}) %collective-permute-start.1) | collective-permute-done | bytes 262176 | tf_op jit(solution)/shard_map/ppermute | solution.py:286
  22.2 0.0 collective-permute-done
  22.2 1.3 %fusion.4 = bf16[4,256,128]{2,1,0:T(8,128)(2,1)S(1)} fusion(bf16[4,256,128]{2,1,0:T(8,128)(2,1)} %collective-permute-done.3, bf16[4,256,128]{2,1,0:T(8,128)(2,1)} %collective-permute-done.2, bf16[4,256,128]{2,1,0:T(8,128)(2,1)} %collective-permute-done.1, bf16[4,256,128]{2,1,0:T(8,128)(2,1)} %collective-permute-done, bf16[1,256,128]{2,1,0:T(8,128)(2,1)S(1)} %slice.38, ...), kind=kLoop, calls=%fused_computation.10 | loop fusion | flops 917504 | bytes 1638402 | tf_op jit(solution)/shard_map/add | solution.py:286
  23.5 0.0 copy-start
  23.5 7.3 %collective-permute-start.5 = (bf16[2,256,128]{2,1,0:T(8,128)(2,1)S(1)}, bf16[2,256,128]{2,1,0:T(8,128)(2,1)S(1)}, u32[]{:S(2)}, u32[]{:S(2)}) collective-permute-start(bf16[2,256,128]{2,1,0:T(8,128)(2,1)S(1)} %slice_select_fusion), channel_id=1, source_target_pairs={{0,2},{2,0},{4,6},{6,4},{8,10},{10,8},{12,14},{14,12},{16,18},{18,... | collective-permute-start | bytes 393224 | tf_op jit(solution)/shard_map/ppermute | solution.py:289
  30.8 0.7 dynamic-slice_bitcast_fusion
  31.5 0.1 collective-permute-start.10
  31.6 0.2 collective-permute-done.5
  31.8 0.1 collective-permute-start.6
  31.9 0.1 pad_add_fusion.1.sc
  32.0 1.0 convert_element_type.21.w
  33.0 0.1 reshape.44.sc
  33.1 0.1 add_convert_fusion.pick
  33.1 4.5 %collective-permute-done.6.slab_a = bf16[2,256,128]{2,1,0:T(8,128)(2,1)S(1)} collective-permute-done((bf16[2,256,128]{2,1,0:T(8,128)(2,1)S(1)}, bf16[2,256,128]{2,1,0:T(8,128)(2,1)S(1)}, u32[]{:S(2)}, u32[]{:S(2)}) %collective-permute-start.6) | collective-permute-done | bytes 131104 | tf_op jit(solution)/shard_map/ppermute | solution.py:294
  37.7 0.1 collective-permute-start.7
  37.8 1.2 %collective-permute-done.7.panel_b = bf16[256,128]{1,0:T(8,128)(2,1)S(1)} collective-permute-done((bf16[256,128]{1,0:T(8,128)(2,1)S(1)}, bf16[256,128]{1,0:T(8,128)(2,1)S(1)}, u32[]{:S(2)}, u32[]{:S(2)}) %collective-permute-start.7) | collective-permute-done | bytes 65568 | tf_op jit(solution)/shard_map/ppermute | solution.py:296
  39.0 1.0 shard_map.64
  40.0 0.0 collective-permute-done.8.refs_3_
  40.0 0.2 collective-permute-start.9
  40.2 0.0 collective-permute-start.12
  40.2 6.0 %shard_map.65 = (f32[256,32768]{1,0:T(8,128)}, f32[128,256]{1,0:T(8,128)S(1)}, f32[8,128]{1,0:T(8,128)S(1)}) custom-call(s32[35]{0:T(128)S(1)} %pad_add_fusion.1.sc, f32[2,256,256]{2,1,0:T(8,128)S(1)} %convert_element_type.21.w, bf16[3,128,256]{2,1,0:T(8,128)(2,1)S(1)} %get-tuple-element.51.refs_0_, ...), custom_call_target="tpu_custom_call", output_to_operand_aliasing={{1}: (4, {})} | custom-call | flops 234881024 | bytes 786432 | tf_op jit(solution)/shard_map/pallas_call | solution.py:195
  46.3 2.2 %collective-permute-done.10.refs_3_ = bf16[4128,128]{1,0:T(8,128)(2,1)} collective-permute-done((bf16[4128,128]{1,0:T(8,128)(2,1)}, bf16[4128,128]{1,0:T(8,128)(2,1)}, u32[]{:S(2)}, u32[]{:S(2)}) %collective-permute-start.10) | collective-permute-done | bytes 1056800 | tf_op jit(solution)/shard_map/ppermute | solution.py:352
  48.5 0.0 collective-permute-start.11
  48.5 2.5 %collective-permute-start.14 = (bf16[4128,128]{1,0:T(8,128)(2,1)}, bf16[4128,128]{1,0:T(8,128)(2,1)S(1)}, u32[]{:S(2)}, u32[]{:S(2)}) collective-permute-start(bf16[4128,128]{1,0:T(8,128)(2,1)} %collective-permute-done.10.refs_3_), channel_id=1, source_target_pairs={{0,8},{8,16},{16,24},{24,28},{28,20},{20,12},{12,4},{4,0},{2,6},{1... | collective-permute-start | bytes 3170312 | tf_op jit(solution)/shard_map/ppermute | solution.py:352
  50.9 0.0 collective-permute-done.9.refs_4_
  50.9 6.1 %shard_map.66 = (f32[256,32768]{1,0:T(8,128)}, f32[128,256]{1,0:T(8,128)S(1)}, f32[8,128]{1,0:T(8,128)S(1)}) custom-call(s32[35]{0:T(128)S(1)} %pad_add_fusion.1.sc, f32[2,256,256]{2,1,0:T(8,128)S(1)} %convert_element_type.21.w, bf16[3,128,256]{2,1,0:T(8,128)(2,1)S(1)} %get-tuple-element.51.refs_0_, ...), custom_call_target="tpu_custom_call", output_to_operand_aliasing={{1}: (4, {}), {0}: (8, {})} | custom-call | flops 234881024 | bytes 786432 | tf_op jit(solution)/shard_map/pallas_call | solution.py:195
  57.1 2.6 %collective-permute-done.12.refs_3_ = bf16[4128,128]{1,0:T(8,128)(2,1)S(1)} collective-permute-done((bf16[4128,128]{1,0:T(8,128)(2,1)S(1)}, bf16[4128,128]{1,0:T(8,128)(2,1)S(1)}, u32[]{:S(2)}, u32[]{:S(2)}) %collective-permute-start.12) | collective-permute-done | bytes 1056800 | tf_op jit(solution)/shard_map/ppermute | solution.py:352
  59.7 0.0 collective-permute-start.13
  59.7 2.5 %collective-permute-start.16 = (bf16[4128,128]{1,0:T(8,128)(2,1)S(1)}, bf16[4128,128]{1,0:T(8,128)(2,1)S(1)}, u32[]{:S(2)}, u32[]{:S(2)}) collective-permute-start(bf16[4128,128]{1,0:T(8,128)(2,1)S(1)} %collective-permute-done.12.refs_3_), channel_id=1, source_target_pairs={{0,8},{8,16},{16,24},{24,28},{28,20},{20,12},{12,4},{4,0},{2,6},{1... | collective-permute-start | bytes 3170312 | tf_op jit(solution)/shard_map/ppermute | solution.py:352
  62.2 0.0 collective-permute-done.11.refs_4_
  62.2 7.0 %shard_map.67 = (f32[256,32768]{1,0:T(8,128)}, f32[128,256]{1,0:T(8,128)S(1)}, f32[8,128]{1,0:T(8,128)S(1)}) custom-call(s32[35]{0:T(128)S(1)} %pad_add_fusion.1.sc, f32[2,256,256]{2,1,0:T(8,128)S(1)} %convert_element_type.21.w, bf16[3,128,256]{2,1,0:T(8,128)(2,1)S(1)} %get-tuple-element.51.refs_0_, ...), custom_call_target="tpu_custom_call", output_to_operand_aliasing={{1}: (4, {}), {0}: (8, {})} | custom-call | flops 234881024 | bytes 786432 | tf_op jit(solution)/shard_map/pallas_call | solution.py:195
  69.1 2.0 %collective-permute-done.14.refs_3_ = bf16[4128,128]{1,0:T(8,128)(2,1)S(1)} collective-permute-done((bf16[4128,128]{1,0:T(8,128)(2,1)}, bf16[4128,128]{1,0:T(8,128)(2,1)S(1)}, u32[]{:S(2)}, u32[]{:S(2)}) %collective-permute-start.14) | collective-permute-done | bytes 1056800 | tf_op jit(solution)/shard_map/ppermute | solution.py:352
  71.1 0.0 collective-permute-start.15
  71.1 2.4 %collective-permute-start.18 = (bf16[4128,128]{1,0:T(8,128)(2,1)S(1)}, bf16[4128,128]{1,0:T(8,128)(2,1)S(1)}, u32[]{:S(2)}, u32[]{:S(2)}) collective-permute-start(bf16[4128,128]{1,0:T(8,128)(2,1)S(1)} %collective-permute-done.14.refs_3_), channel_id=1, source_target_pairs={{0,8},{8,16},{16,24},{24,28},{28,20},{20,12},{12,4},{4,0},{2,6},{1... | collective-permute-start | bytes 3170312 | tf_op jit(solution)/shard_map/ppermute | solution.py:352
  73.5 0.0 collective-permute-done.13.refs_4_
  73.5 6.1 %shard_map.68 = (f32[256,32768]{1,0:T(8,128)}, f32[128,256]{1,0:T(8,128)S(1)}, f32[8,128]{1,0:T(8,128)S(1)}) custom-call(s32[35]{0:T(128)S(1)} %pad_add_fusion.1.sc, f32[2,256,256]{2,1,0:T(8,128)S(1)} %convert_element_type.21.w, bf16[3,128,256]{2,1,0:T(8,128)(2,1)S(1)} %get-tuple-element.51.refs_0_, ...), custom_call_target="tpu_custom_call", output_to_operand_aliasing={{1}: (4, {}), {0}: (8, {})} | custom-call | flops 234881024 | bytes 786432 | tf_op jit(solution)/shard_map/pallas_call | solution.py:195
  79.6 2.7 %collective-permute-done.16.refs_3_ = bf16[4128,128]{1,0:T(8,128)(2,1)S(1)} collective-permute-done((bf16[4128,128]{1,0:T(8,128)(2,1)S(1)}, bf16[4128,128]{1,0:T(8,128)(2,1)S(1)}, u32[]{:S(2)}, u32[]{:S(2)}) %collective-permute-start.16) | collective-permute-done | bytes 1056800 | tf_op jit(solution)/shard_map/ppermute | solution.py:352
  82.3 6.1 %shard_map.69 = (f32[256,32768]{1,0:T(8,128)}, f32[128,256]{1,0:T(8,128)S(1)}, f32[8,128]{1,0:T(8,128)S(1)}) custom-call(s32[35]{0:T(128)S(1)} %pad_add_fusion.1.sc, f32[2,256,256]{2,1,0:T(8,128)S(1)} %convert_element_type.21.w, bf16[3,128,256]{2,1,0:T(8,128)(2,1)S(1)} %get-tuple-element.51.refs_0_, ...), custom_call_target="tpu_custom_call", output_to_operand_aliasing={{1}: (4, {}), {0}: (8, {})} | custom-call | flops 234881024 | bytes 786432 | tf_op jit(solution)/shard_map/pallas_call | solution.py:195
  88.5 5.2 %collective-permute-done.18.refs_3_ = bf16[4128,128]{1,0:T(8,128)(2,1)S(1)} collective-permute-done((bf16[4128,128]{1,0:T(8,128)(2,1)S(1)}, bf16[4128,128]{1,0:T(8,128)(2,1)S(1)}, u32[]{:S(2)}, u32[]{:S(2)}) %collective-permute-start.18) | collective-permute-done | bytes 1056800 | tf_op jit(solution)/shard_map/ppermute | solution.py:352
  93.7 2.5 %collective-permute-start.20 = (bf16[4128,128]{1,0:T(8,128)(2,1)S(1)}, bf16[4128,128]{1,0:T(8,128)(2,1)S(1)}, u32[]{:S(2)}, u32[]{:S(2)}) collective-permute-start(bf16[4128,128]{1,0:T(8,128)(2,1)S(1)} %collective-permute-done.16.refs_3_), channel_id=1, source_target_pairs={{0,8},{8,16},{16,24},{24,28},{28,20},{20,12},{12,4},{4,0},{2,6},{1... | collective-permute-start | bytes 3170312 | tf_op jit(solution)/shard_map/ppermute | solution.py:352
  96.1 0.0 collective-permute-done.17.refs_4_
  96.1 6.7 %shard_map.70 = (f32[256,32768]{1,0:T(8,128)}, f32[128,256]{1,0:T(8,128)S(1)}, f32[8,128]{1,0:T(8,128)}) custom-call(s32[35]{0:T(128)S(1)} %pad_add_fusion.1.sc, f32[2,256,256]{2,1,0:T(8,128)S(1)} %convert_element_type.21.w, bf16[3,128,256]{2,1,0:T(8,128)(2,1)S(1)} %get-tuple-element.51.refs_0_, ...), custom_call_target="tpu_custom_call", output_to_operand_aliasing={{1}: (4, {}), {0}: (8, {})} | custom-call | flops 234881024 | bytes 786432 | tf_op jit(solution)/shard_map/pallas_call | solution.py:195
  102.9 6.1 %shard_map.71 = (f32[256,32768]{1,0:T(8,128)}, f32[128,256]{1,0:T(8,128)S(1)}, f32[8,128]{1,0:T(8,128)S(1)}) custom-call(s32[35]{0:T(128)S(1)} %pad_add_fusion.1.sc, f32[2,256,256]{2,1,0:T(8,128)S(1)} %convert_element_type.21.w, bf16[3,128,256]{2,1,0:T(8,128)(2,1)S(1)} %get-tuple-element.51.refs_0_, ...), custom_call_target="tpu_custom_call", output_to_operand_aliasing={{1}: (4, {}), {0}: (7, {})} | custom-call | flops 234881024 | bytes 786432 | tf_op jit(solution)/shard_map/pallas_call | solution.py:195
  109.0 0.0 collective-permute-done.20.refs_1_.refs_2_
  109.0 0.1 collective-permute-start.21
  109.1 2.7 %collective-permute-done.21.refs_2_.refs_3_ = bf16[4128,128]{1,0:T(8,128)(2,1)S(1)} collective-permute-done((bf16[4128,128]{1,0:T(8,128)(2,1)S(1)}, bf16[4128,128]{1,0:T(8,128)(2,1)S(1)}, u32[]{:S(2)}, u32[]{:S(2)}) %collective-permute-start.21) | collective-permute-done | bytes 1056800 | tf_op jit(solution)/shard_map/ppermute | solution.py:352
  111.7 2.9 %shard_map.72 = (f32[128,256]{1,0:T(8,128)S(1)}, f32[8,128]{1,0:T(8,128)S(1)}) custom-call(s32[35]{0:T(128)S(1)} %pad_add_fusion.1.sc, f32[2,256,256]{2,1,0:T(8,128)S(1)} %convert_element_type.21.w, f32[128,256]{1,0:T(8,128)S(1)} %get-tuple-element.83.refs_0_, ...), custom_call_target="tpu_custom_call", output_to_operand_aliasing={{0}: (2, {})} | custom-call | flops 67108864 | bytes 262144 | tf_op jit(solution)/shard_map/pallas_call | solution.py:195
  114.7 0.1 collective-permute-start.22
  114.8 0.0 copy-start.1
  114.8 5.7 %shard_map.73 = (f32[256,32768]{1,0:T(8,128)}, f32[8,128]{1,0:T(8,128)}) custom-call(s32[35]{0:T(128)S(1)} %pad_add_fusion.1.sc, f32[2,256,256]{2,1,0:T(8,128)S(1)} %convert_element_type.21.w, bf16[3,128,256]{2,1,0:T(8,128)(2,1)S(1)} %get-tuple-element.51.refs_0_, f32[256,128]{1,0:T(8,128)S(1)} %get-tuple-element.53.refs_1_, ...), custom_call_target="tpu_custom_call", output_to_operand_aliasing={{0}: (7, {})} | custom-call | flops 167772160 | bytes 786432 | tf_op jit(solution)/shard_map/pallas_call | solution.py:195
  120.5 0.0 collective-permute-done.22.other
  120.5 2.2 %shard_map.74 = f32[256,32768]{1,0:T(8,128)} custom-call(s32[4]{0:T(128)S(1)} %reshape.44.sc, f32[128,256]{1,0:T(8,128)S(1)} %get-tuple-element.87.gram, f32[128,256]{1,0:T(8,128)S(1)} %collective-permute-done.22.other, f32[2,128]{1,0:T(2,128)S(1)} %copy-done.1, f32[256,32768]{1,0:T(8,128)} %get-tuple-element.90.tiles), custom_call_target="tpu_custom_call", output_to_operand_aliasing={{}: (4, {})} | custom-call | tf_op jit(solution)/shard_map/pallas_call | solution.py:245
  (22 shorter events, 0.2 us)
Async XLA Ops:
  0.0 1.9 %copy-start.2 = (bf16[16,256,128]{2,1,0:T(8,128)(2,1)S(1)}, bf16[16,256,128]{2,1,0:T(8,128)(2,1)}, u32[]{:S(2)}) copy-start(bf16[16,256,128]{2,1,0:T(8,128)(2,1)} %param.6) | copy-start | bytes 3145732
  1.4 22.1 %collective-permute-start.4 = (bf16[4128,128]{1,0:T(8,128)(2,1)S(1)}, bf16[4128,128]{1,0:T(8,128)(2,1)}, u32[]{:S(2)}, u32[]{:S(2)}) collective-permute-start(bf16[4128,128]{1,0:T(8,128)(2,1)S(1)} %pad_maximum_fusion.refs_3_), channel_id=1, source_target_pairs={{0,2},{2,0},{4,6},{6,4},{8,10},{10,8},{12,14},{14,12},{16,18},{18,... | collective-permute-start | bytes 3170312 | tf_op jit(solution)/shard_map/ppermute | solution.py:352
  2.8 12.4 %collective-permute-start.3 = (bf16[4,256,128]{2,1,0:T(8,128)(2,1)S(1)}, bf16[4,256,128]{2,1,0:T(8,128)(2,1)}, u32[]{:S(2)}, u32[]{:S(2)}) collective-permute-start(bf16[4,256,128]{2,1,0:T(8,128)(2,1)S(1)} %get-tuple-element.94), channel_id=1, source_target_pairs={{2,16}} | collective-permute-start | bytes 786440 | tf_op jit(solution)/shard_map/ppermute | solution.py:286
  4.2 12.4 %collective-permute-start.2 = (bf16[4,256,128]{2,1,0:T(8,128)(2,1)}, bf16[4,256,128]{2,1,0:T(8,128)(2,1)}, u32[]{:S(2)}, u32[]{:S(2)}) collective-permute-start(bf16[4,256,128]{2,1,0:T(8,128)(2,1)} %get-tuple-element.93), channel_id=1, source_target_pairs={{2,28},{0,12},{31,7}} | collective-permute-start | bytes 786440 | tf_op jit(solution)/shard_map/ppermute | solution.py:286
  10.4 11.8 %collective-permute-start.1 = (bf16[4,256,128]{2,1,0:T(8,128)(2,1)}, bf16[4,256,128]{2,1,0:T(8,128)(2,1)}, u32[]{:S(2)}, u32[]{:S(2)}) collective-permute-start(bf16[4,256,128]{2,1,0:T(8,128)(2,1)} %get-tuple-element.92), channel_id=1, source_target_pairs={{2,24},{0,8},{31,15}} | collective-permute-start | bytes 786440 | tf_op jit(solution)/shard_map/ppermute | solution.py:286
  12.4 9.8 %collective-permute-start = (bf16[4,256,128]{2,1,0:T(8,128)(2,1)S(1)}, bf16[4,256,128]{2,1,0:T(8,128)(2,1)}, u32[]{:S(2)}, u32[]{:S(2)}) collective-permute-start(bf16[4,256,128]{2,1,0:T(8,128)(2,1)S(1)} %get-tuple-element.91), channel_id=1, source_target_pairs={{2,20},{0,4},{31,23}} | collective-permute-start | bytes 786440 | tf_op jit(solution)/shard_map/ppermute | solution.py:286
  15.2 24.8 %collective-permute-start.8 = (bf16[4128,128]{1,0:T(8,128)(2,1)S(1)}, bf16[4128,128]{1,0:T(8,128)(2,1)S(1)}, u32[]{:S(2)}, u32[]{:S(2)}) collective-permute-start(bf16[4128,128]{1,0:T(8,128)(2,1)S(1)} %pad_maximum_fusion.refs_3_), channel_id=1, source_target_pairs={{0,8},{8,16},{16,24},{24,28},{28,20},{20,12},{12,4},{4,0},{2,6},{1... | collective-permute-start | bytes 3170312 | tf_op jit(solution)/shard_map/ppermute | solution.py:352
  23.5 15.5 %copy-start = (f32[128,128]{1,0:T(8,128)S(1)}, f32[128,128]{1,0:T(8,128)}, u32[]{:S(2)}) copy-start(f32[128,128]{1,0:T(8,128)} %inverse.1) | copy-start | bytes 196612
  23.5 8.3 %collective-permute-start.5 = (bf16[2,256,128]{2,1,0:T(8,128)(2,1)S(1)}, bf16[2,256,128]{2,1,0:T(8,128)(2,1)S(1)}, u32[]{:S(2)}, u32[]{:S(2)}) collective-permute-start(bf16[2,256,128]{2,1,0:T(8,128)(2,1)S(1)} %slice_select_fusion), channel_id=1, source_target_pairs={{0,2},{2,0},{4,6},{6,4},{8,10},{10,8},{12,14},{14,12},{16,18},{18,... | collective-permute-start | bytes 393224 | tf_op jit(solution)/shard_map/ppermute | solution.py:289
  31.5 16.9 %collective-permute-start.10 = (bf16[4128,128]{1,0:T(8,128)(2,1)}, bf16[4128,128]{1,0:T(8,128)(2,1)}, u32[]{:S(2)}, u32[]{:S(2)}) collective-permute-start(bf16[4128,128]{1,0:T(8,128)(2,1)} %collective-permute-done.4.refs_4_), channel_id=1, source_target_pairs={{0,8},{8,16},{16,24},{24,28},{28,20},{20,12},{12,4},{4,0},{2,6},{1... | collective-permute-start | bytes 3170312 | tf_op jit(solution)/shard_map/ppermute | solution.py:352
  31.8 5.8 %collective-permute-start.6 = (bf16[2,256,128]{2,1,0:T(8,128)(2,1)S(1)}, bf16[2,256,128]{2,1,0:T(8,128)(2,1)S(1)}, u32[]{:S(2)}, u32[]{:S(2)}) collective-permute-start(bf16[2,256,128]{2,1,0:T(8,128)(2,1)S(1)} %maximum_select_fusion.slab_b), channel_id=1, source_target_pairs={{0,1},{1,0},{2,3},{3,2},{4,5},{5,4},{6,7},{7,6},{8,9},{9,8},{10,11... | collective-permute-start | bytes 393224 | tf_op jit(solution)/shard_map/ppermute | solution.py:294
  37.7 1.3 %collective-permute-start.7 = (bf16[256,128]{1,0:T(8,128)(2,1)S(1)}, bf16[256,128]{1,0:T(8,128)(2,1)S(1)}, u32[]{:S(2)}, u32[]{:S(2)}) collective-permute-start(bf16[256,128]{1,0:T(8,128)(2,1)S(1)} %fusion.5.panel_a), channel_id=1, source_target_pairs={{0,2},{2,0},{4,6},{6,4},{8,10},{10,8},{12,14},{14,12},{16,18},{18,... | collective-permute-start | bytes 196616 | tf_op jit(solution)/shard_map/ppermute | solution.py:296
  40.0 11.0 %collective-permute-start.9 = (bf16[4128,128]{1,0:T(8,128)(2,1)S(1)}, bf16[4128,128]{1,0:T(8,128)(2,1)S(1)}, u32[]{:S(2)}, u32[]{:S(2)}) collective-permute-start(bf16[4128,128]{1,0:T(8,128)(2,1)S(1)} %collective-permute-done.8.refs_3_), channel_id=1, source_target_pairs={{0,2},{2,0},{4,6},{6,4},{8,10},{10,8},{12,14},{14,12},{16,18},{18,... | collective-permute-start | bytes 3170312 | tf_op jit(solution)/shard_map/ppermute | solution.py:352
  40.2 19.5 %collective-permute-start.12 = (bf16[4128,128]{1,0:T(8,128)(2,1)S(1)}, bf16[4128,128]{1,0:T(8,128)(2,1)S(1)}, u32[]{:S(2)}, u32[]{:S(2)}) collective-permute-start(bf16[4128,128]{1,0:T(8,128)(2,1)S(1)} %collective-permute-done.8.refs_3_), channel_id=1, source_target_pairs={{0,8},{8,16},{16,24},{24,28},{28,20},{20,12},{12,4},{4,0},{2,6},{1... | collective-permute-start | bytes 3170312 | tf_op jit(solution)/shard_map/ppermute | solution.py:352
  48.5 13.7 %collective-permute-start.11 = (bf16[4128,128]{1,0:T(8,128)(2,1)}, bf16[4128,128]{1,0:T(8,128)(2,1)S(1)}, u32[]{:S(2)}, u32[]{:S(2)}) collective-permute-start(bf16[4128,128]{1,0:T(8,128)(2,1)} %collective-permute-done.10.refs_3_), channel_id=1, source_target_pairs={{0,2},{2,0},{4,6},{6,4},{8,10},{10,8},{12,14},{14,12},{16,18},{18,... | collective-permute-start | bytes 3170312 | tf_op jit(solution)/shard_map/ppermute | solution.py:352
  48.5 22.6 %collective-permute-start.14 = (bf16[4128,128]{1,0:T(8,128)(2,1)}, bf16[4128,128]{1,0:T(8,128)(2,1)S(1)}, u32[]{:S(2)}, u32[]{:S(2)}) collective-permute-start(bf16[4128,128]{1,0:T(8,128)(2,1)} %collective-permute-done.10.refs_3_), channel_id=1, source_target_pairs={{0,8},{8,16},{16,24},{24,28},{28,20},{20,12},{12,4},{4,0},{2,6},{1... | collective-permute-start | bytes 3170312 | tf_op jit(solution)/shard_map/ppermute | solution.py:352
  59.7 13.8 %collective-permute-start.13 = (bf16[4128,128]{1,0:T(8,128)(2,1)S(1)}, bf16[4128,128]{1,0:T(8,128)(2,1)S(1)}, u32[]{:S(2)}, u32[]{:S(2)}) collective-permute-start(bf16[4128,128]{1,0:T(8,128)(2,1)S(1)} %collective-permute-done.12.refs_3_), channel_id=1, source_target_pairs={{0,2},{2,0},{4,6},{6,4},{8,10},{10,8},{12,14},{14,12},{16,18},{18,... | collective-permute-start | bytes 3170312 | tf_op jit(solution)/shard_map/ppermute | solution.py:352
  59.7 22.6 %collective-permute-start.16 = (bf16[4128,128]{1,0:T(8,128)(2,1)S(1)}, bf16[4128,128]{1,0:T(8,128)(2,1)S(1)}, u32[]{:S(2)}, u32[]{:S(2)}) collective-permute-start(bf16[4128,128]{1,0:T(8,128)(2,1)S(1)} %collective-permute-done.12.refs_3_), channel_id=1, source_target_pairs={{0,8},{8,16},{16,24},{24,28},{28,20},{20,12},{12,4},{4,0},{2,6},{1... | collective-permute-start | bytes 3170312 | tf_op jit(solution)/shard_map/ppermute | solution.py:352
  71.1 11.2 %collective-permute-start.15 = (bf16[4128,128]{1,0:T(8,128)(2,1)S(1)}, bf16[4128,128]{1,0:T(8,128)(2,1)S(1)}, u32[]{:S(2)}, u32[]{:S(2)}) collective-permute-start(bf16[4128,128]{1,0:T(8,128)(2,1)S(1)} %collective-permute-done.14.refs_3_), channel_id=1, source_target_pairs={{0,2},{2,0},{4,6},{6,4},{8,10},{10,8},{12,14},{14,12},{16,18},{18,... | collective-permute-start | bytes 3170312 | tf_op jit(solution)/shard_map/ppermute | solution.py:352
  71.1 22.5 %collective-permute-start.18 = (bf16[4128,128]{1,0:T(8,128)(2,1)S(1)}, bf16[4128,128]{1,0:T(8,128)(2,1)S(1)}, u32[]{:S(2)}, u32[]{:S(2)}) collective-permute-start(bf16[4128,128]{1,0:T(8,128)(2,1)S(1)} %collective-permute-done.14.refs_3_), channel_id=1, source_target_pairs={{0,8},{8,16},{16,24},{24,28},{28,20},{20,12},{12,4},{4,0},{2,6},{1... | collective-permute-start | bytes 3170312 | tf_op jit(solution)/shard_map/ppermute | solution.py:352
  82.3 13.8 %collective-permute-start.17 = (bf16[4128,128]{1,0:T(8,128)(2,1)S(1)}, bf16[4128,128]{1,0:T(8,128)(2,1)S(1)}, u32[]{:S(2)}, u32[]{:S(2)}) collective-permute-start(bf16[4128,128]{1,0:T(8,128)(2,1)S(1)} %collective-permute-done.16.refs_3_), channel_id=1, source_target_pairs={{0,2},{2,0},{4,6},{6,4},{8,10},{10,8},{12,14},{14,12},{16,18},{18,... | collective-permute-start | bytes 3170312 | tf_op jit(solution)/shard_map/ppermute | solution.py:352
  93.6 9.2 %collective-permute-start.19 = (bf16[4128,128]{1,0:T(8,128)(2,1)S(1)}, bf16[4128,128]{1,0:T(8,128)(2,1)S(1)}, u32[]{:S(2)}, u32[]{:S(2)}) collective-permute-start(bf16[4128,128]{1,0:T(8,128)(2,1)S(1)} %collective-permute-done.18.refs_3_), channel_id=1, source_target_pairs={{0,2},{2,0},{4,6},{6,4},{8,10},{10,8},{12,14},{14,12},{16,18},{18,... | collective-permute-start | bytes 3170312 | tf_op jit(solution)/shard_map/ppermute | solution.py:352
  93.7 15.3 %collective-permute-start.20 = (bf16[4128,128]{1,0:T(8,128)(2,1)S(1)}, bf16[4128,128]{1,0:T(8,128)(2,1)S(1)}, u32[]{:S(2)}, u32[]{:S(2)}) collective-permute-start(bf16[4128,128]{1,0:T(8,128)(2,1)S(1)} %collective-permute-done.16.refs_3_), channel_id=1, source_target_pairs={{0,8},{8,16},{16,24},{24,28},{28,20},{20,12},{12,4},{4,0},{2,6},{1... | collective-permute-start | bytes 3170312 | tf_op jit(solution)/shard_map/ppermute | solution.py:352
  109.0 2.7 %collective-permute-start.21 = (bf16[4128,128]{1,0:T(8,128)(2,1)S(1)}, bf16[4128,128]{1,0:T(8,128)(2,1)S(1)}, u32[]{:S(2)}, u32[]{:S(2)}) collective-permute-start(bf16[4128,128]{1,0:T(8,128)(2,1)S(1)} %collective-permute-done.20.refs_1_.refs_2_), channel_id=1, source_target_pairs={{0,2},{2,0},{4,6},{6,4},{8,10},{10,8},{12,14},{14,12},{16,18},{18,... | collective-permute-start | bytes 3170312 | tf_op jit(solution)/shard_map/ppermute | solution.py:352
  114.7 5.8 %collective-permute-start.22 = (f32[128,256]{1,0:T(8,128)S(1)}, f32[128,256]{1,0:T(8,128)S(1)}, u32[]{:S(2)}, u32[]{:S(2)}) collective-permute-start(f32[128,256]{1,0:T(8,128)S(1)} %get-tuple-element.87.gram), channel_id=1, source_target_pairs={{0,1},{1,0},{2,3},{3,2},{4,5},{5,4},{6,7},{7,6},{8,9},{9,8},{10,11... | collective-permute-start | bytes 393224 | tf_op jit(solution)/shard_map/ppermute | solution.py:431
  114.8 5.7 %copy-start.1 = (f32[2,128]{1,0:T(2,128)S(1)}, f32[2,128]{1,0:T(2,128)}, u32[]{:S(2)}) copy-start(f32[2,128]{1,0:T(2,128)} %damp.1) | copy-start | bytes 3076
